TPU v7x, 32 devices: a whole 2x2x4 slice. The times are simulated.
32 devices in a mesh: dp: 8 (over y, x, core), tensor: 4 (over z).
Axes of the slice: x: 2, y: 2, z: 4, core: 2. Of those that a mesh axis runs over, the one named last changes fastest.
Arguments:
- frames: bfloat16 [16, 256, 1536], P('dp', 'tensor'), may hold values from -6 to 6
- text_states: bfloat16 [16, 64, 1536], P('dp', 'tensor'), may hold values from -6 to 6
- self_q: bfloat16 [1536, 1536], P('dp', 'tensor'), may hold values from -0.15625 to 0.15625
- self_k: bfloat16 [1536, 1536], P('dp', 'tensor'), may hold values from -0.15625 to 0.15625
- self_v: bfloat16 [1536, 1536], P('dp', 'tensor'), may hold values from -0.15625 to 0.15625
- self_out: bfloat16 [1536, 1536], P('tensor', 'dp'), may hold values from -1.25 to 1.25
- cross_q: bfloat16 [1536, 1536], P('dp', 'tensor'), may hold values from -0.15625 to 0.15625
- cross_k: bfloat16 [1536, 1536], P('dp', 'tensor'), may hold values from -0.15625 to 0.15625
- cross_v: bfloat16 [1536, 1536], P('dp', 'tensor'), may hold values from -0.15625 to 0.15625
- cross_out: bfloat16 [1536, 1536], P('tensor', 'dp'), may hold values from -0.625 to 0.625
- mlp_up: bfloat16 [1536, 6144], P('dp', 'tensor'), may hold values from -0.15625 to 0.15625
- mlp_down: bfloat16 [6144, 1536], P('tensor', 'dp'), may hold values from -0.3125 to 0.3125
- norm_gains: float32 [3, 1536], P(None, ('dp', 'tensor')), may hold values from 0.5 to 1.5
- norm_shifts: float32 [3, 1536], P(None, ('dp', 'tensor')), may hold values from -3 to 3
- cotangent: bfloat16 [16, 256, 1536], P('dp', 'tensor'), may hold values from -6 to 6
Outputs:
- activations: bfloat16 [16, 256, 1536], P('dp', 'tensor')
- grad_frames: float32 [16, 256, 1536], P('dp', 'tensor')
- grad_text: float32 [16, 64, 1536], P('dp', 'tensor')
- grad_self_q: float32 [1536, 1536], P('dp', 'tensor')
- grad_self_k: float32 [1536, 1536], P('dp', 'tensor')
- grad_self_v: float32 [1536, 1536], P('dp', 'tensor')
- grad_self_out: float32 [1536, 1536], P('tensor', 'dp')
- grad_cross_q: float32 [1536, 1536], P('dp', 'tensor')
- grad_cross_k: float32 [1536, 1536], P('dp', 'tensor')
- grad_cross_v: float32 [1536, 1536], P('dp', 'tensor')
- grad_cross_out: float32 [1536, 1536], P('tensor', 'dp')
- grad_mlp_up: float32 [1536, 6144], P('dp', 'tensor')
- grad_mlp_down: float32 [6144, 1536], P('tensor', 'dp')
- grad_norm_gains: float32 [3, 1536], P(None, ('dp', 'tensor'))
- grad_norm_shifts: float32 [3, 1536], P(None, ('dp', 'tensor'))
All inputs are finite; a program needn't handle non-finite values.
Results may differ from a plain program's by a relative error of at most 0.028.
Values may be sent and summed in bfloat16 or wider, within the bound.
No kernel may reach another device: no remote copies, remote signals or barrier semaphores. Data moves between devices by JAX's collectives and lax.ppermute only.
A program may use at most 192 MiB of HBM per device.

v0:
```python
import jax
import jax.numpy as jnp
from jax import lax
from jax.sharding import PartitionSpec as P

HEAD_DIM = 64


EPS = 1e-05


def layer_norm(values, gain, shift):
    average = jnp.mean(values, axis=-1, keepdims=True)
    centered = values - average
    variance = jnp.mean(centered * centered, axis=-1, keepdims=True)
    return centered * lax.rsqrt(variance + EPS) * gain + shift


def norm_back(values, gain, shift, upstream):
    result, pullback = jax.vjp(layer_norm, values, gain, shift)
    return pullback(upstream)


def gelu_exact(values):
    return jax.nn.gelu(values, approximate=False)


def product(operand, matrix):
    return jnp.dot(operand, matrix, preferred_element_type=jnp.float32)


def product_left(operand, matrix):
    return lax.dot_general(
        operand, matrix, (((0,), (0,)), ((), ())), preferred_element_type=jnp.float32
    )


def product_right(operand, matrix):
    return lax.dot_general(
        operand, matrix, (((1,), (1,)), ((), ())), preferred_element_type=jnp.float32
    )


def spread(local_rows):
    return lax.all_gather(local_rows, "tensor", axis=0, tiled=True)


def collect(operands, matrices, flipped):
    summed = None
    for operand, matrix in zip(operands, matrices):
        if flipped:
            piece_term = product_right(operand, matrix)
        else:
            piece_term = product(operand, matrix)
        summed = piece_term if summed is None else summed + piece_term
    return lax.psum_scatter(
        summed.astype(jnp.bfloat16), "tensor", scatter_dimension=0, tiled=True
    ).astype(jnp.float32)


def score_table(heads_query, heads_key, causal):
    scores = jnp.einsum(
        "qhd,khd->hqk", heads_query, heads_key, preferred_element_type=jnp.float32
    ) * HEAD_DIM ** (-0.5)
    if causal:
        visible = (
            jnp.arange(heads_query.shape[0])[:, None] >= jnp.arange(heads_key.shape[0])[None, :]
        )
        scores = jnp.where(visible[None, :, :], scores, -1e30)
    return scores


def attend(queries, key_rows, value_rows, causal):
    query_count = queries.shape[0]
    heads_query = queries.reshape(query_count, -1, HEAD_DIM)
    heads_key = key_rows.reshape(key_rows.shape[0], -1, HEAD_DIM)
    heads_value = value_rows.reshape(value_rows.shape[0], -1, HEAD_DIM)
    scores = score_table(heads_query, heads_key, causal)
    log_total = jax.nn.logsumexp(scores, axis=-1, keepdims=True)
    probability = jnp.exp(scores - log_total).astype(jnp.bfloat16)
    mixture = jnp.einsum(
        "hqk,khd->qhd", probability, heads_value, preferred_element_type=jnp.float32
    )
    return (mixture.reshape(query_count, -1).astype(jnp.bfloat16), log_total)


def attend_back(queries, key_rows, value_rows, log_total, upstream, causal):
    query_count = queries.shape[0]
    key_count = key_rows.shape[0]
    heads_query = queries.reshape(query_count, -1, HEAD_DIM)
    heads_key = key_rows.reshape(key_count, -1, HEAD_DIM)
    heads_value = value_rows.reshape(key_count, -1, HEAD_DIM)
    heads_upstream = upstream.reshape(query_count, -1, HEAD_DIM)
    scores = score_table(heads_query, heads_key, causal)
    probability = jnp.exp(scores - log_total)
    probability_low = probability.astype(jnp.bfloat16)
    weight_grad = jnp.einsum(
        "qhd,khd->hqk", heads_upstream, heads_value, preferred_element_type=jnp.float32
    )
    row_dot = jnp.sum(probability * weight_grad, axis=-1, keepdims=True)
    score_grad = (probability * (weight_grad - row_dot)).astype(jnp.bfloat16)
    scaling = HEAD_DIM ** (-0.5)
    grad_query = (
        jnp.einsum("hqk,khd->qhd", score_grad, heads_key, preferred_element_type=jnp.float32)
        * scaling
    )
    grad_key = (
        jnp.einsum("hqk,qhd->khd", score_grad, heads_query, preferred_element_type=jnp.float32)
        * scaling
    )
    grad_value = jnp.einsum(
        "hqk,qhd->khd", probability_low, heads_upstream, preferred_element_type=jnp.float32
    )
    return (
        grad_query.reshape(query_count, -1).astype(jnp.bfloat16),
        grad_key.reshape(key_count, -1).astype(jnp.bfloat16),
        grad_value.reshape(key_count, -1).astype(jnp.bfloat16),
    )


def on_device(
    frames,
    text_states,
    self_q,
    self_k,
    self_v,
    self_out,
    cross_q,
    cross_k,
    cross_v,
    cross_out,
    mlp_up,
    mlp_down,
    norm_gains,
    norm_shifts,
    cotangent,
):
    gain_rows, shift_rows = (
        lax.all_gather(norm_gains, ("dp", "tensor"), axis=1, tiled=True),
        lax.all_gather(norm_shifts, ("dp", "tensor"), axis=1, tiled=True),
    )
    shards = (
        self_q,
        self_k,
        self_v,
        self_out,
        cross_q,
        cross_k,
        cross_v,
        cross_out,
        mlp_up,
        mlp_down,
    )
    gather_dims = (0, 0, 0, 1, 0, 0, 0, 1, 0, 1)
    dp_count = lax.axis_size("dp")
    totals = []
    for shard, along in zip(shards, gather_dims):
        if along == 0:
            totals.append(jnp.zeros((shard.shape[0] * dp_count, shard.shape[1]), jnp.float32))
        else:
            totals.append(jnp.zeros((shard.shape[0], shard.shape[1] * dp_count), jnp.float32))
    gain_total = jnp.zeros(gain_rows.shape, jnp.float32)
    shift_total = jnp.zeros(shift_rows.shape, jnp.float32)
    outputs = []
    frame_grads = []
    word_grads = []
    for batch_index in range(frames.shape[0]):
        weights = (
            lax.all_gather(self_q, "dp", axis=0, tiled=True),
            lax.all_gather(self_k, "dp", axis=0, tiled=True),
            lax.all_gather(self_v, "dp", axis=0, tiled=True),
            lax.all_gather(self_out, "dp", axis=1, tiled=True),
            lax.all_gather(cross_q, "dp", axis=0, tiled=True),
            lax.all_gather(cross_k, "dp", axis=0, tiled=True),
            lax.all_gather(cross_v, "dp", axis=0, tiled=True),
            lax.all_gather(cross_out, "dp", axis=1, tiled=True),
            lax.all_gather(mlp_up, "dp", axis=0, tiled=True),
            lax.all_gather(mlp_down, "dp", axis=1, tiled=True),
        )
        (
            full_q,
            full_k,
            full_v,
            full_out,
            full_cq,
            full_ck,
            full_cv,
            full_cout,
            full_up,
            full_down,
        ) = weights
        input_rows = frames[batch_index].astype(jnp.float32)
        whole_self = spread(
            layer_norm(input_rows, gain_rows[0], shift_rows[0]).astype(jnp.bfloat16)
        )
        query_self = product(whole_self, full_q).astype(jnp.bfloat16)
        key_self = product(whole_self, full_k).astype(jnp.bfloat16)
        value_self = product(whole_self, full_v).astype(jnp.bfloat16)
        mixture_self, total_self = attend(query_self, key_self, value_self, True)
        resid_self = input_rows + collect((mixture_self,), (full_out,), False)
        whole_cross = spread(
            layer_norm(resid_self, gain_rows[1], shift_rows[1]).astype(jnp.bfloat16)
        )
        text_all = lax.all_gather(text_states[batch_index], "tensor", axis=0, tiled=True)
        query_cross = product(whole_cross, full_cq).astype(jnp.bfloat16)
        key_cross = product(text_all, full_ck).astype(jnp.bfloat16)
        value_cross = product(text_all, full_cv).astype(jnp.bfloat16)
        mixture_cross, total_cross = attend(query_cross, key_cross, value_cross, False)
        resid_cross = resid_self + collect((mixture_cross,), (full_cout,), False)
        whole_mlp = spread(
            layer_norm(resid_cross, gain_rows[2], shift_rows[2]).astype(jnp.bfloat16)
        )
        hidden = product(whole_mlp, full_up)
        active = gelu_exact(hidden).astype(jnp.bfloat16)
        resid_mlp = resid_cross + collect((active,), (full_down,), False)
        outputs.append(resid_mlp.astype(jnp.bfloat16))
        upstream_mlp = cotangent[batch_index].astype(jnp.float32)
        spread_mlp = spread(upstream_mlp.astype(jnp.bfloat16))
        totals[9] = totals[9] + product_left(active, spread_mlp)
        active_grad = product_right(spread_mlp, full_down)
        hidden_low = jax.vjp(gelu_exact, hidden)[1](active_grad)[0].astype(jnp.bfloat16)
        totals[8] = totals[8] + product_left(whole_mlp, hidden_low)
        normed_grad = collect((hidden_low,), (full_up,), True)
        change, gain_grad, shift_grad = norm_back(
            resid_cross, gain_rows[2], shift_rows[2], normed_grad
        )
        gain_total = gain_total.at[2].add(gain_grad)
        shift_total = shift_total.at[2].add(shift_grad)
        upstream_cross = upstream_mlp + change
        spread_cross = spread(upstream_cross.astype(jnp.bfloat16))
        totals[7] = totals[7] + product_left(mixture_cross, spread_cross)
        mixed_grad = product_right(spread_cross, full_cout).astype(jnp.bfloat16)
        grad_qc, grad_kc, grad_vc = attend_back(
            query_cross, key_cross, value_cross, total_cross, mixed_grad, False
        )
        totals[4] = totals[4] + product_left(whole_cross, grad_qc)
        totals[5] = totals[5] + product_left(text_all, grad_kc)
        totals[6] = totals[6] + product_left(text_all, grad_vc)
        text_term = product_right(grad_kc, full_ck) + product_right(grad_vc, full_cv)
        word_grads.append(
            lax.psum_scatter(
                text_term.astype(jnp.bfloat16), "tensor", scatter_dimension=0, tiled=True
            ).astype(jnp.float32)
        )
        normed_grad = collect((grad_qc,), (full_cq,), True)
        change, gain_grad, shift_grad = norm_back(
            resid_self, gain_rows[1], shift_rows[1], normed_grad
        )
        gain_total = gain_total.at[1].add(gain_grad)
        shift_total = shift_total.at[1].add(shift_grad)
        upstream_self = upstream_cross + change
        spread_self = spread(upstream_self.astype(jnp.bfloat16))
        totals[3] = totals[3] + product_left(mixture_self, spread_self)
        mixed_grad = product_right(spread_self, full_out).astype(jnp.bfloat16)
        grad_qs, grad_ks, grad_vs = attend_back(
            query_self, key_self, value_self, total_self, mixed_grad, True
        )
        totals[0] = totals[0] + product_left(whole_self, grad_qs)
        totals[1] = totals[1] + product_left(whole_self, grad_ks)
        totals[2] = totals[2] + product_left(whole_self, grad_vs)
        normed_grad = collect((grad_qs, grad_ks, grad_vs), (full_q, full_k, full_v), True)
        change, gain_grad, shift_grad = norm_back(
            input_rows, gain_rows[0], shift_rows[0], normed_grad
        )
        gain_total = gain_total.at[0].add(gain_grad)
        shift_total = shift_total.at[0].add(shift_grad)
        frame_grads.append(upstream_self + change)
    summed = (
        lax.psum_scatter(totals[0], "dp", scatter_dimension=0, tiled=True),
        lax.psum_scatter(totals[1], "dp", scatter_dimension=0, tiled=True),
        lax.psum_scatter(totals[2], "dp", scatter_dimension=0, tiled=True),
        lax.psum_scatter(totals[3], "dp", scatter_dimension=1, tiled=True),
        lax.psum_scatter(totals[4], "dp", scatter_dimension=0, tiled=True),
        lax.psum_scatter(totals[5], "dp", scatter_dimension=0, tiled=True),
        lax.psum_scatter(totals[6], "dp", scatter_dimension=0, tiled=True),
        lax.psum_scatter(totals[7], "dp", scatter_dimension=1, tiled=True),
        lax.psum_scatter(totals[8], "dp", scatter_dimension=0, tiled=True),
        lax.psum_scatter(totals[9], "dp", scatter_dimension=1, tiled=True),
    )
    gain_sums, shift_sums = (
        lax.psum_scatter(gain_total, ("dp", "tensor"), scatter_dimension=1, tiled=True),
        lax.psum_scatter(shift_total, ("dp", "tensor"), scatter_dimension=1, tiled=True),
    )
    return (
        jnp.stack(outputs),
        jnp.stack(frame_grads),
        jnp.stack(word_grads),
        summed[0],
        summed[1],
        summed[2],
        summed[3],
        summed[4],
        summed[5],
        summed[6],
        summed[7],
        summed[8],
        summed[9],
        gain_sums,
        shift_sums,
    )


def solution(mesh):
    in_specs = (
        P("dp", "tensor", None),
        P("dp", "tensor", None),
        P("dp", "tensor"),
        P("dp", "tensor"),
        P("dp", "tensor"),
        P("tensor", "dp"),
        P("dp", "tensor"),
        P("dp", "tensor"),
        P("dp", "tensor"),
        P("tensor", "dp"),
        P("dp", "tensor"),
        P("tensor", "dp"),
        P(None, ("dp", "tensor")),
        P(None, ("dp", "tensor")),
        P("dp", "tensor", None),
    )
    out_specs = (
        P("dp", "tensor", None),
        P("dp", "tensor", None),
        P("dp", "tensor", None),
        P("dp", "tensor"),
        P("dp", "tensor"),
        P("dp", "tensor"),
        P("tensor", "dp"),
        P("dp", "tensor"),
        P("dp", "tensor"),
        P("dp", "tensor"),
        P("tensor", "dp"),
        P("dp", "tensor"),
        P("tensor", "dp"),
        P(None, ("dp", "tensor")),
        P(None, ("dp", "tensor")),
    )
    return jax.shard_map(
        on_device, mesh=mesh, in_specs=in_specs, out_specs=out_specs, check_vma=False
    )
```

profile of v0, /device:TPU:0, one launch (start us, length us, event | category | flops | bytes accessed | tf_op | source)
XLA Modules:
  0.0 1563.7 jit_solution(44874968497070089)
XLA Ops:
  12.4 70.7 %all-gather.4 = f32[32,48,3]{1,2,0:T(4,128)S(1)} all-gather(f32[1,48,3]{1,2,0:T(4,128)} %bitcast.458), channel_id=1, replica_groups=mesh['dp'=8,'tensor'=4] {'dp','tensor'}, dimensions={0}, use_global_device_ids=true | all-gather | bytes 19008 | tf_op jit(solution)/shard_map/all_gather | solution.py:139
  83.8 64.3 %all-gather.5 = f32[32,48,3]{1,2,0:T(4,128)S(1)} all-gather(f32[1,48,3]{1,2,0:T(4,128)} %bitcast.459), channel_id=1, replica_groups=mesh['dp'=8,'tensor'=4] {'dp','tensor'}, dimensions={0}, use_global_device_ids=true | all-gather | bytes 19008 | tf_op jit(solution)/shard_map/all_gather | solution.py:140
  178.4 20.1 %reduce-scatter.35.cloned.1.call-done = bf16[64,1536]{1,0:T(8,128)(2,1)} async-done(((bf16[256,1536]{1,0:T(8,128)(2,1)}), bf16[64,1536]{1,0:T(8,128)(2,1)}) %reduce-scatter.35.cloned.1.call-update) | async-done | bytes 196624 | tf_op jit(solution)/shard_map/reduce_scatter | solution.py:56
  330.2 29.2 %all_gather.97 = bf16[256,1536]{1,0:T(8,128)(2,1)S(1)} all-gather(bf16[64,1536]{1,0:T(8,128)(2,1)} %get-tuple-element.254), channel_id=1, replica_groups=mesh['dp'=8,'tensor'=4] {'tensor'}, dimensions={0}, use_global_device_ids=true | all-gather | bytes 983040 | tf_op jit(solution)/shard_map/all_gather | solution.py:45
  372.4 29.6 %all-gather.2 = bf16[1,256,1536]{2,1,0:T(8,128)(2,1)} all-gather(bf16[1,64,1536]{2,1,0:T(8,128)(2,1)S(1)} %get-tuple-element.262), channel_id=4, replica_groups=mesh['dp'=8,'tensor'=4] {'tensor'}, dimensions={1}, use_global_device_ids=true | all-gather | bytes 983040 | tf_op jit(solution)/shard_map/all_gather | solution.py:45
  422.9 18.8 %all_gather.101 = bf16[256,1536]{1,0:T(8,128)(2,1)} all-gather(bf16[64,1536]{1,0:T(8,128)(2,1)S(1)} %get-tuple-element.268), channel_id=1, replica_groups=mesh['dp'=8,'tensor'=4] {'tensor'}, dimensions={0}, use_global_device_ids=true | all-gather | bytes 983040 | tf_op jit(solution)/shard_map/all_gather | solution.py:45
  525.0 19.2 %reduce-scatter.53.cloned.1.call-done = bf16[64,1536]{1,0:T(8,128)(2,1)} async-done(((bf16[256,1536]{1,0:T(8,128)(2,1)}), bf16[64,1536]{1,0:T(8,128)(2,1)}) %reduce-scatter.53.cloned.1.call-update) | async-done | bytes 196624 | tf_op jit(solution)/shard_map/reduce_scatter | solution.py:56
  548.7 20.2 %reduce-scatter.39.cloned.1.call-done = bf16[64,1536]{1,0:T(8,128)(2,1)} async-done(((bf16[256,1536]{1,0:T(8,128)(2,1)}), bf16[64,1536]{1,0:T(8,128)(2,1)}) %reduce-scatter.39.cloned.1.call-update) | async-done | bytes 196624 | tf_op jit(solution)/shard_map/reduce_scatter | solution.py:56
  568.9 24.8 %reduce-scatter.45.cloned.1.call-done = bf16[64,1536]{1,0:T(8,128)(2,1)} async-done(((bf16[256,1536]{1,0:T(8,128)(2,1)}), bf16[64,1536]{1,0:T(8,128)(2,1)}) %reduce-scatter.45.cloned.1.call-update) | async-done | bytes 196624 | tf_op jit(solution)/shard_map/reduce_scatter | solution.py:56
  624.8 25.1 %all_gather.109 = bf16[256,1536]{1,0:T(8,128)(2,1)S(1)} all-gather(bf16[64,1536]{1,0:T(8,128)(2,1)} %get-tuple-element.259), channel_id=1, replica_groups=mesh['dp'=8,'tensor'=4] {'tensor'}, dimensions={0}, use_global_device_ids=true | all-gather | bytes 983040 | tf_op jit(solution)/shard_map/all_gather | solution.py:45
  660.8 23.8 %reduce-scatter.49.cloned.1.call-done = bf16[64,1536]{1,0:T(8,128)(2,1)} async-done(((bf16[256,1536]{1,0:T(8,128)(2,1)}), bf16[64,1536]{1,0:T(8,128)(2,1)}) %reduce-scatter.49.cloned.1.call-update) | async-done | bytes 196624 | tf_op jit(solution)/shard_map/reduce_scatter | solution.py:56
  724.2 28.2 %all_gather.110 = bf16[256,1536]{1,0:T(8,128)(2,1)S(1)} all-gather(bf16[64,1536]{1,0:T(8,128)(2,1)S(1)} %get-tuple-element.242), channel_id=1, replica_groups=mesh['dp'=8,'tensor'=4] {'tensor'}, dimensions={0}, use_global_device_ids=true | all-gather | bytes 983040 | tf_op jit(solution)/shard_map/all_gather | solution.py:45
  848.7 76.0 %reduce-scatter.85.cloned.1.call-done = f32[48,3]{1,0:T(8,128)} async-done(((f32[1536,3]{1,0:T(8,128)}), f32[48,3]{1,0:T(8,128)}) %reduce-scatter.85.cloned.1.call-update) | async-done | bytes 592
  926.1 98.1 %reduce-scatter.83.cloned.1.call-done = f32[48,3]{1,0:T(8,128)} async-done(((f32[1536,3]{1,0:T(8,128)}), f32[48,3]{1,0:T(8,128)}) %reduce-scatter.83.cloned.1.call-update) | async-done | bytes 592
  1025.6 44.0 %reduce-scatter.73.cloned.1.call-done = f32[384,192]{0,1:T(8,128)} async-done(((f32[384,1536]{0,1:T(8,128)}), f32[384,192]{0,1:T(8,128)}) %reduce-scatter.73.cloned.1.call-update) | async-done | bytes 294928 | tf_op jit(solution)/shard_map/reduce_scatter | solution.py:276
  1069.6 46.8 %reduce-scatter.81.cloned.1.call-done = f32[192,384]{1,0:T(8,128)} async-done(((f32[1536,384]{1,0:T(8,128)}), f32[192,384]{1,0:T(8,128)}) %reduce-scatter.81.cloned.1.call-update) | async-done | bytes 294928
  1116.4 46.5 %reduce-scatter.79.cloned.1.call-done = f32[192,384]{1,0:T(8,128)} async-done(((f32[1536,384]{1,0:T(8,128)}), f32[192,384]{1,0:T(8,128)}) %reduce-scatter.79.cloned.1.call-update) | async-done | bytes 294928
  1162.9 46.7 %reduce-scatter.71.cloned.1.call-done = f32[192,384]{1,0:T(8,128)} async-done(((f32[1536,384]{1,0:T(8,128)}), f32[192,384]{1,0:T(8,128)}) %reduce-scatter.71.cloned.1.call-update) | async-done | bytes 294928 | tf_op jit(solution)/shard_map/reduce_scatter | solution.py:273
  1209.6 46.5 %reduce-scatter.69.cloned.1.call-done = f32[384,192]{0,1:T(8,128)} async-done(((f32[384,1536]{0,1:T(8,128)}), f32[384,192]{0,1:T(8,128)}) %reduce-scatter.69.cloned.1.call-update) | async-done | bytes 294928 | tf_op jit(solution)/shard_map/reduce_scatter | solution.py:272
  1256.0 46.8 %reduce-scatter.67.cloned.1.call-done = f32[192,384]{1,0:T(8,128)} async-done(((f32[1536,384]{1,0:T(8,128)}), f32[192,384]{1,0:T(8,128)}) %reduce-scatter.67.cloned.1.call-update) | async-done | bytes 294928 | tf_op jit(solution)/shard_map/reduce_scatter | solution.py:271
  1302.8 46.3 %reduce-scatter.65.cloned.1.call-done = f32[192,384]{1,0:T(8,128)} async-done(((f32[1536,384]{1,0:T(8,128)}), f32[192,384]{1,0:T(8,128)}) %reduce-scatter.65.cloned.1.call-update) | async-done | bytes 294928 | tf_op jit(solution)/shard_map/reduce_scatter | solution.py:270
  1349.1 46.8 %reduce-scatter.63.cloned.1.call-done = f32[192,384]{1,0:T(8,128)} async-done(((f32[1536,384]{1,0:T(8,128)}), f32[192,384]{1,0:T(8,128)}) %reduce-scatter.63.cloned.1.call-update) | async-done | bytes 294928 | tf_op jit(solution)/shard_map/reduce_scatter | solution.py:269
  1395.9 80.6 %reduce-scatter.75.cloned.1.call-done = f32[192,1536]{1,0:T(8,128)} async-done(((f32[1536,1536]{1,0:T(8,128)}), f32[192,1536]{1,0:T(8,128)}) %reduce-scatter.75.cloned.1.call-update) | async-done | bytes 1179664 | tf_op jit(solution)/shard_map/reduce_scatter | solution.py:277
  1476.5 80.4 %reduce-scatter.77.cloned.1.call-done = f32[1536,192]{0,1:T(8,128)} async-done(((f32[1536,1536]{0,1:T(8,128)}), f32[1536,192]{0,1:T(8,128)}) %reduce-scatter.77.cloned.1.call-update) | async-done | bytes 1179664 | tf_op jit(solution)/shard_map/reduce_scatter | solution.py:278
  (638 shorter events, 467.5 us)
Async XLA Ops:
  7.2 159.3 %all-gather.19.cloned.1.call-start = ((), (), s32[]{:S(2)}) async-start(), calls=%async_computation.27 | async-start | bytes 1327104 | tf_op jit(solution)/shard_map/all_gather | solution.py:169
  7.9 160.9 %all-gather.21.cloned.1.call-start = ((), (), s32[]{:S(2)}) async-start(), calls=%async_computation.28 | async-start | bytes 1327104 | tf_op jit(solution)/shard_map/all_gather | solution.py:170
  8.7 162.2 %all-gather.17.cloned.1.call-start = ((), (), s32[]{:S(2)}) async-start(), calls=%async_computation.26 | async-start | bytes 1327104 | tf_op jit(solution)/shard_map/all_gather | solution.py:171
  9.4 164.7 %all-gather.23.cloned.1.call-start = ((), (), s32[]{:S(2)}) async-start(), calls=%async_computation.29 | async-start | bytes 1327104 | tf_op jit(solution)/shard_map/all_gather | solution.py:172
  10.0 188.5 %reduce-scatter.35.cloned.1.call-start = ((), (), s32[]{:S(2)}) async-start(), calls=%async_computation.30 | async-start | bytes 983040 | tf_op jit(solution)/shard_map/reduce_scatter | solution.py:56
  178.3 102.3 %reduce-scatter.41.cloned.1.call-start = ((), (), s32[]{:S(2)}) async-start(), calls=%async_computation.39 | async-start | bytes 983040 | tf_op jit(solution)/shard_map/reduce_scatter | solution.py:56
  233.1 94.2 %all-gather.31.cloned.1.call-start = ((), (), s32[]{:S(2)}) async-start(), calls=%async_computation.34 | async-start | bytes 1327104 | tf_op jit(solution)/shard_map/all_gather | solution.py:176
  233.7 186.5 %reduce-scatter.43.cloned.1.call-start = ((), (), s32[]{:S(2)}) async-start(), calls=%async_computation.40 | async-start | bytes 983040 | tf_op jit(solution)/shard_map/reduce_scatter | solution.py:56
  370.7 113.7 %all-gather.35.cloned.1.call-start = ((), (), s32[]{:S(2)}) async-start(), calls=%async_computation.37 | async-start | bytes 5308416 | tf_op jit(solution)/shard_map/all_gather | solution.py:178
  371.3 153.7 %reduce-scatter.47.cloned.1.call-start = ((), (), s32[]{:S(2)}) async-start(), calls=%async_computation.42 | async-start | bytes 983040 | tf_op jit(solution)/shard_map/reduce_scatter | solution.py:56
  524.5 136.2 %reduce-scatter.55.cloned.1.call-start = ((), (), s32[]{:S(2)}) async-start(), calls=%async_computation.46 | async-start | bytes 983040 | tf_op jit(solution)/shard_map/reduce_scatter | solution.py:56
  660.7 113.0 %reduce-scatter.57.cloned.1.call-start = ((), (), s32[]{:S(2)}) async-start(), calls=%async_computation.47 | async-start | bytes 983040 | tf_op jit(solution)/shard_map/reduce_scatter | solution.py:56
  773.3 151.4 %reduce-scatter.85.cloned.1.call-start = ((), (), s32[]{:S(2)}) async-start(), calls=%async_computation.61 | async-start | bytes 811008
  789.2 235.0 %reduce-scatter.83.cloned.1.call-start = ((), (), s32[]{:S(2)}) async-start(), calls=%async_computation.60 | async-start | bytes 811008
  790.6 279.0 %reduce-scatter.73.cloned.1.call-start = ((), (), s32[]{:S(2)}) async-start(), calls=%async_computation.55 | async-start | bytes 2654208 | tf_op jit(solution)/shard_map/reduce_scatter | solution.py:276
  794.5 321.9 %reduce-scatter.81.cloned.1.call-start = ((), (), s32[]{:S(2)}) async-start(), calls=%async_computation.59 | async-start | bytes 2654208
  800.9 362.0 %reduce-scatter.79.cloned.1.call-start = ((), (), s32[]{:S(2)}) async-start(), calls=%async_computation.58 | async-start | bytes 2654208
  807.2 402.3 %reduce-scatter.71.cloned.1.call-start = ((), (), s32[]{:S(2)}) async-start(), calls=%async_computation.54 | async-start | bytes 2654208 | tf_op jit(solution)/shard_map/reduce_scatter | solution.py:273
  811.1 444.9 %reduce-scatter.69.cloned.1.call-start = ((), (), s32[]{:S(2)}) async-start(), calls=%async_computation.53 | async-start | bytes 2654208 | tf_op jit(solution)/shard_map/reduce_scatter | solution.py:272
  814.9 487.9 %reduce-scatter.67.cloned.1.call-start = ((), (), s32[]{:S(2)}) async-start(), calls=%async_computation.52 | async-start | bytes 2654208 | tf_op jit(solution)/shard_map/reduce_scatter | solution.py:271
  818.8 530.3 %reduce-scatter.65.cloned.1.call-start = ((), (), s32[]{:S(2)}) async-start(), calls=%async_computation.51 | async-start | bytes 2654208 | tf_op jit(solution)/shard_map/reduce_scatter | solution.py:270
  822.4 573.6 %reduce-scatter.63.cloned.1.call-start = ((), (), s32[]{:S(2)}) async-start(), calls=%async_computation.50 | async-start | bytes 2654208 | tf_op jit(solution)/shard_map/reduce_scatter | solution.py:269
  825.9 650.6 %reduce-scatter.75.cloned.1.call-start = ((), (), s32[]{:S(2)}) async-start(), calls=%async_computation.56 | async-start | bytes 10616832 | tf_op jit(solution)/shard_map/reduce_scatter | solution.py:277
  833.9 723.1 %reduce-scatter.77.cloned.1.call-start = ((), (), s32[]{:S(2)}) async-start(), calls=%async_computation.57 | async-start | bytes 10616832 | tf_op jit(solution)/shard_map/reduce_scatter | solution.py:278
  (179 other events, 2266.7 us)
Sparse Core Ops, SparseCore 0:
  9.9 26.7 all-gather.18
  38.6 24.1 all-gather.20
  64.6 24.0 all-gather.16
  90.4 24.0 all-gather.22
  225.4 24.0 all-gather.24
  303.2 24.0 all-gather.30
  330.3 31.3 reduce-scatter.42
  370.1 31.7 reduce-scatter.36
  403.8 39.8 all-gather.32
  445.4 38.9 all-gather.34
  624.8 29.2 reduce-scatter.54
  721.4 31.9 reduce-scatter.56
  830.9 93.7 reduce-scatter.84
  929.7 94.5 reduce-scatter.82
  1028.0 41.5 reduce-scatter.72
  1073.9 42.4 reduce-scatter.80
  1120.4 42.4 reduce-scatter.78
  1167.0 42.4 reduce-scatter.70
  1213.5 42.4 reduce-scatter.68
  1260.3 42.4 reduce-scatter.66
  1306.6 42.4 reduce-scatter.64
  1353.4 42.4 reduce-scatter.62
  1400.0 76.4 reduce-scatter.74
  1480.4 76.4 reduce-scatter.76
  (12 shorter events, 264.5 us)
where the time goes:
time: 1570 us; the launch traced here: 1560 us
  waiting for transfers between devices  863 us (55%)
  blocking collectives  420 us (27%)
  matrix products  158 us (10%)
  local copies, waits for them, and re-layouts  64 us (4%)
  other arithmetic  39.6 us (3%)
  between operations  16.8 us (1%)
    unnamed x40, waiting for transfers between devices  274 us
    all_gather x12, blocking collectives, spread(): return lax.all_gather(local_rows, 'tensor', axis=0, tiled=True)  255 us
    reduce_scatter x12, waiting for transfers between devices, collect(): lax.psum_scatter(summed.astype(jnp.bfloat16), 'tensor', scatter_dimension...  119 us
    reduce_scatter x1, waiting for transfers between devices, on_device(): lax.psum_scatter(totals[8], 'dp', scatter_dimension=0, tiled=True)  80.6 us
    reduce_scatter x1, waiting for transfers between devices, on_device(): lax.psum_scatter(totals[9], 'dp', scatter_dimension=1, tiled=True)  80.4 us
    all_gather x1, blocking collectives, on_device(): lax.all_gather(norm_gains, ('dp', 'tensor'), axis=1, tiled=True)  70.7 us
    all_gather x1, blocking collectives, on_device(): lax.all_gather(norm_shifts, ('dp', 'tensor'), axis=1, tiled=True)  64.3 us
    dot_general x20, matrix products, product(): return jnp.dot(operand, matrix, preferred_element_type=jnp.float32)  60.6 us
  transfers between devices with their start and end apart: 36, of which 20 were waited for; matrix products, arithmetic and copies ran while one was open for 12% of the time, Pallas kernels for 0%

commit v1 on v0

v1 whole, which is shorter than its diff:
```python
import jax
import jax.numpy as jnp
from jax import lax
from jax.sharding import PartitionSpec as P

HEAD_DIM = 64
EPS = 1e-05
LOW = jnp.bfloat16
WIDE = jnp.float32


def norm_forward(values, gain, shift):
    average = jnp.mean(values, axis=-1, keepdims=True)
    centered = values - average
    variance = jnp.mean(centered * centered, axis=-1, keepdims=True)
    inverse = lax.rsqrt(variance + EPS)
    unit = centered * inverse
    return unit * gain + shift, unit, inverse


def norm_back(unit, inverse, gain, upstream):
    scaled = upstream * gain
    mean_scaled = jnp.mean(scaled, axis=-1, keepdims=True)
    mean_product = jnp.mean(scaled * unit, axis=-1, keepdims=True)
    change = inverse * (scaled - mean_scaled - unit * mean_product)
    return change, jnp.sum(upstream * unit, axis=0), jnp.sum(upstream, axis=0)


def gelu_exact(values):
    return jax.nn.gelu(values, approximate=False)


def product(operand, matrix):
    return jnp.dot(operand, matrix, preferred_element_type=WIDE)


def product_left(operand, matrix):
    return lax.dot_general(operand, matrix, (((0,), (0,)), ((), ())), preferred_element_type=WIDE)


def product_right(operand, matrix):
    return lax.dot_general(operand, matrix, (((1,), (1,)), ((), ())), preferred_element_type=WIDE)


def swap(value, axis, stride):
    size = lax.axis_size(axis)
    return lax.ppermute(value, axis, [(i, i ^ stride) for i in range(size)])


def levels():
    found, stride = [], 1
    for axis in ("tensor", "dp"):
        step = 1
        while step < lax.axis_size(axis):
            found.append((axis, step))
            step *= 2
    return found


def gather_small(value):
    for axis, step in levels():
        upper = (lax.axis_index(axis) // step) % 2 == 1
        other = swap(value, axis, step)
        value = jnp.where(
            upper,
            jnp.concatenate([other, value], axis=-1),
            jnp.concatenate([value, other], axis=-1),
        )
    return value


def scatter_small(value):
    for axis, step in reversed(levels()):
        upper = (lax.axis_index(axis) // step) % 2 == 1
        half = value.shape[-1] // 2
        low, high = value[..., :half], value[..., half:]
        other = swap(jnp.where(upper, low, high), axis, step)
        value = jnp.where(upper, high, low) + other
    return value


def spread(local):
    gathered = lax.all_gather(local, "tensor", axis=0, tiled=False)
    return gathered.reshape(-1, local.shape[-1])


def collect(partial, shape):
    summed = lax.psum_scatter(
        partial.astype(LOW), "tensor", scatter_dimension=0, tiled=True
    )
    return summed.astype(WIDE)


def by_heads(rows, count, seqs):
    frames = rows.shape[0] // (count * seqs)
    split = rows.reshape(count, seqs, frames, -1, HEAD_DIM)
    return split.transpose(1, 3, 0, 2, 4).reshape(seqs, -1, count * frames, HEAD_DIM)


def by_rows(heads, count, seqs):
    frames = heads.shape[2] // count
    split = heads.reshape(seqs, heads.shape[1], count, frames, HEAD_DIM)
    return split.transpose(2, 0, 3, 1, 4).reshape(count * seqs * frames, -1)


def weights_of(queries, keys, causal):
    scores = jnp.einsum("shqd,shkd->shqk", queries, keys, preferred_element_type=WIDE)
    scores = scores * HEAD_DIM**-0.5
    if causal:
        length = queries.shape[2]
        visible = jnp.arange(length)[:, None] >= jnp.arange(length)[None, :]
        scores = jnp.where(visible, scores, -1e30)
    largest = jnp.max(scores, axis=-1, keepdims=True)
    raw = jnp.exp(scores - largest)
    return raw / jnp.sum(raw, axis=-1, keepdims=True)


def attend(queries, keys, values, causal):
    chance = weights_of(queries, keys, causal).astype(LOW)
    return jnp.einsum("shqk,shkd->shqd", chance, values, preferred_element_type=WIDE).astype(LOW)


def attend_back(queries, keys, values, upstream, causal):
    chance = weights_of(queries, keys, causal)
    grad = jnp.einsum("shqd,shkd->shqk", upstream, values, preferred_element_type=WIDE)
    dots = jnp.sum(chance * grad, axis=-1, keepdims=True)
    score_grad = (chance * (grad - dots)).astype(LOW)
    scaling = HEAD_DIM**-0.5
    grad_q = jnp.einsum("shqk,shkd->shqd", score_grad, keys, preferred_element_type=WIDE)
    grad_k = jnp.einsum("shqk,shqd->shkd", score_grad, queries, preferred_element_type=WIDE)
    grad_v = jnp.einsum("shqk,shqd->shkd", chance.astype(LOW), upstream, preferred_element_type=WIDE)
    return (grad_q * scaling).astype(LOW), (grad_k * scaling).astype(LOW), grad_v.astype(LOW)


def on_device(
    frames,
    text_states,
    self_q,
    self_k,
    self_v,
    self_out,
    cross_q,
    cross_k,
    cross_v,
    cross_out,
    mlp_up,
    mlp_down,
    norm_gains,
    norm_shifts,
    cotangent,
):
    seqs, own, width = frames.shape
    text_own = text_states.shape[1]
    count = lax.axis_size("tensor")
    inner = self_q.shape[1]

    norms = gather_small(jnp.concatenate([norm_gains, norm_shifts], axis=0))
    gains, shifts = norms[:3], norms[3:]

    whole_grad = spread(cotangent.reshape(-1, width))
    whole_text = spread(text_states.reshape(-1, width))

    def gather(parts):
        joined = parts[0] if len(parts) == 1 else jnp.concatenate(parts, axis=1)
        return lax.all_gather(joined, "dp", axis=0, tiled=True)

    full_qkv = gather([self_q, self_k, self_v])
    full_mid = gather([self_out.T, cross_q, cross_k, cross_v, cross_out.T])
    full_mlp = gather([mlp_up, mlp_down.T])
    full_out = full_mid[:, :inner]
    full_cq = full_mid[:, inner : 2 * inner]
    full_ckv = full_mid[:, 2 * inner : 4 * inner]
    full_cout = full_mid[:, 4 * inner :]
    hidden_own = mlp_up.shape[1]
    full_up, full_down = full_mlp[:, :hidden_own], full_mlp[:, hidden_own:]

    x0 = frames.reshape(-1, width).astype(WIDE)
    a1, unit0, inverse0 = norm_forward(x0, gains[0], shifts[0])
    whole_self = spread(a1.astype(LOW))
    qkv = product(whole_self, full_qkv).astype(LOW)
    query1 = by_heads(qkv[:, :inner], count, seqs)
    key1 = by_heads(qkv[:, inner : 2 * inner], count, seqs)
    value1 = by_heads(qkv[:, 2 * inner :], count, seqs)
    mix1 = by_rows(attend(query1, key1, value1, True), count, seqs)
    x1 = x0 + collect(product_right(mix1, full_out), None)

    a2, unit1, inverse1 = norm_forward(x1, gains[1], shifts[1])
    whole_cross = spread(a2.astype(LOW))
    query2 = by_heads(product(whole_cross, full_cq).astype(LOW), count, seqs)
    text_kv = product(whole_text, full_ckv).astype(LOW)
    key2 = by_heads(text_kv[:, :inner], count, seqs)
    value2 = by_heads(text_kv[:, inner:], count, seqs)
    mix2 = by_rows(attend(query2, key2, value2, False), count, seqs)
    x2 = x1 + collect(product_right(mix2, full_cout), None)

    a3, unit2, inverse2 = norm_forward(x2, gains[2], shifts[2])
    whole_mlp = spread(a3.astype(LOW))
    hidden = product(whole_mlp, full_up)
    active_grad = product(whole_grad, full_down)
    active, pullback = jax.vjp(gelu_exact, hidden)
    active = active.astype(LOW)
    hidden_low = pullback(active_grad)[0].astype(LOW)
    h3 = collect(product_right(hidden_low, full_up), None)
    activations = (x2 + collect(product_right(active, full_down), None)).astype(LOW)

    def reduce(parts):
        joined = parts[0] if len(parts) == 1 else jnp.concatenate(parts, axis=1)
        return lax.psum_scatter(joined, "dp", scatter_dimension=0, tiled=True).astype(WIDE)

    sum_mlp = reduce(
        [
            product_left(whole_mlp, hidden_low).astype(LOW),
            product_left(whole_grad, active).astype(LOW),
        ]
    )

    e3 = cotangent.reshape(-1, width).astype(WIDE)
    change, gain2, shift2 = norm_back(unit2, inverse2, gains[2], h3)
    e2 = e3 + change
    whole_c2 = spread(e2.astype(LOW))
    d2 = by_heads(product(whole_c2, full_cout).astype(LOW), count, seqs)
    grad_q2, grad_k2, grad_v2 = attend_back(query2, key2, value2, d2, False)
    grad_q2 = by_rows(grad_q2, count, seqs)
    grad_kv2 = jnp.concatenate(
        [by_rows(grad_k2, count, seqs), by_rows(grad_v2, count, seqs)], axis=1
    )
    h2 = collect(product_right(grad_q2, full_cq), None)
    grad_text = collect(product_right(grad_kv2, full_ckv), None)
    sum_cross = reduce(
        [
            product_left(whole_cross, grad_q2).astype(LOW),
            product_left(whole_text, grad_kv2).astype(LOW),
            product_left(whole_c2, mix2).astype(LOW),
        ]
    )

    change, gain1, shift1 = norm_back(unit1, inverse1, gains[1], h2)
    e1 = e2 + change
    whole_c1 = spread(e1.astype(LOW))
    d1 = by_heads(product(whole_c1, full_out).astype(LOW), count, seqs)
    grads = attend_back(query1, key1, value1, d1, True)
    grad_qkv = jnp.concatenate([by_rows(part, count, seqs) for part in grads], axis=1)
    h1 = collect(product_right(grad_qkv, full_qkv), None)
    sum_self = reduce(
        [
            product_left(whole_self, grad_qkv).astype(LOW),
            product_left(whole_c1, mix1).astype(LOW),
        ]
    )
    change, gain0, shift0 = norm_back(unit0, inverse0, gains[0], h1)
    grad_frames = e1 + change

    norm_sums = scatter_small(jnp.stack([gain0, gain1, gain2, shift0, shift1, shift2]))

    def cut(joined, index):
        return joined[:, index * inner : (index + 1) * inner]

    return (
        activations.reshape(frames.shape),
        grad_frames.reshape(frames.shape),
        grad_text.reshape(text_states.shape),
        cut(sum_self, 0),
        cut(sum_self, 1),
        cut(sum_self, 2),
        cut(sum_self, 3).T,
        cut(sum_cross, 0),
        cut(sum_cross, 1),
        cut(sum_cross, 2),
        cut(sum_cross, 3).T,
        sum_mlp[:, :hidden_own],
        sum_mlp[:, hidden_own:].T,
        norm_sums[:3],
        norm_sums[3:],
    )


def solution(mesh):
    rows = P("dp", "tensor", None)
    into = P("dp", "tensor")
    out_of = P("tensor", "dp")
    norms = P(None, ("dp", "tensor"))
    weights = (into, into, into, out_of, into, into, into, out_of, into, out_of)
    return jax.shard_map(
        on_device,
        mesh=mesh,
        in_specs=(rows, rows, *weights, norms, norms, rows),
        out_specs=(rows, rows, rows, *weights, norms, norms),
        check_vma=False,
    )
```

time: 1570 us -> 898 us (0.57)
  blocking collectives: 420 us -> 17.6 us
  waiting for transfers between devices: 863 us -> 604 us
  matrix products: 158 us -> 97.9 us
  starting transfers between devices: 2.29 us -> 18.8 us
  local copies, waits for them, and re-layouts: 64 us -> 80 us
    all_gather x16 -> x1, blocking collectives: 420 us -> 17.6 us  [spread(): gathered = lax.all_gather(local, 'tensor', axis=0, tiled=False)]
    reduce_scatter x22 -> x7, waiting for transfers between devices: 557 us -> 200 us  [collect(): lax.psum_scatter(partial.astype(LOW), 'tensor', scatter_dimension=0, tile...]
    all_gather x10 -> x9, waiting for transfers between devices: 32.2 us -> 289 us  [the longest x6 169 us: spread(): gathered = lax.all_gather(local, 'tensor', axis=0, tiled=False)]
    unnamed x40 -> x22, waiting for transfers between devices: 274 us -> 107 us
    dot_general x44 -> x17, matrix products: 81.6 us -> 49.2 us  [the longest x7 36.7 us: product(): return jnp.dot(operand, matrix, preferred_element_type=WIDE)]
    dot_general x20 -> x7, matrix products: 39.1 us -> 15.7 us  [product_left(): lax.dot_general(operand, matrix, (((0,), (0,)), ((), ())), preferred_elem...]
    concatenate x0 -> x6, other arithmetic: none -> 21 us  [the longest x3 17.1 us: reduce(): joined = parts[0] if len(parts) == 1 else jnp.concatenate(parts, axis=1)]
    ppermute x0 -> x10, starting transfers between devices: none -> 16.5 us  [swap(): return lax.ppermute(value, axis, [(i, i ^ stride) for i in range(size)])]
  transfers between devices with their start and end apart: 36 -> 29, of which waited for: 20 -> 26; matrix products, arithmetic and copies ran while one was open for 12% -> 19% of each run, Pallas kernels for 0% -> 0%
where the time goes in v1:
time: 898 us; the launch traced here: 887 us
  waiting for transfers between devices  604 us (67%)
  matrix products  97.9 us (11%)
  local copies, waits for them, and re-layouts  80 us (9%)
  other arithmetic  52.9 us (6%)
  starting transfers between devices  18.8 us (2%)
  blocking collectives  17.6 us (2%)
  between operations  16 us (2%)
    reduce_scatter x7, waiting for transfers between devices, collect(): lax.psum_scatter(partial.astype(LOW), 'tensor', scatter_dimension=0, tile...  200 us
    all_gather x6, waiting for transfers between devices, spread(): gathered = lax.all_gather(local, 'tensor', axis=0, tiled=False)  169 us
    all_gather x3, waiting for transfers between devices, gather(): return lax.all_gather(joined, 'dp', axis=0, tiled=True)  120 us
    unnamed x22, waiting for transfers between devices  107 us
    unnamed x159, local copies, waits for them, and re-layouts  49 us
    dot_general x7, matrix products, product(): return jnp.dot(operand, matrix, preferred_element_type=WIDE)  36.7 us
    dot_general x7, matrix products, product_right(): lax.dot_general(operand, matrix, (((1,), (1,)), ((), ())), preferred_elem...  29.9 us
  transfers between devices with their start and end apart: 29, of which 26 were waited for; matrix products, arithmetic and copies ran while one was open for 19% of the time, Pallas kernels for 0%

profile of v1, /device:TPU:0, one launch (start us, length us, event | category | flops | bytes accessed | tf_op | source)
XLA Modules:
  0.0 887.2 jit_solution(10013777133366202010)
XLA Ops:
  31.5 36.1 %all-gather.14.cloned.1.call-done = bf16[4,128,1536]{2,1,0:T(8,128)(2,1)} async-done(((bf16[1,128,1536]{2,1,0:T(8,128)(2,1)}), bf16[4,128,1536]{2,1,0:T(8,128)(2,1)}) %all-gather.14.cloned.1.call-update) | async-done | bytes 1572880 | tf_op jit(solution)/shard_map/all_gather | solution.py:83
  67.6 35.3 %all-gather.16.cloned.1.call-done = bf16[1536,1152]{1,0:T(8,128)(2,1)} async-done(((bf16[192,1152]{1,0:T(8,128)(2,1)}), bf16[1536,1152]{1,0:T(8,128)(2,1)}) %all-gather.16.cloned.1.call-update) | async-done | bytes 3538960 | tf_op jit(solution)/shard_map/all_gather | solution.py:165
  121.3 28.0 %all-gather.18.cloned.1.call-done = bf16[1536,1920]{1,0:T(8,128)(2,1)} async-done(((bf16[192,1920]{1,0:T(8,128)(2,1)}), bf16[1536,1920]{1,0:T(8,128)(2,1)}) %all-gather.18.cloned.1.call-update) | async-done | bytes 5898256 | tf_op jit(solution)/shard_map/all_gather | solution.py:165
  153.0 35.2 %reduce-scatter.17.cloned.1.call-done = bf16[128,1536]{1,0:T(8,128)(2,1)} async-done(((bf16[512,1536]{1,0:T(8,128)(2,1)}), bf16[128,1536]{1,0:T(8,128)(2,1)}) %reduce-scatter.17.cloned.1.call-update) | async-done | bytes 393232 | tf_op jit(solution)/shard_map/reduce_scatter | solution.py:88
  192.7 17.6 %all_gather.48 = bf16[4,32,1536]{2,1,0:T(8,128)(2,1)S(1)} all-gather(bf16[1,32,1536]{2,1,0:T(8,128)(2,1)S(1)} %bitcast.263), channel_id=1, replica_groups=mesh['dp'=8,'tensor'=4] {'tensor'}, dimensions={0}, use_global_device_ids=true | all-gather | bytes 491520 | tf_op jit(solution)/shard_map/all_gather | solution.py:83
  213.7 16.6 %all-gather.24.cloned.1.call-done = bf16[512,1536]{1,0:T(8,128)(2,1)} async-done(((bf16[128,1536]{1,0:T(8,128)(2,1)}), bf16[512,1536]{1,0:T(8,128)(2,1)}) %all-gather.24.cloned.1.call-update) | async-done | bytes 1572880 | tf_op jit(solution)/shard_map/all_gather | solution.py:83
  243.5 32.8 %reduce-scatter.19.cloned.1.call-done = bf16[128,1536]{1,0:T(8,128)(2,1)} async-done(((bf16[512,1536]{1,0:T(8,128)(2,1)}), bf16[128,1536]{1,0:T(8,128)(2,1)}) %reduce-scatter.19.cloned.1.call-update) | async-done | bytes 393232 | tf_op jit(solution)/shard_map/reduce_scatter | solution.py:88
  279.9 56.6 %all-gather.20.cloned.1.call-done = bf16[1536,3072]{1,0:T(8,128)(2,1)} async-done(((bf16[192,3072]{1,0:T(8,128)(2,1)}), bf16[1536,3072]{1,0:T(8,128)(2,1)}) %all-gather.20.cloned.1.call-update) | async-done | bytes 9437200 | tf_op jit(solution)/shard_map/all_gather | solution.py:165
  336.6 39.3 %all-gather.26.cloned.1.call-done = bf16[512,1536]{1,0:T(8,128)(2,1)} async-done(((bf16[128,1536]{1,0:T(8,128)(2,1)}), bf16[512,1536]{1,0:T(8,128)(2,1)}) %all-gather.26.cloned.1.call-update) | async-done | bytes 1572880 | tf_op jit(solution)/shard_map/all_gather | solution.py:83
  375.8 13.0 %multiply_convert_fusion.1 = (bf16[512,1536]{1,0:T(8,128)(2,1)}, f32[512,1536]{1,0:T(8,128)}, f32[512,1536]{1,0:T(8,128)}) fusion(bf16[512,1536]{1,0:T(8,128)(2,1)} %all-gather.26.cloned.1.call-done, bf16[1536,3072]{1,0:T(8,128)(2,1)} %all-gather.20.cloned.1.call-done), kind=kOutput, calls=%fused_computation.24 | convolution fusion | flops 2467037184 | bytes 14155776 | tf_op jit(solution)/shard_map/dot_general | solution.py:34
  388.9 24.5 %all-gather.22.cloned.1.call-done = bf16[4,128,1536]{2,1,0:T(8,128)(2,1)} async-done(((bf16[1,128,1536]{2,1,0:T(8,128)(2,1)}), bf16[4,128,1536]{2,1,0:T(8,128)(2,1)}) %all-gather.22.cloned.1.call-update) | async-done | bytes 1572880 | tf_op jit(solution)/shard_map/all_gather | solution.py:83
  413.4 8.1 add_convert_fusion
  433.2 27.6 %reduce-scatter.23.cloned.1.call-done = bf16[128,1536]{1,0:T(8,128)(2,1)} async-done(((bf16[512,1536]{1,0:T(8,128)(2,1)}), bf16[128,1536]{1,0:T(8,128)(2,1)}) %reduce-scatter.23.cloned.1.call-update) | async-done | bytes 393232 | tf_op jit(solution)/shard_map/reduce_scatter | solution.py:88
  462.7 34.6 %reduce-scatter.21.cloned.1.call-done = bf16[128,1536]{1,0:T(8,128)(2,1)} async-done(((bf16[512,1536]{1,0:T(8,128)(2,1)}), bf16[128,1536]{1,0:T(8,128)(2,1)}) %reduce-scatter.21.cloned.1.call-update) | async-done | bytes 393232 | tf_op jit(solution)/shard_map/reduce_scatter | solution.py:88
  500.4 36.0 %all-gather.28.cloned.1.call-done = bf16[512,1536]{1,0:T(8,128)(2,1)} async-done(((bf16[128,1536]{1,0:T(8,128)(2,1)}), bf16[512,1536]{1,0:T(8,128)(2,1)}) %all-gather.28.cloned.1.call-update) | async-done | bytes 1572880 | tf_op jit(solution)/shard_map/all_gather | solution.py:83
  548.8 34.3 %reduce-scatter.25.cloned.1.call-done = bf16[128,1536]{1,0:T(8,128)(2,1)} async-done(((bf16[512,1536]{1,0:T(8,128)(2,1)}), bf16[128,1536]{1,0:T(8,128)(2,1)}) %reduce-scatter.25.cloned.1.call-update) | async-done | bytes 393232 | tf_op jit(solution)/shard_map/reduce_scatter | solution.py:88
  600.1 6.6 copy.184
  607.0 16.8 %all-gather.30.cloned.1.call-done = bf16[512,1536]{1,0:T(8,128)(2,1)} async-done(((bf16[128,1536]{1,0:T(8,128)(2,1)}), bf16[512,1536]{1,0:T(8,128)(2,1)}) %all-gather.30.cloned.1.call-update) | async-done | bytes 1572880 | tf_op jit(solution)/shard_map/all_gather | solution.py:83
  657.6 12.3 %pad_maximum_fusion = bf16[1536,3072]{0,1:T(8,128)(2,1)} fusion(bf16[1536,1536]{0,1:T(8,128)(2,1)S(1)} %fusion.2, bf16[1536,1536]{0,1:T(8,128)(2,1)S(1)} %convolution_convert_fusion.1), kind=kLoop, calls=%fused_computation.2 | loop fusion | flops 18874368 | bytes 18874368 | tf_op jit(solution)/shard_map/concatenate | solution.py:207
  669.9 12.9 %copy.186 = bf16[1536,3072]{1,0:T(8,128)(2,1)} copy(bf16[1536,3072]{0,1:T(8,128)(2,1)} %pad_maximum_fusion) | data formatting | bytes 18874368
  690.4 6.6 copy.182
  703.6 35.2 %reduce-scatter.27.cloned.1.call-done = bf16[128,1536]{1,0:T(8,128)(2,1)} async-done(((bf16[512,1536]{1,0:T(8,128)(2,1)}), bf16[128,1536]{1,0:T(8,128)(2,1)}) %reduce-scatter.27.cloned.1.call-update) | async-done | bytes 393232 | tf_op jit(solution)/shard_map/reduce_scatter | solution.py:88
  748.1 69.5 %reduce-scatter.35.cloned.1.call-done = bf16[192,3072]{1,0:T(8,128)(2,1)} async-done(((bf16[1536,3072]{1,0:T(8,128)(2,1)}), bf16[192,3072]{1,0:T(8,128)(2,1)}) %reduce-scatter.35.cloned.1.call-update) | async-done | bytes 1179664
  839.2 35.9 %reduce-scatter.31.cloned.1.call-done = bf16[192,1536]{1,0:T(8,128)(2,1)} async-done(((bf16[1536,1536]{1,0:T(8,128)(2,1)}), bf16[192,1536]{1,0:T(8,128)(2,1)}) %reduce-scatter.31.cloned.1.call-update) | async-done | bytes 589840
  (375 shorter events, 199.9 us)
Async XLA Ops:
  7.3 60.3 %all-gather.14.cloned.1.call-start = ((), (), s32[]{:S(2)}) async-start(), calls=%async_computation.10 | async-start | bytes 1966080 | tf_op jit(solution)/shard_map/all_gather | solution.py:83
  8.2 4.6 collective-permute-start
  13.6 4.6 collective-permute-start.1
  28.8 74.1 %all-gather.16.cloned.1.call-start = ((), (), s32[]{:S(2)}) async-start(), calls=%async_computation.11 | async-start | bytes 3981312 | tf_op jit(solution)/shard_map/all_gather | solution.py:165
  29.7 119.6 %all-gather.18.cloned.1.call-start = ((), (), s32[]{:S(2)}) async-start(), calls=%async_computation.12 | async-start | bytes 6635520 | tf_op jit(solution)/shard_map/all_gather | solution.py:165
  30.8 157.4 %reduce-scatter.17.cloned.1.call-start = ((), (), s32[]{:S(2)}) async-start(), calls=%async_computation.13 | async-start | bytes 1966080 | tf_op jit(solution)/shard_map/reduce_scatter | solution.py:88
  152.8 77.6 %all-gather.24.cloned.1.call-start = ((), (), s32[]{:S(2)}) async-start(), calls=%async_computation.22 | async-start | bytes 1966080 | tf_op jit(solution)/shard_map/all_gather | solution.py:83
  192.7 83.6 %reduce-scatter.19.cloned.1.call-start = ((), (), s32[]{:S(2)}) async-start(), calls=%async_computation.14 | async-start | bytes 1966080 | tf_op jit(solution)/shard_map/reduce_scatter | solution.py:88
  241.1 95.5 %all-gather.20.cloned.1.call-start = ((), (), s32[]{:S(2)}) async-start(), calls=%async_computation.15 | async-start | bytes 10616832 | tf_op jit(solution)/shard_map/all_gather | solution.py:165
  243.4 132.4 %all-gather.26.cloned.1.call-start = ((), (), s32[]{:S(2)}) async-start(), calls=%async_computation.23 | async-start | bytes 1966080 | tf_op jit(solution)/shard_map/all_gather | solution.py:83
  278.8 134.6 %all-gather.22.cloned.1.call-start = ((), (), s32[]{:S(2)}) async-start(), calls=%async_computation.17 | async-start | bytes 1966080 | tf_op jit(solution)/shard_map/all_gather | solution.py:83
  279.5 181.3 %reduce-scatter.23.cloned.1.call-start = ((), (), s32[]{:S(2)}) async-start(), calls=%async_computation.18 | async-start | bytes 1966080 | tf_op jit(solution)/shard_map/reduce_scatter | solution.py:88
  426.4 70.9 %reduce-scatter.21.cloned.1.call-start = ((), (), s32[]{:S(2)}) async-start(), calls=%async_computation.16 | async-start | bytes 1966080 | tf_op jit(solution)/shard_map/reduce_scatter | solution.py:88
  433.2 103.2 %all-gather.28.cloned.1.call-start = ((), (), s32[]{:S(2)}) async-start(), calls=%async_computation.24 | async-start | bytes 1966080 | tf_op jit(solution)/shard_map/all_gather | solution.py:83
  500.1 82.9 %reduce-scatter.25.cloned.1.call-start = ((), (), s32[]{:S(2)}) async-start(), calls=%async_computation.19 | async-start | bytes 1966080 | tf_op jit(solution)/shard_map/reduce_scatter | solution.py:88
  548.7 75.1 %all-gather.30.cloned.1.call-start = ((), (), s32[]{:S(2)}) async-start(), calls=%async_computation.25 | async-start | bytes 1966080 | tf_op jit(solution)/shard_map/all_gather | solution.py:83
  587.6 110.7 %reduce-scatter.29.cloned.1.call-start = ((), (), s32[]{:S(2)}) async-start(), calls=%async_computation.21 | async-start | bytes 491520 | tf_op jit(solution)/shard_map/reduce_scatter | solution.py:88
  593.5 107.8 %reduce-scatter.33.cloned.1.call-start = ((), (), s32[]{:S(2)}) async-start(), calls=%async_computation.27 | async-start | bytes 5308416
  606.7 132.0 %reduce-scatter.27.cloned.1.call-start = ((), (), s32[]{:S(2)}) async-start(), calls=%async_computation.20 | async-start | bytes 1966080 | tf_op jit(solution)/shard_map/reduce_scatter | solution.py:88
  649.6 168.0 %reduce-scatter.35.cloned.1.call-start = ((), (), s32[]{:S(2)}) async-start(), calls=%async_computation.28 | async-start | bytes 10616832
  682.8 192.3 %reduce-scatter.31.cloned.1.call-start = ((), (), s32[]{:S(2)}) async-start(), calls=%async_computation.26 | async-start | bytes 5308416
  742.1 77.4 %collective-permute-start.5 = (f32[6,768]{1,0:T(8,128)}, f32[6,768]{1,0:T(8,128)}, u32[]{:S(2)}, u32[]{:S(2)}) collective-permute-start(f32[6,768]{1,0:T(8,128)} %slice_select_fusion), channel_id=1, source_target_pairs={{0,16},{4,20},{8,24},{12,28},{16,0},{20,4},{24,8},{28,12},{1,17},{... | collective-permute-start | bytes 55304 | tf_op jit(solution)/shard_map/ppermute | solution.py:47
  820.9 7.3 collective-permute-start.6
  830.3 4.5 collective-permute-start.8
  (73 other events, 1273.8 us)
Sparse Core Ops, SparseCore 0:
  28.9 38.6 all-gather.13
  70.0 32.8 all-gather.15
  105.4 43.8 all-gather.17
  152.9 35.2 reduce-scatter.16
  192.8 37.5 all-gather.23
  241.2 35.0 reduce-scatter.18
  278.7 57.7 all-gather.19
  338.7 37.0 all-gather.25
  377.4 35.9 all-gather.21
  426.6 34.1 reduce-scatter.22
  463.1 34.2 reduce-scatter.20
  500.3 36.0 all-gather.27
  548.8 34.1 reduce-scatter.24
  587.7 36.0 all-gather.29
  626.0 19.4 reduce-scatter.28
  649.1 52.1 reduce-scatter.32
  703.5 35.2 reduce-scatter.26
  742.1 75.4 reduce-scatter.34
  821.1 53.9 reduce-scatter.30

commit v2 on v1

--- a/solution.py
+++ b/solution.py
@@ -1,6 +1,9 @@
+import functools
+
 import jax
 import jax.numpy as jnp
 from jax import lax
+from jax.experimental import pallas as pl
 from jax.sharding import PartitionSpec as P
 
 HEAD_DIM = 64
@@ -274,14 +277,677 @@
     )
 
 
+ROW, COLUMN, CORE, FAR, NEAR = 16, 8, 4, 2, 1
+
+
+def exchange(value, mask):
+    return lax.ppermute(value, ("dp", "tensor"), [(i, i ^ mask) for i in range(32)])
+
+
+def bit(mask):
+    index = lax.axis_index("dp") * 4 + lax.axis_index("tensor")
+    return (index // mask) % 2 == 1
+
+
+def ordered(flag, own, other, axis):
+    return jnp.where(
+        flag,
+        jnp.concatenate([other, own], axis=axis),
+        jnp.concatenate([own, other], axis=axis),
+    )
+
+
+def to_local_order(value):
+    width = value.shape[-1] // 8
+    parts = [value[..., i * width : (i + 1) * width] for i in range(8)]
+    column, core = bit(COLUMN), bit(CORE)
+    found = []
+    for near_core in range(2):
+        for near_column in range(2):
+            for row in range(2):
+
+                def pick(c, k):
+                    return parts[row * 4 + (near_column ^ c) * 2 + (near_core ^ k)]
+
+                found.append(
+                    jnp.where(
+                        column,
+                        jnp.where(core, pick(1, 1), pick(1, 0)),
+                        jnp.where(core, pick(0, 1), pick(0, 0)),
+                    )
+                )
+    return jnp.concatenate(found, axis=-1)
+
+
+def from_local_order(value):
+    width = value.shape[-1] // 8
+    parts = [value[..., i * width : (i + 1) * width] for i in range(8)]
+    column, core = bit(COLUMN), bit(CORE)
+    found = []
+    for row in range(2):
+        for there in range(2):
+            for side in range(2):
+
+                def pick(c, k):
+                    return parts[(side ^ k) * 4 + (there ^ c) * 2 + row]
+
+                found.append(
+                    jnp.where(
+                        column,
+                        jnp.where(core, pick(1, 1), pick(1, 0)),
+                        jnp.where(core, pick(0, 1), pick(0, 0)),
+                    )
+                )
+    return jnp.concatenate(found, axis=-1)
+
+
+def trade_rows(local):
+    far = bit(FAR)
+    keep = jnp.where(far, local[1], local[0])
+    give = jnp.where(far, local[0], local[1])
+    return jnp.concatenate([keep, exchange(give, FAR)], axis=0)
+
+
+def return_rows(local, kind):
+    half = local.shape[0] // 2
+    other = exchange(local[half:].astype(LOW), FAR).astype(kind)
+    own = local[:half].astype(kind)
+    far = bit(FAR)
+    return jnp.stack([jnp.where(far, other, own), jnp.where(far, own, other)])
+
+
+class Line:
+    def __init__(self):
+        self.last = None
+
+    def run(self, label, work, *values):
+        with jax.named_scope(label):
+            if self.last is not None:
+                values, _ = lax.optimization_barrier((values, self.last))
+            self.last = work(*values)
+            return self.last
+
+
+class Rows:
+    def __init__(self, line, label, first, second):
+        self.line, self.label, self.own = line, "rows_" + label, (first, second)
+        with jax.named_scope(self.label):
+            self.cross = exchange(first, ROW), exchange(second, NEAR)
+            self.rest = exchange(first, NEAR), exchange(second, ROW)
+
+    def relay(self):
+        one, two = self.line.run(self.label, lambda *v: v, *self.cross)
+        with jax.named_scope(self.label):
+            self.cross = one, two
+            self.both = exchange(one, NEAR), exchange(two, ROW)
+
+    def finish(self):
+        return self.line.run(
+            self.label,
+            lambda *v: jnp.concatenate(v, axis=0),
+            *self.own,
+            self.rest[0],
+            self.cross[1],
+            self.cross[0],
+            self.rest[1],
+            *self.both,
+        )
+
+
+class Sums:
+    def __init__(self, line, label, work, *values):
+        self.line, self.label = line, "sums_" + label
+
+        def pieces(*v):
+            low = work(*v).astype(LOW)
+            half = low.shape[0] // 8
+            return [low[i * half : (i + 1) * half] for i in range(8)]
+
+        self.piece = line.run(self.label, pieces, *values)
+        with jax.named_scope(self.label):
+            self.relays = exchange(self.piece[6], ROW), exchange(self.piece[7], NEAR)
+            self.direct = exchange(self.piece[4], ROW), exchange(self.piece[3], NEAR)
+
+    def relay(self):
+        def add(a, b, c, d):
+            return (
+                (a.astype(WIDE) + b.astype(WIDE)).astype(LOW),
+                (c.astype(WIDE) + d.astype(WIDE)).astype(LOW),
+            )
+
+        one, two = self.line.run(
+            self.label, add, self.piece[2], self.relays[0], self.piece[5], self.relays[1]
+        )
+        with jax.named_scope(self.label):
+            self.second = exchange(one, NEAR), exchange(two, ROW)
+
+    def finish(self, work, *more):
+        def total(a, b, c, d, e, f, *v):
+            first = a.astype(WIDE) + b.astype(WIDE) + c.astype(WIDE)
+            second = d.astype(WIDE) + e.astype(WIDE) + f.astype(WIDE)
+            return work(jnp.concatenate([first, second], axis=0), *v)
+
+        return self.line.run(
+            self.label,
+            total,
+            self.piece[0],
+            self.direct[0],
+            self.second[0],
+            self.piece[1],
+            self.direct[1],
+            self.second[1],
+            *more,
+        )
+
+
+class Weights:
+    def __init__(self, line, label, *parts):
+        self.line, self.label = line, "weights_" + label
+        self.cuts = [part.shape[1] // 2 for part in parts]
+
+        def split(*shards):
+            row = bit(ROW)
+            lows = jnp.concatenate([p[:, :c] for p, c in zip(shards, self.cuts)], axis=1)
+            highs = jnp.concatenate([p[:, c:] for p, c in zip(shards, self.cuts)], axis=1)
+            return jnp.where(row, highs, lows), jnp.where(row, lows, highs)
+
+        self.own, give = line.run(self.label, split, *parts)
+        self.send(give, ROW)
+
+    def send(self, value, mask):
+        with jax.named_scope(self.label):
+            self.got = exchange(value, mask)
+
+    def far(self):
+        self.own = self.line.run(
+            self.label, lambda o, g: ordered(bit(ROW), o, g, 0), self.own, self.got
+        )
+        self.send(self.own, FAR)
+
+    def column(self):
+        def join(own, other):
+            pieces, start = [], 0
+            for c in self.cuts:
+                pieces += [own[:, start : start + c], other[:, start : start + c]]
+                start += c
+            return jnp.concatenate(pieces, axis=1)
+
+        self.own = self.line.run(self.label, join, self.own, self.got)
+        self.send(self.own, COLUMN)
+
+    def core(self):
+        self.own = self.line.run(
+            self.label, lambda o, g: jnp.concatenate([o, g], axis=0), self.own, self.got
+        )
+        self.send(self.own, CORE)
+
+    def finish(self):
+        return self.line.run(
+            self.label, lambda o, g: jnp.concatenate([o, g], axis=0), self.own, self.got
+        )
+
+
+class Gradients:
+    def __init__(self, line, label, cuts, work, *values):
+        self.line, self.label, self.cuts = line, "grads_" + label, cuts
+
+        def halves(*v):
+            pairs = work(*v)
+            keep = [gradient(a[:, : a.shape[1] // 2], u).astype(LOW) for a, u in pairs]
+            give = [gradient(a[:, a.shape[1] // 2 :], u).astype(LOW) for a, u in pairs]
+            return (join(keep, 1), join(give, 1))
+
+        self.own, give = line.run(self.label, halves, *values)
+        self.send(give, CORE)
+
+    def send(self, value, mask):
+        with jax.named_scope(self.label):
+            self.got = exchange(value, mask)
+
+    def column(self):
+        def cut(own, got):
+            half = own.shape[0] // 2
+            return (
+                (own[:half].astype(WIDE) + got[:half].astype(WIDE)).astype(LOW),
+                (own[half:].astype(WIDE) + got[half:].astype(WIDE)).astype(LOW),
+            )
+
+        self.own, give = self.line.run(self.label, cut, self.own, self.got)
+        self.send(give, COLUMN)
+
+    def far(self):
+        def cut(own, got):
+            total = own.astype(WIDE) + got.astype(WIDE)
+            stay, leave, start = [], [], 0
+            for c in self.cuts:
+                stay.append(total[:, start : start + c])
+                leave.append(total[:, start + c : start + 2 * c])
+                start += 2 * c
+            return join(stay, 1), join(leave, 1).astype(LOW)
+
+        self.own, give = self.line.run(self.label, cut, self.own, self.got)
+        self.send(give, FAR)
+
+    def row(self):
+        def cut(own, got):
+            total = own + got.astype(WIDE)
+            row, half = bit(ROW), own.shape[0] // 2
+            return (
+                jnp.where(row, total[half:], total[:half]),
+                jnp.where(row, total[:half], total[half:]).astype(LOW),
+            )
+
+        self.own, give = self.line.run(self.label, cut, self.own, self.got)
+        self.send(give, ROW)
+
+    def finish(self):
+        def place(own, got):
+            got, row = got.astype(WIDE), bit(ROW)
+            found, start = [], 0
+            for c in self.cuts:
+                found.append(ordered(row, own[:, start : start + c], got[:, start : start + c], 1))
+                start += c
+            return found
+
+        return self.line.run(self.label, place, self.own, self.got)
+
+
+def join(parts, axis):
+    return parts[0] if len(parts) == 1 else jnp.concatenate(parts, axis=axis)
+
+
+def gradient(operand, upstream):
+    return product_left(operand, upstream)
+
+
+def head_weights(queries, keys, mask):
+    scores = lax.dot_general(queries, keys, (((1,), (1,)), ((), ())), preferred_element_type=WIDE)
+    scores = scores * HEAD_DIM**-0.5
+    if mask is not None:
+        scores = jnp.where(mask, scores, -1e30)
+    raw = jnp.exp(scores - jnp.max(scores, axis=-1, keepdims=True))
+    return raw * (1.0 / jnp.sum(raw, axis=-1, keepdims=True))
+
+
+def attend_kernel(heads, causal, q_ref, k_ref, v_ref, down_ref, along_ref, out_ref):
+    mask = down_ref[...] >= along_ref[...] if causal else None
+    for head in range(heads):
+        columns = slice(head * HEAD_DIM, (head + 1) * HEAD_DIM)
+        chance = head_weights(q_ref[:, columns], k_ref[:, columns], mask)
+        mixed = jnp.dot(chance.astype(LOW), v_ref[:, columns], preferred_element_type=WIDE)
+        out_ref[:, columns] = mixed.astype(LOW)
+
+
+def attend_back_kernel(
+    heads, causal, q_ref, k_ref, v_ref, up_ref, down_ref, along_ref, dq_ref, dk_ref, dv_ref
+):
+    mask = down_ref[...] >= along_ref[...] if causal else None
+    scaling = HEAD_DIM**-0.5
+    for head in range(heads):
+        columns = slice(head * HEAD_DIM, (head + 1) * HEAD_DIM)
+        queries, keys, upstream = q_ref[:, columns], k_ref[:, columns], up_ref[:, columns]
+        chance = head_weights(queries, keys, mask)
+        grad = lax.dot_general(
+            upstream, v_ref[:, columns], (((1,), (1,)), ((), ())), preferred_element_type=WIDE
+        )
+        dots = jnp.sum(chance * grad, axis=-1, keepdims=True)
+        score_grad = (chance * (grad - dots)).astype(LOW)
+        dq_ref[:, columns] = (
+            jnp.dot(score_grad, keys, preferred_element_type=WIDE) * scaling
+        ).astype(LOW)
+        dk_ref[:, columns] = (product_left(score_grad, queries) * scaling).astype(LOW)
+        dv_ref[:, columns] = product_left(chance.astype(LOW), upstream).astype(LOW)
+
+
+def column_block(rows, width, index):
+    return pl.BlockSpec((rows, width), lambda s: (s, index))
+
+
+def attention(queries, keys, values, places, causal):
+    width = places[2]
+    rows, key_rows = queries[0].shape[0] // 2, keys[0].shape[0] // 2
+    heads = width // HEAD_DIM
+    return pl.pallas_call(
+        functools.partial(attend_kernel, heads, causal),
+        grid=(2,),
+        in_specs=[
+            column_block(rows, width, queries[1]),
+            column_block(key_rows, width, keys[1]),
+            column_block(key_rows, width, values[1]),
+            pl.BlockSpec(places[0].shape, lambda s: (0, 0)),
+            pl.BlockSpec(places[1].shape, lambda s: (0, 0)),
+        ],
+        out_specs=column_block(rows, width, 0),
+        out_shape=jax.ShapeDtypeStruct((2 * rows, width), LOW),
+        cost_estimate=pl.CostEstimate(
+            flops=8 * rows * key_rows * width, bytes_accessed=8 * rows * width * 2, transcendentals=2 * heads * rows * key_rows
+        ),
+        name="attend",
+    )(queries[0], keys[0], values[0], places[0], places[1])
+
+
+def attention_back(queries, keys, values, upstream, places, causal):
+    width = places[2]
+    rows, key_rows = queries[0].shape[0] // 2, keys[0].shape[0] // 2
+    heads = width // HEAD_DIM
+    return pl.pallas_call(
+        functools.partial(attend_back_kernel, heads, causal),
+        grid=(2,),
+        in_specs=[
+            column_block(rows, width, queries[1]),
+            column_block(key_rows, width, keys[1]),
+            column_block(key_rows, width, values[1]),
+            column_block(rows, width, 0),
+            pl.BlockSpec(places[0].shape, lambda s: (0, 0)),
+            pl.BlockSpec(places[1].shape, lambda s: (0, 0)),
+        ],
+        out_specs=[
+            column_block(rows, width, 0),
+            column_block(key_rows, width, 0),
+            column_block(key_rows, width, 0),
+        ],
+        out_shape=[
+            jax.ShapeDtypeStruct((2 * rows, width), LOW),
+            jax.ShapeDtypeStruct((2 * key_rows, width), LOW),
+            jax.ShapeDtypeStruct((2 * key_rows, width), LOW),
+        ],
+        cost_estimate=pl.CostEstimate(
+            flops=20 * rows * key_rows * width, bytes_accessed=14 * rows * width * 2, transcendentals=2 * heads * rows * key_rows
+        ),
+        name="attend_back",
+    )(queries[0], keys[0], values[0], upstream, places[0], places[1])
+
+
+def on_device_pairs(
+    frames,
+    text_states,
+    self_q,
+    self_k,
+    self_v,
+    self_out,
+    cross_q,
+    cross_k,
+    cross_v,
+    cross_out,
+    mlp_up,
+    mlp_down,
+    norm_gains,
+    norm_shifts,
+    cotangent,
+):
+    inner, units = self_q.shape[1], mlp_up.shape[1]
+    own_frames = frames.shape[1]
+    line = Line()
+
+    far_bit = bit(FAR)
+
+    def divide(v):
+        return jnp.where(far_bit, v[1], v[0]), jnp.where(far_bit, v[0], v[1])
+
+    keep_frames, give_frames = line.run("frames", divide, frames)
+    got_frames = exchange(give_frames, FAR)
+    w_qkv = Weights(line, "qkv", self_q, self_k, self_v)
+    w_out = Weights(line, "out", self_out.T)
+    norms = line.run("norms", lambda a, b: jnp.concatenate([a, b], axis=0), norm_gains, norm_shifts)
+    for axis, step in levels():
+        got = swap(norms, axis, step)
+        upper = (lax.axis_index(axis) // step) % 2 == 1
+        norms = line.run("norms", lambda o, g: ordered(upper, o, g, 1), norms, got)
+        if step == 1 and axis == "dp":
+            w_qkv.far()
+    norms = line.run("norms", to_local_order, norms)
+    gains, shifts = norms[:3], norms[3:]
+
+    near, far = bit(NEAR).astype(jnp.int32), bit(FAR).astype(jnp.int32)
+    starts = [2 * far + near, 2 * (1 - far) + near, 2 * far + 1 - near, 2 * (1 - far) + 1 - near]
+    steps = jnp.arange(own_frames, dtype=jnp.int32)
+    position = jnp.concatenate([start * own_frames + steps for start in starts])
+    places = (position[:, None], position[None, :], inner)
+
+    def halves(v):
+        half = v.shape[0] // 2
+        return v[:half], v[half:]
+
+    def open_rows(kept, got, gain, shift):
+        x0 = to_local_order(jnp.concatenate([kept, got], axis=0)).astype(WIDE)
+        a1, unit, inverse = norm_forward(x0, gain, shift)
+        return (x0, unit, inverse, *halves(a1.astype(LOW)))
+
+    x0, unit0, inverse0, *a1 = line.run(
+        "norm0", open_rows, keep_frames, got_frames, gains[0], shifts[0]
+    )
+    rows_a1 = Rows(line, "a1", *a1)
+    w_out.far()
+    keep_text, give_text = line.run("text", divide, text_states)
+    got_text = exchange(give_text, FAR)
+    keep_grad, give_grad = line.run("cotangent", divide, cotangent)
+    got_grad = exchange(give_grad, FAR)
+    w_mid = Weights(line, "mid", cross_q, cross_k, cross_v, cross_out.T)
+    w_up = Weights(line, "up", mlp_up)
+    w_down = Weights(line, "down", mlp_down.T)
+    rows_a1.relay()
+    w_qkv.column()
+    w_out.column()
+    w_mid.far()
+    whole_self = rows_a1.finish()
+    w_up.far()
+    w_down.far()
+
+    def trade(kept, got):
+        return halves(to_local_order(jnp.concatenate([kept, got], axis=0)))
+
+    text_local = line.run("text", trade, keep_text, got_text)
+    rows_text = Rows(line, "text", *text_local)
+    grad_local = line.run("cotangent", trade, keep_grad, got_grad)
+    rows_c3 = Rows(line, "c3", *grad_local)
+    w_qkv.core()
+    rows_text.relay()
+    full_qkv = w_qkv.finish()
+    w_out.core()
+    rows_c3.relay()
+    qkv = line.run("qkv", lambda a, w: product(a, w).astype(LOW), whole_self, full_qkv)
+    full_out = w_out.finish()
+    w_mid.column()
+    mix1 = line.run("mix1", lambda q: attention((q, 0), (q, 1), (q, 2), places, True), qkv)
+    sums_x1 = Sums(line, "x1", product_right, mix1, full_out)
+    whole_text = rows_text.finish()
+    whole_grad = rows_c3.finish()
+    sums_x1.relay()
+    w_up.column()
+
+    def open_next(total, before, gain, shift):
+        x = before + total
+        a, unit, inverse = norm_forward(x, gain, shift)
+        return (x, unit, inverse, *halves(a.astype(LOW)))
+
+    x1, unit1, inverse1, *a2 = sums_x1.finish(open_next, x0, gains[1], shifts[1])
+    rows_a2 = Rows(line, "a2", *a2)
+    w_mid.core()
+    rows_a2.relay()
+    full_mid = w_mid.finish()
+    full_cq = full_mid[:, :inner]
+    full_ckv = full_mid[:, inner : 3 * inner]
+    full_cout = full_mid[:, 3 * inner :]
+    text_kv = line.run(
+        "text_kv", lambda a, w: product(a, w).astype(LOW), whole_text, full_ckv
+    )
+    whole_cross = rows_a2.finish()
+    query2 = line.run("query2", lambda a, w: product(a, w).astype(LOW), whole_cross, full_cq)
+    mix2 = line.run(
+        "mix2",
+        lambda q, kv: attention((q, 0), (kv, 0), (kv, 1), places, False),
+        query2,
+        text_kv,
+    )
+    sums_x2 = Sums(line, "x2", product_right, mix2, full_cout)
+    w_up.core()
+    w_down.column()
+    sums_x2.relay()
+    full_up = w_up.finish()
+    x2, unit2, inverse2, *a3 = sums_x2.finish(open_next, x1, gains[2], shifts[2])
+    rows_a3 = Rows(line, "a3", *a3)
+    w_down.core()
+    rows_a3.relay()
+    full_down = w_down.finish()
+    active_grad = line.run("active_grad", product, whole_grad, full_down)
+    whole_mlp = rows_a3.finish()
+
+    def middle(rows, weights, upstream):
+        hidden = product(rows, weights)
+        active, pullback = jax.vjp(gelu_exact, hidden)
+        return active.astype(LOW), pullback(upstream)[0].astype(LOW)
+
+    active, hidden_low = line.run("hidden", middle, whole_mlp, full_up, active_grad)
+    sums_h3 = Sums(line, "h3", product_right, hidden_low, full_up)
+    g_up = Gradients(line, "up", [units // 2], lambda a, u: [(a, u)], whole_mlp, hidden_low)
+    sums_h3.relay()
+    g_up.column()
+    g_down = Gradients(line, "down", [units // 2], lambda a, u: [(a, u)], whole_grad, active)
+
+    def close_norm(total, unit, inverse, gain, before):
+        change, gain_grad, shift_grad = norm_back(unit, inverse, gain, total)
+        e = before + change
+        return (e, gain_grad, shift_grad, *halves(e.astype(LOW)))
+
+    e3 = jnp.concatenate(grad_local, axis=0).astype(WIDE)
+    e2, gain2, shift2, *c2 = sums_h3.finish(close_norm, unit2, inverse2, gains[2], e3)
+    rows_c2 = Rows(line, "c2", *c2)
+    g_down.column()
+    rows_c2.relay()
+    sums_act = Sums(line, "act", product_right, active, full_down)
+    whole_c2 = rows_c2.finish()
+    d2 = line.run("d2", lambda a, w: product(a, w).astype(LOW), whole_c2, full_cout)
+    grad_q2, grad_k2, grad_v2 = line.run(
+        "mix2_back",
+        lambda q, kv, d: attention_back((q, 0), (kv, 0), (kv, 1), d, places, False),
+        query2,
+        text_kv,
+        d2,
+    )
+    sums_h2 = Sums(line, "h2", product_right, grad_q2, full_cq)
+    g_up.far()
+    sums_act.relay()
+    g_cross = Gradients(
+        line,
+        "cross",
+        [inner // 2] * 4,
+        lambda a, q, t, k, v, c, m: [(a, q), (t, k), (t, v), (c, m)],
+        whole_cross,
+        grad_q2,
+        whole_text,
+        grad_k2,
+        grad_v2,
+        whole_c2,
+        mix2,
+    )
+    sums_h2.relay()
+    g_cross.column()
+    sums_text = Sums(
+        line,
+        "text",
+        lambda k, v, w: product_right(k, w[:, :inner]) + product_right(v, w[:, inner:]),
+        grad_k2,
+        grad_v2,
+        full_ckv,
+    )
+    e1, gain1, shift1, *c1 = sums_h2.finish(close_norm, unit1, inverse1, gains[1], e2)
+    rows_c1 = Rows(line, "c1", *c1)
+    g_down.far()
+    rows_c1.relay()
+    g_up.row()
+    sums_text.relay()
+    whole_c1 = rows_c1.finish()
+    d1 = line.run("d1", lambda a, w: product(a, w).astype(LOW), whole_c1, full_out)
+    grads1 = line.run(
+        "mix1_back",
+        lambda q, d: attention_back((q, 0), (q, 1), (q, 2), d, places, True),
+        qkv,
+        d1,
+    )
+    grad_qkv = jnp.concatenate(grads1, axis=1)
+    sums_h1 = Sums(line, "h1", product_right, grad_qkv, full_qkv)
+    g_self = Gradients(
+        line,
+        "self",
+        [inner // 2] * 4,
+        lambda a, u, c, m: [(a, u), (c, m)],
+        whole_self,
+        grad_qkv,
+        whole_c1,
+        mix1,
+    )
+    sums_h1.relay()
+    g_self.column()
+    g_cross.far()
+    g_down.row()
+    e0, gain0, shift0, *_ = sums_h1.finish(close_norm, unit0, inverse0, gains[0], e1)
+
+    def leave(local):
+        local = from_local_order(local)
+        half = local.shape[0] // 2
+        return local[:half], local[half:].astype(LOW)
+
+    keep_e0, give_e0 = line.run("frames", leave, e0)
+    got_e0 = exchange(give_e0, FAR)
+    act_local = sums_act.finish(lambda total, x: (x + total).astype(LOW), x2)
+    keep_act, give_act = line.run("act", leave, act_local)
+    got_act = exchange(give_act, FAR)
+    text_sum = sums_text.finish(lambda total: total)
+    keep_text, give_text = line.run("text", leave, text_sum)
+    got_text = exchange(give_text, FAR)
+    norm_sums = jnp.stack([gain0, gain1, gain2, shift0, shift1, shift2])
+    norm_sums = line.run("norm_sums", from_local_order, norm_sums)
+    g_self.far()
+    g_cross.row()
+    for axis, step in reversed(levels()):
+        upper = (lax.axis_index(axis) // step) % 2 == 1
+        half = norm_sums.shape[1] // 2
+        give = line.run("norm_sums", lambda v: jnp.where(upper, v[:, :half], v[:, half:]), norm_sums)
+        got = swap(give, axis, step)
+        norm_sums = line.run(
+            "norm_sums",
+            lambda v, g: jnp.where(upper, v[:, half:], v[:, :half]) + g,
+            norm_sums,
+            got,
+        )
+    (grad_up,) = g_up.finish()
+    (grad_down,) = g_down.finish()
+    grad_cq, grad_ck, grad_cv, grad_cout = g_cross.finish()
+    g_self.row()
+    grad_q, grad_k, grad_v, grad_out = g_self.finish()
+
+    def arrive(own, other):
+        own, other = own, other.astype(own.dtype)
+        return jnp.stack([jnp.where(far_bit, other, own), jnp.where(far_bit, own, other)])
+
+    return (
+        arrive(keep_act, got_act),
+        arrive(keep_e0, got_e0),
+        arrive(keep_text, got_text),
+        grad_q,
+        grad_k,
+        grad_v,
+        grad_out.T,
+        grad_cq,
+        grad_ck,
+        grad_cv,
+        grad_cout.T,
+        grad_up,
+        grad_down.T,
+        norm_sums[:3],
+        norm_sums[3:],
+    )
+
+
 def solution(mesh):
     rows = P("dp", "tensor", None)
     into = P("dp", "tensor")
     out_of = P("tensor", "dp")
     norms = P(None, ("dp", "tensor"))
     weights = (into, into, into, out_of, into, into, into, out_of, into, out_of)
+    paired = dict(mesh.shape) == {"dp": 8, "tensor": 4}
     return jax.shard_map(
-        on_device,
+        on_device_pairs if paired else on_device,
         mesh=mesh,
         in_specs=(rows, rows, *weights, norms, norms, rows),
         out_specs=(rows, rows, rows, *weights, norms, norms),

time: 898 us -> 648 us (0.72)
  waiting for transfers between devices: 604 us -> 266 us
  starting transfers between devices: 18.8 us -> 138 us
  matrix products: 97.9 us -> 55.3 us
  Pallas kernels: 0 us -> 28.2 us
  other arithmetic: 52.9 us -> 76.1 us
  blocking collectives: 17.6 us -> 0 us
  between operations: 16 us -> 3.46 us
    all_gather x9 -> x0, waiting for transfers between devices: 289 us -> none  [the longest x6 169 us: spread(): gathered = lax.all_gather(local, 'tensor', axis=0, tiled=False)]
    ppermute x0 -> x126, waiting for transfers between devices: none -> 254 us  [exchange(): lax.ppermute(value, ('dp', 'tensor'), [(i, i ^ mask) for i in range(32)])]
    reduce_scatter x7 -> x0, waiting for transfers between devices: 200 us -> none  [collect(): lax.psum_scatter(partial.astype(LOW), 'tensor', scatter_dimension=0, tile...]
    ppermute x0 -> x126, starting transfers between devices: none -> 125 us  [exchange(): lax.ppermute(value, ('dp', 'tensor'), [(i, i ^ mask) for i in range(32)])]
    unnamed x22 -> x0, waiting for transfers between devices: 107 us -> none
    pallas_call x0 -> x4, Pallas kernels: none -> 28.2 us  [the longest x2 17.2 us: attention_back(): pl.pallas_call(functools.partial(attend_back_kernel, heads, causal), grid...]
    select_n x10 -> x50, other arithmetic: 2.45 us -> 27.9 us  [the longest x17 11.7 us: ordered(): jnp.where(flag, jnp.concatenate([other, own], axis=axis), jnp.concatenate...]
    reshape x36 -> x0, local copies, waits for them, and re-layouts: 21.2 us -> none  [the longest x14 9.46 us: by_rows(): split = heads.reshape(seqs, heads.shape[1], count, frames, HEAD_DIM)]
  transfers between devices with their start and end apart: 29 -> 136, of which waited for: 26 -> 56; matrix products, arithmetic and copies ran while one was open for 19% -> 23% of each run, Pallas kernels for 0% -> 3%
where the time goes in v2:
time: 648 us; the launch traced here: 642 us
  waiting for transfers between devices  266 us (41%)
  starting transfers between devices  138 us (21%)
  other arithmetic  76.1 us (12%)
  local copies, waits for them, and re-layouts  75.2 us (12%)
  matrix products  55.3 us (9%)
  Pallas kernels  28.2 us (4%)
    ppermute x126, waiting for transfers between devices, exchange(): lax.ppermute(value, ('dp', 'tensor'), [(i, i ^ mask) for i in range(32)])  254 us
    ppermute x126, starting transfers between devices, exchange(): lax.ppermute(value, ('dp', 'tensor'), [(i, i ^ mask) for i in range(32)])  125 us
    unnamed x240, local copies, waits for them, and re-layouts  35 us
    dot_general x7, matrix products, product(): return jnp.dot(operand, matrix, preferred_element_type=WIDE)  24.9 us
    dot_general x8, matrix products, product_right(): lax.dot_general(operand, matrix, (((1,), (1,)), ((), ())), preferred_elem...  17.3 us
    pallas_call x2, Pallas kernels, attention_back(): pl.pallas_call(functools.partial(attend_back_kernel, heads, causal), grid...  17.2 us
    dot_general x16, matrix products, product_left(): lax.dot_general(operand, matrix, (((0,), (0,)), ((), ())), preferred_elem...  13.1 us
  transfers between devices with their start and end apart: 136, of which 56 were waited for; matrix products, arithmetic and copies ran while one was open for 23% of the time, Pallas kernels for 3%

profile of v2, /device:TPU:0, one launch (start us, length us, event | category | flops | bytes accessed | tf_op | source)
XLA Modules:
  0.0 641.7 jit_solution(4015344048673794338)
XLA Ops:
  24.8 18.6 %collective-permute-done = bf16[64,1536]{1,0:T(8,128)(2,1)S(1)} collective-permute-done((bf16[64,1536]{1,0:T(8,128)(2,1)S(1)}, bf16[64,1536]{1,0:T(8,128)(2,1)S(1)}, u32[]{:S(2)}, u32[]{:S(2)}) %collective-permute-start) | collective-permute-done | bytes 196640 | tf_op jit(solution)/shard_map/ppermute | solution.py:284
  88.3 16.7 %collective-permute-done.17 = bf16[384,1152]{1,0:T(8,128)(2,1)S(1)} collective-permute-done((bf16[384,1152]{1,0:T(8,128)(2,1)S(1)}, bf16[384,1152]{1,0:T(8,128)(2,1)S(1)}, u32[]{:S(2)}, u32[]{:S(2)}) %collective-permute-start.17) | collective-permute-done | bytes 884768 | tf_op jit(solution)/shard_map/weights_qkv/ppermute | solution.py:284
  122.7 5.7 convolution_convert_fusion.7.q_ref.k_ref.v_ref
  131.4 17.4 %collective-permute-done.28 = bf16[384,768]{1,0:T(8,128)(2,1)S(1)} collective-permute-done((bf16[384,768]{1,0:T(8,128)(2,1)S(1)}, bf16[384,768]{1,0:T(8,128)(2,1)S(1)}, u32[]{:S(2)}, u32[]{:S(2)}) %collective-permute-start.28) | collective-permute-done | bytes 589856 | tf_op jit(solution)/shard_map/weights_mid/ppermute | solution.py:284
  154.0 6.9 %attend.2 = bf16[512,384]{1,0:T(8,128)(2,1)} custom-call(bf16[512,1152]{1,0:T(8,128)(2,1)} %convolution_convert_fusion.7.q_ref.k_ref.v_ref, bf16[512,1152]{1,0:T(8,128)(2,1)} %convolution_convert_fusion.7.q_ref.k_ref.v_ref, bf16[512,1152]{1,0:T(8,128)(2,1)} %convolution_convert_fusion.7.q_ref.k_ref.v_ref, s32[256,1]{1,0:T(8,128)} %copy.40.down_ref, ...), custom_call_target="tpu_custom_call" | custom-call | flops 201326592 | bytes 1572864 | tf_op jit(solution)/shard_map/mix1/attend/pallas_call | solution.py:610
  175.3 7.4 %collective-permute-done.35 = bf16[64,1536]{1,0:T(8,128)(2,1)S(1)} collective-permute-done((bf16[64,1536]{1,0:T(8,128)(2,1)S(1)}, bf16[64,1536]{1,0:T(8,128)(2,1)S(1)}, u32[]{:S(2)}, u32[]{:S(2)}) %collective-permute-start.35) | collective-permute-done | bytes 196640 | tf_op jit(solution)/shard_map/rows_c3/ppermute | solution.py:284
  203.2 10.7 %collective-permute-done.48 = bf16[384,1536]{1,0:T(8,128)(2,1)S(1)} collective-permute-done((bf16[384,1536]{1,0:T(8,128)(2,1)S(1)}, bf16[384,1536]{1,0:T(8,128)(2,1)S(1)}, u32[]{:S(2)}, u32[]{:S(2)}) %collective-permute-start.48) | collective-permute-done | bytes 1179680 | tf_op jit(solution)/shard_map/weights_mid/ppermute | solution.py:284
  235.4 4.1 attend.3
  250.2 25.1 %collective-permute-done.56 = bf16[384,768]{1,0:T(8,128)(2,1)S(1)} collective-permute-done((bf16[384,768]{1,0:T(8,128)(2,1)S(1)}, bf16[384,768]{1,0:T(8,128)(2,1)S(1)}, u32[]{:S(2)}, u32[]{:S(2)}) %collective-permute-start.56) | collective-permute-done | bytes 589856 | tf_op jit(solution)/shard_map/weights_down/ppermute | solution.py:284
  287.2 15.8 %collective-permute-done.65 = bf16[384,1536]{1,0:T(8,128)(2,1)S(1)} collective-permute-done((bf16[384,1536]{1,0:T(8,128)(2,1)S(1)}, bf16[384,1536]{1,0:T(8,128)(2,1)S(1)}, u32[]{:S(2)}, u32[]{:S(2)}) %collective-permute-start.65) | collective-permute-done | bytes 1179680 | tf_op jit(solution)/shard_map/weights_down/ppermute | solution.py:284
  307.4 3.6 collective-permute-done.63
  320.3 10.3 %add_convert_fusion = (bf16[512,1536]{1,0:T(8,128)(2,1)S(1)}, f32[512,1536]{1,0:T(8,128)S(1)}, f32[512,1536]{1,0:T(8,128)S(1)}) fusion(f32[512,1536]{1,0:T(8,128)S(1)} %fusion.83, bf16[512,1536]{1,0:T(8,128)(2,1)S(1)} %constant_dynamic-update-slice_fusion.62, bf16[1536,1536]{1,0:T(8,128)(2,1)S(1)} %constant_dynamic-update-slice_fusion.56), kind=kOutput, calls=%fused_computation.8 | convolution fusion | flops 2472542208 | bytes 17301504 | tf_op jit(solution)/shard_map/hidden/dot_general | solution.py:37
  363.7 4.1 collective-permute-done.78
  379.4 7.5 %attend_back.2 = (bf16[512,384]{1,0:T(8,128)(2,1)}, bf16[128,384]{1,0:T(8,128)(2,1)}, bf16[128,384]{1,0:T(8,128)(2,1)}) custom-call(bf16[512,384]{1,0:T(8,128)(2,1)} %convolution_convert_fusion.25.q_ref, bf16[128,768]{1,0:T(8,128)(2,1)} %convolution_convert_fusion.26.k_ref.v_ref, bf16[128,768]{1,0:T(8,128)(2,1)} %convolution_convert_fusion.26.k_ref.v_ref, ...), custom_call_target="tpu_custom_call" | custom-call | flops 125829120 | bytes 2752512 | tf_op jit(solution)/shard_map/mix2_back/attend_back/pallas_call | solution.py:633
  436.7 4.5 collective-permute-done.107
  452.0 9.7 %attend_back.3 = (bf16[512,384]{1,0:T(8,128)(2,1)}, bf16[512,384]{1,0:T(8,128)(2,1)}, bf16[512,384]{1,0:T(8,128)(2,1)}) custom-call(bf16[512,1152]{1,0:T(8,128)(2,1)} %convolution_convert_fusion.7.q_ref.k_ref.v_ref, bf16[512,1152]{1,0:T(8,128)(2,1)} %convolution_convert_fusion.7.q_ref.k_ref.v_ref, ...), custom_call_target="tpu_custom_call" | custom-call | flops 503316480 | bytes 2752512 | tf_op jit(solution)/shard_map/mix1_back/attend_back/pallas_call | solution.py:633
  463.9 4.2 convolution_convert_fusion.6
  479.7 5.0 collective-permute-done.109
  489.4 12.5 %collective-permute-done.115 = bf16[384,1536]{1,0:T(8,128)(2,1)S(1)} collective-permute-done((bf16[384,1536]{1,0:T(8,128)(2,1)S(1)}, bf16[384,1536]{1,0:T(8,128)(2,1)S(1)}, u32[]{:S(2)}, u32[]{:S(2)}) %collective-permute-start.115) | collective-permute-done | bytes 1179680 | tf_op jit(solution)/shard_map/grads_cross/ppermute | solution.py:284
  505.3 7.4 %collective-permute-done.114 = bf16[384,768]{1,0:T(8,128)(2,1)S(1)} collective-permute-done((bf16[384,768]{1,0:T(8,128)(2,1)S(1)}, bf16[384,768]{1,0:T(8,128)(2,1)S(1)}, u32[]{:S(2)}, u32[]{:S(2)}) %collective-permute-start.114) | collective-permute-done | bytes 589856 | tf_op jit(solution)/shard_map/grads_down/ppermute | solution.py:284
  555.9 5.9 collective-permute-done.124
  565.1 19.1 %collective-permute-done.126 = bf16[384,768]{1,0:T(8,128)(2,1)} collective-permute-done((bf16[384,768]{1,0:T(8,128)(2,1)}, bf16[384,768]{1,0:T(8,128)(2,1)}, u32[]{:S(2)}, u32[]{:S(2)}) %collective-permute-start.126) | collective-permute-done | bytes 589856 | tf_op jit(solution)/shard_map/grads_cross/ppermute | solution.py:284
  611.7 17.9 %collective-permute-done.125 = bf16[384,768]{1,0:T(8,128)(2,1)S(1)} collective-permute-done((bf16[384,768]{1,0:T(8,128)(2,1)S(1)}, bf16[384,768]{1,0:T(8,128)(2,1)S(1)}, u32[]{:S(2)}, u32[]{:S(2)}) %collective-permute-start.125) | collective-permute-done | bytes 589856 | tf_op jit(solution)/shard_map/grads_self/ppermute | solution.py:284
  631.2 6.4 collective-permute-done.135
  (768 shorter events, 391.6 us)
Async XLA Ops:
  23.8 34.9 %collective-permute-start.16 = (bf16[384,576]{1,0:T(8,128)(2,1)S(1)}, bf16[384,576]{1,0:T(8,128)(2,1)S(1)}, u32[]{:S(2)}, u32[]{:S(2)}) collective-permute-start(bf16[384,576]{1,0:T(8,128)(2,1)S(1)} %maximum_select_fusion.5), channel_id=1, source_target_pairs={{0,2},{1,3},{2,0},{3,1},{4,6},{5,7},{6,4},{7,5},{8,10},{9,11},{10,... | collective-permute-start | bytes 1327112 | tf_op jit(solution)/shard_map/weights_qkv/ppermute | solution.py:284
  119.5 29.3 %collective-permute-start.28 = (bf16[384,768]{1,0:T(8,128)(2,1)S(1)}, bf16[384,768]{1,0:T(8,128)(2,1)S(1)}, u32[]{:S(2)}, u32[]{:S(2)}) collective-permute-start(bf16[384,768]{1,0:T(8,128)(2,1)S(1)} %copy-done.13), channel_id=1, source_target_pairs={{0,2},{1,3},{2,0},{3,1},{4,6},{5,7},{6,4},{7,5},{8,10},{9,11},{10,... | collective-permute-start | bytes 1769480 | tf_op jit(solution)/shard_map/weights_mid/ppermute | solution.py:284
  120.1 42.9 %collective-permute-start.37 = (bf16[16,1536]{1,0:T(8,128)(2,1)}, bf16[16,1536]{1,0:T(8,128)(2,1)}, u32[]{:S(2)}, u32[]{:S(2)}) collective-permute-start(bf16[16,1536]{1,0:T(8,128)(2,1)} %get-tuple-element.429), channel_id=1, source_target_pairs={{0,1},{1,0},{2,3},{3,2},{4,5},{5,4},{6,7},{7,6},{8,9},{9,8},{10,11... | collective-permute-start | bytes 147464 | tf_op jit(solution)/shard_map/rows_text/ppermute | solution.py:284
  120.9 43.8 %collective-permute-start.38 = (bf16[16,1536]{1,0:T(8,128)(2,1)}, bf16[16,1536]{1,0:T(8,128)(2,1)}, u32[]{:S(2)}, u32[]{:S(2)}) collective-permute-start(bf16[16,1536]{1,0:T(8,128)(2,1)} %get-tuple-element.430), channel_id=1, source_target_pairs={{0,16},{1,17},{2,18},{3,19},{4,20},{5,21},{6,22},{7,23},{8,24},{9,... | collective-permute-start | bytes 147464 | tf_op jit(solution)/shard_map/rows_text/ppermute | solution.py:284
  121.7 51.9 %collective-permute-start.33 = (bf16[64,1536]{1,0:T(8,128)(2,1)}, bf16[64,1536]{1,0:T(8,128)(2,1)}, u32[]{:S(2)}, u32[]{:S(2)}) collective-permute-start(bf16[64,1536]{1,0:T(8,128)(2,1)} %get-tuple-element.437), channel_id=1, source_target_pairs={{0,1},{1,0},{2,3},{3,2},{4,5},{5,4},{6,7},{7,6},{8,9},{9,8},{10,11... | collective-permute-start | bytes 589832 | tf_op jit(solution)/shard_map/rows_c3/ppermute | solution.py:284
  129.2 35.5 %collective-permute-start.39 = (bf16[16,1536]{1,0:T(8,128)(2,1)}, bf16[16,1536]{1,0:T(8,128)(2,1)}, u32[]{:S(2)}, u32[]{:S(2)}) collective-permute-start(bf16[16,1536]{1,0:T(8,128)(2,1)} %collective-permute-done.23), channel_id=1, source_target_pairs={{0,1},{1,0},{2,3},{3,2},{4,5},{5,4},{6,7},{7,6},{8,9},{9,8},{10,11... | collective-permute-start | bytes 147464 | tf_op jit(solution)/shard_map/rows_text/ppermute | solution.py:284
  164.7 30.3 %collective-permute-start.44 = (bf16[384,768]{1,0:T(8,128)(2,1)S(1)}, bf16[384,768]{1,0:T(8,128)(2,1)S(1)}, u32[]{:S(2)}, u32[]{:S(2)}) collective-permute-start(bf16[384,768]{1,0:T(8,128)(2,1)S(1)} %copy-done.22), channel_id=1, source_target_pairs={{0,2},{1,3},{2,0},{3,1},{4,6},{5,7},{6,4},{7,5},{8,10},{9,11},{10,... | collective-permute-start | bytes 1769480 | tf_op jit(solution)/shard_map/weights_up/ppermute | solution.py:284
  215.1 28.1 %collective-permute-start.57 = (bf16[384,1536]{1,0:T(8,128)(2,1)}, bf16[384,1536]{1,0:T(8,128)(2,1)}, u32[]{:S(2)}, u32[]{:S(2)}) collective-permute-start(bf16[384,1536]{1,0:T(8,128)(2,1)} %constant_dynamic-update-slice_fusion.38), channel_id=1, source_target_pairs={{0,8},{1,9},{2,10},{3,11},{4,12},{5,13},{6,14},{7,15},{8,0},{9,1},... | collective-permute-start | bytes 3538952 | tf_op jit(solution)/shard_map/weights_up/ppermute | solution.py:284
  245.9 32.6 %collective-permute-start.61 = (bf16[768,1536]{1,0:T(8,128)(2,1)S(1)}, bf16[768,1536]{1,0:T(8,128)(2,1)S(1)}, u32[]{:S(2)}, u32[]{:S(2)}) collective-permute-start(bf16[768,1536]{1,0:T(8,128)(2,1)S(1)} %constant_dynamic-update-slice_fusion.52), channel_id=1, source_target_pairs={{0,4},{1,5},{2,6},{3,7},{4,0},{5,1},{6,2},{7,3},{8,12},{9,13},{10,... | collective-permute-start | bytes 7077896 | tf_op jit(solution)/shard_map/weights_up/ppermute | solution.py:284
  246.0 29.3 %collective-permute-start.56 = (bf16[384,768]{1,0:T(8,128)(2,1)S(1)}, bf16[384,768]{1,0:T(8,128)(2,1)S(1)}, u32[]{:S(2)}, u32[]{:S(2)}) collective-permute-start(bf16[384,768]{1,0:T(8,128)(2,1)S(1)} %copy-done.20), channel_id=1, source_target_pairs={{0,2},{1,3},{2,0},{3,1},{4,6},{5,7},{6,4},{7,5},{8,10},{9,11},{10,... | collective-permute-start | bytes 1769480 | tf_op jit(solution)/shard_map/weights_down/ppermute | solution.py:284
  249.3 27.7 %collective-permute-start.55 = (bf16[64,1536]{1,0:T(8,128)(2,1)S(1)}, bf16[64,1536]{1,0:T(8,128)(2,1)S(1)}, u32[]{:S(2)}, u32[]{:S(2)}) collective-permute-start(bf16[64,1536]{1,0:T(8,128)(2,1)S(1)} %get-tuple-element.790), channel_id=1, source_target_pairs={{0,1},{1,0},{2,3},{3,2},{4,5},{5,4},{6,7},{7,6},{8,9},{9,8},{10,11... | collective-permute-start | bytes 589832 | tf_op jit(solution)/shard_map/sums_x2/ppermute | solution.py:284
  249.6 31.4 %collective-permute-start.53 = (bf16[64,1536]{1,0:T(8,128)(2,1)S(1)}, bf16[64,1536]{1,0:T(8,128)(2,1)S(1)}, u32[]{:S(2)}, u32[]{:S(2)}) collective-permute-start(bf16[64,1536]{1,0:T(8,128)(2,1)S(1)} %get-tuple-element.794), channel_id=1, source_target_pairs={{0,16},{1,17},{2,18},{3,19},{4,20},{5,21},{6,22},{7,23},{8,24},{9,... | collective-permute-start | bytes 589832 | tf_op jit(solution)/shard_map/sums_x2/ppermute | solution.py:284
  275.4 27.6 %collective-permute-start.65 = (bf16[384,1536]{1,0:T(8,128)(2,1)S(1)}, bf16[384,1536]{1,0:T(8,128)(2,1)S(1)}, u32[]{:S(2)}, u32[]{:S(2)}) collective-permute-start(bf16[384,1536]{1,0:T(8,128)(2,1)S(1)} %constant_dynamic-update-slice_fusion.54), channel_id=1, source_target_pairs={{0,8},{1,9},{2,10},{3,11},{4,12},{5,13},{6,14},{7,15},{8,0},{9,1},... | collective-permute-start | bytes 3538952 | tf_op jit(solution)/shard_map/weights_down/ppermute | solution.py:284
  360.0 29.1 %collective-permute-start.83 = (bf16[384,1536]{1,0:T(8,128)(2,1)}, bf16[384,1536]{1,0:T(8,128)(2,1)}, u32[]{:S(2)}, u32[]{:S(2)}) collective-permute-start(bf16[384,1536]{1,0:T(8,128)(2,1)} %get-tuple-element.740), channel_id=1, source_target_pairs={{0,8},{1,9},{2,10},{3,11},{4,12},{5,13},{6,14},{7,15},{8,0},{9,1},... | collective-permute-start | bytes 3538952 | tf_op jit(solution)/shard_map/grads_up/ppermute | solution.py:284
  473.3 53.6 %collective-permute-start.80 = (bf16[64,1536]{1,0:T(8,128)(2,1)}, bf16[64,1536]{1,0:T(8,128)(2,1)}, u32[]{:S(2)}, u32[]{:S(2)}) collective-permute-start(bf16[64,1536]{1,0:T(8,128)(2,1)} %get-tuple-element.778), channel_id=1, source_target_pairs={{0,16},{1,17},{2,18},{3,19},{4,20},{5,21},{6,22},{7,23},{8,24},{9,... | collective-permute-start | bytes 589832 | tf_op jit(solution)/shard_map/sums_act/ppermute | solution.py:284
  474.1 27.7 %collective-permute-start.115 = (bf16[384,1536]{1,0:T(8,128)(2,1)S(1)}, bf16[384,1536]{1,0:T(8,128)(2,1)S(1)}, u32[]{:S(2)}, u32[]{:S(2)}) collective-permute-start(bf16[384,1536]{1,0:T(8,128)(2,1)S(1)} %copy-done.25), channel_id=1, source_target_pairs={{0,8},{1,9},{2,10},{3,11},{4,12},{5,13},{6,14},{7,15},{8,0},{9,1},... | collective-permute-start | bytes 3538952 | tf_op jit(solution)/shard_map/grads_cross/ppermute | solution.py:284
  484.6 28.1 %collective-permute-start.114 = (bf16[384,768]{1,0:T(8,128)(2,1)S(1)}, bf16[384,768]{1,0:T(8,128)(2,1)S(1)}, u32[]{:S(2)}, u32[]{:S(2)}) collective-permute-start(bf16[384,768]{1,0:T(8,128)(2,1)S(1)} %copy-done.41), channel_id=1, source_target_pairs={{0,2},{1,3},{2,0},{3,1},{4,6},{5,7},{6,4},{7,5},{8,10},{9,11},{10,... | collective-permute-start | bytes 1769480 | tf_op jit(solution)/shard_map/grads_down/ppermute | solution.py:284
  485.5 29.0 %collective-permute-start.108 = (bf16[64,1536]{1,0:T(8,128)(2,1)S(1)}, bf16[64,1536]{1,0:T(8,128)(2,1)S(1)}, u32[]{:S(2)}, u32[]{:S(2)}) collective-permute-start(bf16[64,1536]{1,0:T(8,128)(2,1)S(1)} %get-tuple-element.762), channel_id=1, source_target_pairs={{0,16},{1,17},{2,18},{3,19},{4,20},{5,21},{6,22},{7,23},{8,24},{9,... | collective-permute-start | bytes 589832 | tf_op jit(solution)/shard_map/sums_h1/ppermute | solution.py:284
  486.3 30.3 %collective-permute-start.112 = (bf16[64,1536]{1,0:T(8,128)(2,1)S(1)}, bf16[64,1536]{1,0:T(8,128)(2,1)S(1)}, u32[]{:S(2)}, u32[]{:S(2)}) collective-permute-start(bf16[64,1536]{1,0:T(8,128)(2,1)S(1)} %get-tuple-element.756), channel_id=1, source_target_pairs={{0,1},{1,0},{2,3},{3,2},{4,5},{5,4},{6,7},{7,6},{8,9},{9,8},{10,11... | collective-permute-start | bytes 589832 | tf_op jit(solution)/shard_map/sums_h1/ppermute | solution.py:284
  530.1 74.9 %collective-permute-start.129 = (bf16[192,768]{1,0:T(8,128)(2,1)}, bf16[192,768]{1,0:T(8,128)(2,1)}, u32[]{:S(2)}, u32[]{:S(2)}) collective-permute-start(bf16[192,768]{1,0:T(8,128)(2,1)} %select_convert_fusion.3), channel_id=1, source_target_pairs={{0,16},{1,17},{2,18},{3,19},{4,20},{5,21},{6,22},{7,23},{8,24},{9,... | collective-permute-start | bytes 884744 | tf_op jit(solution)/shard_map/grads_up/ppermute | solution.py:284
  548.9 35.3 %collective-permute-start.126 = (bf16[384,768]{1,0:T(8,128)(2,1)}, bf16[384,768]{1,0:T(8,128)(2,1)}, u32[]{:S(2)}, u32[]{:S(2)}) collective-permute-start(bf16[384,768]{1,0:T(8,128)(2,1)} %pad_maximum_fusion.10), channel_id=1, source_target_pairs={{0,2},{1,3},{2,0},{3,1},{4,6},{5,7},{6,4},{7,5},{8,10},{9,11},{10,... | collective-permute-start | bytes 1769480 | tf_op jit(solution)/shard_map/grads_cross/ppermute | solution.py:284
  551.8 55.3 %collective-permute-start.128 = (bf16[192,768]{1,0:T(8,128)(2,1)}, bf16[192,768]{1,0:T(8,128)(2,1)}, u32[]{:S(2)}, u32[]{:S(2)}) collective-permute-start(bf16[192,768]{1,0:T(8,128)(2,1)} %select_convert_fusion.2), channel_id=1, source_target_pairs={{0,16},{1,17},{2,18},{3,19},{4,20},{5,21},{6,22},{7,23},{8,24},{9,... | collective-permute-start | bytes 884744 | tf_op jit(solution)/shard_map/grads_down/ppermute | solution.py:284
  554.4 37.1 %collective-permute-start.118 = (bf16[64,1536]{1,0:T(8,128)(2,1)}, bf16[64,1536]{1,0:T(8,128)(2,1)S(1)}, u32[]{:S(2)}, u32[]{:S(2)}) collective-permute-start(bf16[64,1536]{1,0:T(8,128)(2,1)} %slice.2129), channel_id=1, source_target_pairs={{0,2},{1,3},{2,0},{3,1},{4,6},{5,7},{6,4},{7,5},{8,10},{9,11},{10,... | collective-permute-start | bytes 589832 | tf_op jit(solution)/shard_map/ppermute | solution.py:284
  561.8 32.1 %collective-permute-start.117 = (bf16[64,1536]{1,0:T(8,128)(2,1)}, bf16[64,1536]{1,0:T(8,128)(2,1)S(1)}, u32[]{:S(2)}, u32[]{:S(2)}) collective-permute-start(bf16[64,1536]{1,0:T(8,128)(2,1)} %slice.1327), channel_id=1, source_target_pairs={{0,2},{1,3},{2,0},{3,1},{4,6},{5,7},{6,4},{7,5},{8,10},{9,11},{10,... | collective-permute-start | bytes 589832 | tf_op jit(solution)/shard_map/ppermute | solution.py:284
  (201 other events, 1713.7 us)

commit v3 on v1

--- a/solution.py
+++ b/solution.py
@@ -1,7 +1,12 @@
+import functools
+import math
+
 import jax
 import jax.numpy as jnp
 from jax import lax
-from jax.sharding import PartitionSpec as P
+from jax.experimental import pallas as pl
+from jax.experimental.pallas import tpu as pltpu
+from jax.sharding import Mesh, PartitionSpec as P
 
 HEAD_DIM = 64
 EPS = 1e-05
@@ -274,15 +279,1003 @@
     )
 
 
+def exchange(value, axis):
+    return lax.ppermute(value, axis, [(0, 1), (1, 0)])
+
+
+def bit(axis):
+    return lax.axis_index(axis) == 1
+
+
+def ordered(flag, own, other, axis):
+    return jnp.where(
+        flag,
+        jnp.concatenate([other, own], axis=axis),
+        jnp.concatenate([own, other], axis=axis),
+    )
+
+
+def regroup(value, outer):
+    width, inner = value.shape[-1] // 8, 8 // outer
+    parts = [value[..., i * width : (i + 1) * width] for i in range(8)]
+    order = [parts[o * inner + i] for i in range(inner) for o in range(outer)]
+    return jnp.concatenate(order, axis=-1)
+
+
+def halves(v):
+    half = v.shape[0] // 2
+    return v[:half], v[half:]
+
+
+def join(parts, axis):
+    return parts[0] if len(parts) == 1 else jnp.concatenate(parts, axis=axis)
+
+
+VMEM_BYTES = 40 << 20
+
+
+def whole_block(shape):
+    return pl.BlockSpec(shape, lambda *i: (0,) * len(shape), pipeline_mode=pl.Buffered(1))
+
+
+def settings():
+    return dict(
+        cost_estimate=pl.CostEstimate(flops=1, bytes_accessed=1, transcendentals=0),
+        compiler_params=pltpu.CompilerParams(vmem_limit_bytes=VMEM_BYTES),
+    )
+
+
+def fill(pieces, whole_ref):
+    start = 0
+    for piece in pieces:
+        whole_ref[start : start + piece.shape[0], :] = piece[...]
+        start += piece.shape[0]
+
+
+def rows_product(pieces, weights, first, count, tile):
+    depth = weights.shape[0]
+    rows = sum(p.shape[0] for p in pieces)
+
+    def body(*refs):
+        w_ref, whole_ref, out_ref = refs[len(pieces) :]
+
+        @pl.when(pl.program_id(0) == 0)
+        def _():
+            fill(refs[: len(pieces)], whole_ref)
+
+        out_ref[...] = jnp.dot(
+            whole_ref[...], w_ref[...], preferred_element_type=WIDE
+        ).astype(LOW)
+
+    return pl.pallas_call(
+        body,
+        grid=(count // tile,),
+        in_specs=[whole_block(p.shape) for p in pieces]
+        + [pl.BlockSpec((depth, tile), lambda j: (0, first + j))],
+        out_specs=[
+            pl.BlockSpec((rows, depth), lambda j: (0, 0)),
+            pl.BlockSpec((rows, tile), lambda j: (0, j)),
+        ],
+        out_shape=[
+            jax.ShapeDtypeStruct((rows, depth), LOW),
+            jax.ShapeDtypeStruct((rows, count), LOW),
+        ],
+        name="rows_product",
+        **settings(),
+    )(*pieces, weights)
+
+
+def middle_kernel(*refs):
+    pieces, (up_ref, down_ref, grad_ref, whole_ref, active_ref, low_ref) = refs[:7], refs[7:]
+
+    @pl.when(pl.program_id(0) == 0)
+    def _():
+        fill(line_pieces([piece[...] for piece in pieces]), whole_ref)
+
+    hidden = jnp.dot(whole_ref[...], up_ref[...], preferred_element_type=WIDE)
+    upstream = jnp.dot(grad_ref[...], down_ref[...], preferred_element_type=WIDE)
+    share = 0.5 + 0.5 * lax.erf(hidden * 0.5**0.5)
+    density = jnp.exp(-0.5 * hidden * hidden) * (2.0 * math.pi) ** -0.5
+    active_ref[...] = (hidden * share).astype(LOW)
+    low_ref[...] = (upstream * (share + hidden * density)).astype(LOW)
+
+
+def middle(pieces, weights, grad, tile):
+    depth, count = weights.shape[0], weights.shape[1] // 2
+    rows = grad.shape[0]
+    tiles = count // tile
+    out = pl.BlockSpec((rows, tile), lambda j: (0, j))
+    return pl.pallas_call(
+        middle_kernel,
+        grid=(tiles,),
+        in_specs=[whole_block(p.shape) for p in pieces]
+        + [
+            pl.BlockSpec((depth, tile), lambda j: (0, j)),
+            pl.BlockSpec((depth, tile), lambda j: (0, tiles + j)),
+            whole_block(grad.shape),
+        ],
+        out_specs=[pl.BlockSpec((rows, depth), lambda j: (0, 0)), out, out],
+        out_shape=[jax.ShapeDtypeStruct((rows, n), LOW) for n in (depth, count, count)],
+        name="middle",
+        **settings(),
+    )(*pieces, weights, weights, grad)
+
+
+def pieces_product(terms, tile, cuts=(2, 2, 2, 1, 1)):
+    rows, depth = terms[0][0].shape[0], terms[0][1].shape[0]
+    unit = rows // sum(cuts)
+
+    def body(*refs):
+        total = None
+        for i in range(len(terms)):
+            term = lax.dot_general(
+                refs[2 * i][...],
+                refs[2 * i + 1][...],
+                (((1,), (1,)), ((), ())),
+                preferred_element_type=WIDE,
+            )
+            total = term if total is None else total + term
+        fill_from = 0
+        for ref in refs[2 * len(terms) :]:
+            ref[...] = total[fill_from : fill_from + ref.shape[0]].astype(LOW)
+            fill_from += ref.shape[0]
+
+    specs, operands = [], []
+    for x, w, block in terms:
+        specs.append(whole_block(x.shape))
+        specs.append(pl.BlockSpec((tile, x.shape[1]), lambda i, block=block: (i, block)))
+        operands += [x, w]
+    sizes = [unit * cut for cut in cuts]
+    return pl.pallas_call(
+        body,
+        grid=(depth // tile,),
+        in_specs=specs,
+        out_specs=[pl.BlockSpec((n, tile), lambda i: (0, i)) for n in sizes],
+        out_shape=[jax.ShapeDtypeStruct((n, depth), LOW) for n in sizes],
+        name="pieces_product",
+        **settings(),
+    )(*operands)
+
+
+def gradient_product(pairs, tile):
+    depth = pairs[0][0].shape[1]
+    tiles = [u.shape[1] // tile for _, u in pairs]
+    starts = [sum(tiles[:i]) for i in range(len(tiles))]
+
+    def body(*refs):
+        out_ref, j = refs[-1], pl.program_id(0)
+        for i in range(len(pairs)):
+
+            @pl.when((j >= starts[i]) & (j < starts[i] + tiles[i]))
+            def _(i=i):
+                out_ref[...] = product_left(refs[2 * i][...], refs[2 * i + 1][...]).astype(LOW)
+
+    specs, operands = [], []
+    for (a, u), start, count in zip(pairs, starts, tiles):
+        specs.append(whole_block(a.shape))
+        specs.append(
+            pl.BlockSpec(
+                (u.shape[0], tile),
+                lambda j, start=start, count=count: (0, jnp.clip(j - start, 0, count - 1)),
+            )
+        )
+        operands += [a, u]
+    return pl.pallas_call(
+        body,
+        grid=(sum(tiles),),
+        in_specs=specs,
+        out_specs=pl.BlockSpec((depth, tile), lambda j: (0, j)),
+        out_shape=jax.ShapeDtypeStruct((depth, tile * sum(tiles)), LOW),
+        name="gradient_product",
+        **settings(),
+    )(*operands)
+
+
+def relay_kernel(near_ref, row_ref, one_ref, two_ref, near_out, row_out):
+    half = one_ref.shape[0]
+    near_out[:half] = (near_ref[:half].astype(WIDE) + one_ref[...].astype(WIDE)).astype(LOW)
+    near_out[half:] = near_ref[half:]
+    row_out[:half] = row_ref[:half]
+    row_out[half:] = (row_ref[half:].astype(WIDE) + two_ref[...].astype(WIDE)).astype(LOW)
+
+
+def relay_sums(near, row, one, two):
+    return pl.pallas_call(
+        relay_kernel,
+        out_shape=[jax.ShapeDtypeStruct(near.shape, LOW)] * 2,
+        name="relay_sums",
+        **settings(),
+    )(near, row, one, two)
+
+
+def open_kernel(own_ref, near_ref, row_ref, x_ref, gain_ref, shift_ref, x_out, a_out):
+    total = own_ref[...].astype(WIDE) + near_ref[...].astype(WIDE) + row_ref[...].astype(WIDE)
+    x = x_ref[...] + total
+    x_out[...] = x
+    a_out[...] = norm_forward(x, gain_ref[...], shift_ref[...])[0].astype(LOW)
+
+
+def open_norm(own, near, row, x, gain, shift):
+    return pl.pallas_call(
+        open_kernel,
+        out_shape=[jax.ShapeDtypeStruct(x.shape, WIDE), jax.ShapeDtypeStruct(x.shape, LOW)],
+        name="open_norm",
+        **settings(),
+    )(own, near, row, x, gain, shift)
+
+
+def close_kernel(own_ref, near_ref, row_ref, x_ref, gain_ref, e_ref, e_out, c_out, sums_out):
+    total = own_ref[...].astype(WIDE) + near_ref[...].astype(WIDE) + row_ref[...].astype(WIDE)
+    _, unit, inverse = norm_forward(x_ref[...], gain_ref[...], 0.0)
+    change, gain_grad, shift_grad = norm_back(unit, inverse, gain_ref[...], total)
+    e = e_ref[...].astype(WIDE) + change
+    e_out[...] = e
+    c_out[...] = e.astype(LOW)
+    sums_out[...] = jnp.concatenate([gain_grad[None], shift_grad[None]], axis=0)
+
+
+def close_norm(own, near, row, x, gain, e):
+    return pl.pallas_call(
+        close_kernel,
+        out_shape=[
+            jax.ShapeDtypeStruct(x.shape, WIDE),
+            jax.ShapeDtypeStruct(x.shape, LOW),
+            jax.ShapeDtypeStruct((2, x.shape[1]), WIDE),
+        ],
+        name="close_norm",
+        **settings(),
+    )(own, near, row, x, gain, e)
+
+
+def plain_total(a, b, c):
+    return a.astype(WIDE) + b.astype(WIDE) + c.astype(WIDE)
+
+
+def head_weights(queries, keys, mask):
+    scores = lax.dot_general(queries, keys, (((1,), (1,)), ((), ())), preferred_element_type=WIDE)
+    scores = scores * HEAD_DIM**-0.5
+    if mask is not None:
+        scores = jnp.where(mask, scores, -1e30)
+    raw = jnp.exp(scores - jnp.max(scores, axis=-1, keepdims=True))
+    return raw * (1.0 / jnp.sum(raw, axis=-1, keepdims=True))
+
+
+def attend_kernel(heads, causal, q_ref, k_ref, v_ref, down_ref, along_ref, out_ref):
+    mask = down_ref[...] >= along_ref[...] if causal else None
+    for head in range(heads):
+        columns = slice(head * HEAD_DIM, (head + 1) * HEAD_DIM)
+        chance = head_weights(q_ref[:, columns], k_ref[:, columns], mask)
+        mixed = jnp.dot(chance.astype(LOW), v_ref[:, columns], preferred_element_type=WIDE)
+        out_ref[:, columns] = mixed.astype(LOW)
+
+
+def attend_back_kernel(
+    heads, causal, q_ref, k_ref, v_ref, up_ref, down_ref, along_ref, dq_ref, dk_ref, dv_ref
+):
+    mask = down_ref[...] >= along_ref[...] if causal else None
+    scaling = HEAD_DIM**-0.5
+    for head in range(heads):
+        columns = slice(head * HEAD_DIM, (head + 1) * HEAD_DIM)
+        queries, keys, upstream = q_ref[:, columns], k_ref[:, columns], up_ref[:, columns]
+        chance = head_weights(queries, keys, mask)
+        grad = lax.dot_general(
+            upstream, v_ref[:, columns], (((1,), (1,)), ((), ())), preferred_element_type=WIDE
+        )
+        dots = jnp.sum(chance * grad, axis=-1, keepdims=True)
+        score_grad = (chance * (grad - dots)).astype(LOW)
+        dq_ref[:, columns] = (
+            jnp.dot(score_grad, keys, preferred_element_type=WIDE) * scaling
+        ).astype(LOW)
+        dk_ref[:, columns] = (product_left(score_grad, queries) * scaling).astype(LOW)
+        dv_ref[:, columns] = product_left(chance.astype(LOW), upstream).astype(LOW)
+
+
+def column_block(rows, width, index):
+    return pl.BlockSpec((rows, width), lambda s: (s, index))
+
+
+def attention(queries, keys, values, places, causal):
+    width = places[2]
+    rows, key_rows = queries[0].shape[0] // 2, keys[0].shape[0] // 2
+    heads = width // HEAD_DIM
+    return pl.pallas_call(
+        functools.partial(attend_kernel, heads, causal),
+        grid=(2,),
+        in_specs=[
+            column_block(rows, width, queries[1]),
+            column_block(key_rows, width, keys[1]),
+            column_block(key_rows, width, values[1]),
+            pl.BlockSpec(places[0].shape, lambda s: (0, 0)),
+            pl.BlockSpec(places[1].shape, lambda s: (0, 0)),
+        ],
+        out_specs=column_block(rows, width, 0),
+        out_shape=jax.ShapeDtypeStruct((2 * rows, width), LOW),
+        **settings(),
+        name="attend",
+    )(queries[0], keys[0], values[0], places[0], places[1])
+
+
+def attention_back(queries, keys, values, upstream, places, causal):
+    width = places[2]
+    rows, key_rows = queries[0].shape[0] // 2, keys[0].shape[0] // 2
+    heads = width // HEAD_DIM
+    return pl.pallas_call(
+        functools.partial(attend_back_kernel, heads, causal),
+        grid=(2,),
+        in_specs=[
+            column_block(rows, width, queries[1]),
+            column_block(key_rows, width, keys[1]),
+            column_block(key_rows, width, values[1]),
+            column_block(rows, width, 0),
+            pl.BlockSpec(places[0].shape, lambda s: (0, 0)),
+            pl.BlockSpec(places[1].shape, lambda s: (0, 0)),
+        ],
+        out_specs=[
+            column_block(rows, width, 0),
+            column_block(key_rows, width, 0),
+            column_block(key_rows, width, 0),
+        ],
+        out_shape=[
+            jax.ShapeDtypeStruct((2 * rows, width), LOW),
+            jax.ShapeDtypeStruct((2 * key_rows, width), LOW),
+            jax.ShapeDtypeStruct((2 * key_rows, width), LOW),
+        ],
+        **settings(),
+        name="attend_back",
+    )(queries[0], keys[0], values[0], upstream, places[0], places[1])
+
+
+def line_pieces(pieces):
+    local, d1, u3, d2, u2, u1, d3 = pieces
+    return local, d1 + u3, d2 + u2, u1 + d3
+
+
+class Name:
+    def __getattr__(self, key):
+        return self.__dict__.setdefault(key, Name())
+
+
+def swapping(axis):
+    return lambda v: exchange(v, axis)
+
+
+def stepping(*perm):
+    return lambda v: lax.ppermute(v, ("far", "near"), perm)
+
+
+to_row, to_column, to_core = swapping("row"), swapping("column"), swapping("core")
+to_far, to_near = swapping("far"), swapping("near")
+up_all, up_last2, up_last = stepping((0, 1), (1, 2), (2, 3)), stepping((1, 2), (2, 3)), stepping((2, 3))
+up_first, up_first2 = stepping((0, 1)), stepping((0, 1), (1, 2))
+down_all, down_last2, down_last = (
+    stepping((3, 2), (2, 1), (1, 0)),
+    stepping((2, 1), (1, 0)),
+    stepping((1, 0)),
+)
+down_first, down_first2 = stepping((3, 2)), stepping((3, 2), (2, 1))
+
+
+def to_all(v):
+    return lax.all_gather(v, ("column", "core"), axis=0, tiled=True)
+
+
+def to_sum(v):
+    return lax.psum_scatter(v, ("column", "core"), scatter_dimension=0, tiled=True)
+
+
+def run_steps(values, order):
+    last = None
+    for needs, gives, work, *sends in order:
+        taken = [values[n] for n in needs]
+        if last is not None:
+            taken, _ = lax.optimization_barrier((taken, last))
+        last = work(*taken)
+        values.update(zip(gives, last, strict=True))
+        for result, source, move in sends:
+            values[result] = move(values[source])
+    return values
+
+
+def keep(*values):
+    return values
+
+
+def row_sends(local):
+    return (local.row, local, to_row), (local.near, local, to_near)
+
+
+def rows_steps(local, work, needs, gives):
+    def relay(row, near):
+        return halves(row)[0], halves(near)[1]
+
+    return (
+        (
+            (local.row, local.near),
+            (local.p, local.q),
+            relay,
+            (local.one, local.p, to_near),
+            (local.two, local.q, to_row),
+        ),
+        ((local.one, local.two), (local.three, local.four), keep),
+        (
+            (local, local.near, local.row, local.three, local.four, *needs),
+            gives,
+            lambda *v: work(v[:5], *v[5:]),
+        ),
+    )
+
+
+def line_sends(local):
+    return (local.u1, local, up_all), (local.d1, local, down_all)
+
+
+def line_rows_steps(local, work, needs, gives):
+    c = local
+    return (
+        ((c.u1, c.d1), (c.v1, c.w1), keep, (c.u2, c.v1, up_last2), (c.d2, c.w1, down_last2)),
+        ((c.u2, c.d2), (c.v2, c.w2), keep, (c.u3, c.v2, up_last), (c.d3, c.w2, down_last)),
+        ((c.u3, c.d3), (c.v3, c.w3), keep),
+        (
+            (c, c.w1, c.v3, c.w2, c.v2, c.v1, c.w3, *needs),
+            gives,
+            lambda *u: work(u[:7], *u[7:]),
+        ),
+    )
+
+
+def line_sums_steps(terms, weights, blocks, work, needs, gives, *sends):
+    count, c = len(terms), Name()
+
+    def start(*v):
+        return pieces_product(list(zip(v[:count], v[count:], blocks)), 384, (1, 1, 1, 1))
+
+    def add(a, b, c, d):
+        return (
+            (a.astype(WIDE) + b.astype(WIDE)).astype(LOW),
+            (c.astype(WIDE) + d.astype(WIDE)).astype(LOW),
+        )
+
+    return (
+        ((*terms, *weights), (c.q0, c.q1, c.q2, c.q3), start),
+        (
+            (c.q0, c.q1, c.q2, c.q3),
+            (c.p0, c.p1, c.p2, c.p3),
+            keep,
+            (c.d3, c.p1, down_first),
+            (c.u3, c.p3, up_first),
+        ),
+        (
+            (c.p2, c.d3, c.p2, c.u3),
+            (c.a2, c.b2),
+            add,
+            (c.d2, c.a2, down_first2),
+            (c.u2, c.b2, up_first2),
+        ),
+        (
+            (c.p3, c.d2, c.p1, c.u2),
+            (c.a1, c.b1),
+            add,
+            (c.d1, c.a1, down_all),
+            (c.u1, c.b1, up_all),
+        ),
+        ((c.p0, c.d1, c.u1, *needs), gives, work, *sends),
+    )
+
+
+def sums_steps(terms, weights, blocks, work, needs, gives, *sends):
+    count, c = len(terms), Name()
+
+    def start(*v):
+        return pieces_product(list(zip(v[:count], v[count:], blocks)), 384)
+
+    return (
+        (
+            (*terms, *weights),
+            (c.own, c.n, c.r, c.one, c.two),
+            start,
+            (c.a, c.one, to_row),
+            (c.b, c.two, to_near),
+        ),
+        (
+            (c.n, c.r, c.a, c.b),
+            (c.c, c.d),
+            relay_sums,
+            (c.x, c.c, to_near),
+            (c.y, c.d, to_row),
+        ),
+        ((c.own, c.x, c.y, *needs), gives, work, *sends),
+    )
+
+
+def weights_steps(parts, cuts, full):
+    c = Name()
+
+    def split(*shards):
+        row = bit("row")
+        lows = join([p[:, :w] for p, w in zip(shards, cuts)], 1)
+        highs = join([p[:, w:] for p, w in zip(shards, cuts)], 1)
+        return jnp.where(row, highs, lows), jnp.where(row, lows, highs)
+
+    def stack(own, got):
+        return (ordered(bit("row"), own, got, 0),)
+
+    def side_by_side(own, other):
+        pieces, start = [], 0
+        for w in cuts:
+            pieces += [own[:, start : start + w], other[:, start : start + w]]
+            start += w
+        return (jnp.concatenate(pieces, axis=1),)
+
+    return (
+        (parts, (c.a, c.b), split, (c.c, c.b, to_row)),
+        ((c.a, c.c), (c.d,), stack, (c.e, c.d, to_far)),
+        ((c.d, c.e), (c.f,), side_by_side, (full, c.f, to_all)),
+    )
+
+
+def gradients_steps(pairs, cuts, gives):
+    n = Name()
+
+    def make(*v):
+        return (gradient_product(list(zip(v[::2], v[1::2])), 384),)
+
+    def cut_far(total):
+        stay, leave, start = [], [], 0
+        for c in cuts:
+            stay.append(total[:, start : start + c])
+            leave.append(total[:, start + c : start + 2 * c])
+            start += 2 * c
+        return join(stay, 1), join(leave, 1)
+
+    def cut_row(own, got):
+        total, row = own.astype(WIDE) + got.astype(WIDE), bit("row")
+        first, second = halves(total)
+        return jnp.where(row, second, first), jnp.where(row, first, second).astype(LOW)
+
+    def place(own, got):
+        got, row = got.astype(WIDE), bit("row")
+        found, start = [], 0
+        for c in cuts:
+            found.append(ordered(row, own[:, start : start + c], got[:, start : start + c], 1))
+            start += c
+        return found
+
+    return (
+        (pairs, (n.a,), make, (n.b, n.a, to_sum)),
+        ((n.b,), (n.c, n.d), cut_far, (n.e, n.d, to_far)),
+        ((n.c, n.e), (n.f, n.g), cut_row, (n.h, n.g, to_row)),
+        ((n.f, n.h), gives, place),
+    )
+
+
+def plan_pairs(n, inner, units, own_frames, own_text):
+    s, far_bit = Name(), bit("far")
+
+    def divide(v):
+        return jnp.where(far_bit, v[1], v[0]), jnp.where(far_bit, v[0], v[1])
+
+    half, wide = inner // 2, units // 2
+    s.frames = ((n.frames,), (n.keep_f, n.give_f), divide, (n.got_f, n.give_f, to_far))
+    s.frames_in = ((n.got_f,), (n.got_f2,), keep)
+    s.w_self, s.w_self_far, s.w_self_all = weights_steps(
+        (n.self_q, n.self_k, n.self_v, n.self_out), [half] * 4, n.full_self
+    )
+    s.w_cross, s.w_cross_far, s.w_cross_all = weights_steps(
+        (n.cross_q, n.cross_k, n.cross_v, n.cross_out), [half] * 4, n.full_cross
+    )
+    s.w_mlp = (
+        (n.mlp_up, n.mlp_down),
+        (n.own_mlp,),
+        lambda a, b: (jnp.concatenate([a, b], axis=1),),
+        (n.got_mlp, n.own_mlp, to_row),
+    )
+    s.w_mlp_all = (
+        (n.own_mlp, n.got_mlp),
+        (n.both_mlp,),
+        lambda a, b: (ordered(bit("row"), a, b, 0),),
+    )
+    s.w_mlp_go = ((n.both_mlp,), (n.both_mlp2,), keep, (n.full_mlp, n.both_mlp2, to_all))
+
+    axes, moves = ("near", "far", "core", "column", "row"), (to_near, to_far, to_core, to_column, to_row)
+
+    def widen(axis):
+        return lambda o, g: (ordered(bit(axis), o, g, 1),)
+
+    s.n0 = (
+        (n.norm_gains, n.norm_shifts),
+        (n.v0,),
+        lambda a, b: (jnp.concatenate([a, b], axis=0),),
+        (n.g0, n.v0, moves[0]),
+    )
+    s.n1 = ((n.v0, n.g0), (n.v1,), widen(axes[0]), (n.g1, n.v1, moves[1]))
+    s.n2 = ((n.v1, n.g1), (n.v2,), widen(axes[1]), (n.g2, n.v2, moves[2]))
+    s.n3 = ((n.v2, n.g2), (n.v3,), widen(axes[2]), (n.g3, n.v3, moves[3]))
+    s.n4 = ((n.v3, n.g3), (n.v4,), widen(axes[3]), (n.g4, n.v4, moves[4]))
+
+    def open_rows(kept, got, v, g):
+        norms = regroup(ordered(bit("row"), v, g, 1), 2)
+        x0 = regroup(jnp.concatenate([kept, got], axis=0), 2).astype(WIDE)
+        found = [norms[i : i + 1] for i in range(6)]
+        return x0, norm_forward(x0, found[0], found[3])[0].astype(LOW), *found
+
+    s.norm0 = (
+        (n.keep_f, n.got_f2, n.v4, n.g4),
+        (n.x0, n.a1, n.gain0, n.gain1, n.gain2, n.shift0, n.shift1, n.shift2),
+        open_rows,
+        *row_sends(n.a1),
+    )
+
+    near, far = lax.axis_index("near"), lax.axis_index("far")
+    starts = [2 * far + near, 2 * (1 - far) + near, 2 * far + 1 - near, 2 * (1 - far) + 1 - near]
+    steps = jnp.arange(own_frames, dtype=jnp.int32)
+    position = jnp.concatenate([start * own_frames + steps for start in starts])
+    places = (position[:, None], position[None, :], inner)
+
+    def part_ways(t, c):
+        return [jnp.concatenate(v, axis=0) for v in zip(divide(t), divide(c))]
+
+    def trade(kept, got):
+        text = jnp.concatenate([kept[:own_text], got[:own_text]], axis=0)
+        grad = jnp.concatenate([kept[own_text:], got[own_text:]], axis=0)
+        return regroup(text, 2), regroup(grad, 2)
+
+    def gathered(pieces):
+        return (jnp.concatenate(pieces, axis=0),)
+
+    s.trade = (
+        (n.text_states, n.cotangent),
+        (n.keep_b, n.give_b),
+        part_ways,
+        (n.got_b, n.give_b, to_far),
+    )
+    s.both = ((n.keep_b, n.got_b), (n.text0, n.c3), trade, *line_sends(n.c3))
+    s.text_go = ((n.text0,), (n.text,), keep, *row_sends(n.text))
+    s.text_on, s.text_in, s.text_all = rows_steps(n.text, gathered, (), (n.whole_text,))
+    s.c3_on, s.c3_on2, s.c3_in, s.c3_all = line_rows_steps(
+        n.c3, lambda p: gathered(line_pieces(p)), (), (n.whole_grad,)
+    )
+
+    def product_of(first, count):
+        return lambda p, w: rows_product(p, w, first, count * inner, inner)
+
+    s.a1_on, s.a1_in, s.qkv = rows_steps(
+        n.a1, product_of(0, 3), (n.full_self,), (n.whole_self, n.qkv)
+    )
+    s.mix1 = (
+        (n.qkv,),
+        (n.mix1,),
+        lambda q: (attention((q, 0), (q, 1), (q, 2), places, True),),
+    )
+    s.x1, s.x1_on, s.x1_end = sums_steps(
+        (n.mix1,),
+        (n.full_self,),
+        (3,),
+        open_norm,
+        (n.x0, n.gain1, n.shift1),
+        (n.x1, n.a2),
+        *row_sends(n.a2),
+    )
+    s.a2_on, s.a2_in, s.query2 = rows_steps(
+        n.a2, product_of(0, 1), (n.full_cross,), (n.whole_cross, n.query2)
+    )
+    s.text_kv = (
+        (n.whole_text, n.full_cross),
+        (n.text_kv,),
+        lambda a, w: rows_product([a], w, 1, 2 * inner, inner)[1:],
+    )
+    s.mix2 = (
+        (n.query2, n.text_kv),
+        (n.mix2,),
+        lambda q, kv: (attention((q, 0), (kv, 0), (kv, 1), places, False),),
+    )
+    s.x2, s.x2_on, s.x2_end = sums_steps(
+        (n.mix2,),
+        (n.full_cross,),
+        (3,),
+        open_norm,
+        (n.x1, n.gain2, n.shift2),
+        (n.x2, n.a3),
+        *line_sends(n.a3),
+    )
+    s.a3_on, s.a3_on2, s.a3_in, s.middle = line_rows_steps(
+        n.a3,
+        lambda p, w, g: middle(p, w, g, inner),
+        (n.full_mlp, n.whole_grad),
+        (n.whole_mlp, n.active, n.hidden_low),
+    )
+    s.h3, s.h3_go, s.h3_on, s.h3_on2, s.h3_end = line_sums_steps(
+        (n.hidden_low,),
+        (n.full_mlp,),
+        (0,),
+        close_norm,
+        (n.x2, n.gain2, n.c3),
+        (n.e2, n.c2, n.norm2),
+        *row_sends(n.c2),
+    )
+    s.g_mlp = (
+        (n.whole_mlp, n.hidden_low, n.whole_grad, n.active),
+        (n.g_both,),
+        lambda a, u, b, v: (gradient_product([(a, u), (b, v)], 384),),
+        (n.g_sum, n.g_both, to_sum),
+    )
+
+    def share(v):
+        row = bit("row")
+        first, second = halves(v)
+        return jnp.where(row, second, first), jnp.where(row, first, second)
+
+    def last_sum(a, b):
+        total = a.astype(WIDE) + b.astype(WIDE)
+        return total[:, :units], total[:, units:]
+
+    s.g_mlp_row = ((n.g_sum,), (n.g_keep, n.g_give), share, (n.g_got, n.g_give, to_row))
+    s.g_mlp_end = ((n.g_keep, n.g_got), (n.grad_up, n.grad_down), last_sum)
+    s.act, s.act_go, s.act_on, s.act_on2, s.act_end = line_sums_steps(
+        (n.active,),
+        (n.full_mlp,),
+        (1,),
+        lambda a, b, c, x: ((x + plain_total(a, b, c)).astype(LOW),),
+        (n.x2,),
+        (n.act_local,),
+    )
+    s.c2_on, s.c2_in, s.d2 = rows_steps(
+        n.c2, product_of(3, 1), (n.full_cross,), (n.whole_c2, n.d2)
+    )
+    s.mix2_back = (
+        (n.query2, n.text_kv, n.d2),
+        (n.dq2, n.dk2, n.dv2),
+        lambda q, kv, d: attention_back((q, 0), (kv, 0), (kv, 1), d, places, False),
+    )
+    s.h2, s.h2_on, s.h2_end = sums_steps(
+        (n.dq2,),
+        (n.full_cross,),
+        (0,),
+        close_norm,
+        (n.x1, n.gain1, n.e2),
+        (n.e1, n.c1, n.norm1),
+        *row_sends(n.c1),
+    )
+    s.g_cross, s.g_cross_far, s.g_cross_row, s.g_cross_end = gradients_steps(
+        (n.whole_cross, n.dq2, n.whole_text, n.dk2, n.whole_text, n.dv2, n.whole_c2, n.mix2),
+        [half] * 4,
+        (n.grad_cq, n.grad_ck, n.grad_cv, n.grad_cout),
+    )
+    s.tg, s.tg_on, s.tg_end = sums_steps(
+        (n.dk2, n.dv2),
+        (n.full_cross, n.full_cross),
+        (1, 2),
+        lambda *v: (plain_total(*v),),
+        (),
+        (n.text_sum,),
+    )
+    s.c1_on, s.c1_in, s.d1 = rows_steps(
+        n.c1, product_of(3, 1), (n.full_self,), (n.whole_c1, n.d1)
+    )
+    s.mix1_back = (
+        (n.qkv, n.d1),
+        (n.dq1, n.dk1, n.dv1),
+        lambda q, d: attention_back((q, 0), (q, 1), (q, 2), d, places, True),
+    )
+    s.h1, s.h1_on, s.h1_end = sums_steps(
+        (n.dq1, n.dk1, n.dv1),
+        (n.full_self,) * 3,
+        (0, 1, 2),
+        close_norm,
+        (n.x0, n.gain0, n.e1),
+        (n.e0, n.c0, n.norm0),
+    )
+    s.g_self, s.g_self_far, s.g_self_row, s.g_self_end = gradients_steps(
+        (n.whole_self, n.dq1, n.whole_self, n.dk1, n.whole_self, n.dv1, n.whole_c1, n.mix1),
+        [half] * 4,
+        (n.grad_q, n.grad_k, n.grad_v, n.grad_out),
+    )
+
+    def leave(*locals_):
+        cut = [halves(regroup(v, 4)) for v in locals_]
+        return *[v[0] for v in cut], jnp.concatenate([v[1].astype(LOW) for v in cut], axis=0)
+
+    s.leave = (
+        (n.act_local, n.text_sum),
+        (n.keep_act, n.keep_text, n.give_o),
+        leave,
+        (n.got_o, n.give_o, to_far),
+    )
+    s.sent = ((n.got_o,), (n.got_o2,), keep)
+    s.last = ((n.e0,), (n.keep_e, n.give_e), leave, (n.got_e, n.give_e, to_far))
+
+    def narrow(axis, value):
+        middle, upper = value.shape[1] // 2, bit(axis)
+        low, high = value[:, :middle], value[:, middle:]
+        return jnp.where(upper, high, low), jnp.where(upper, low, high)
+
+    def sum_narrow(axis):
+        return lambda v, g: narrow(axis, v + g)
+
+    s.s0 = (
+        (n.norm0, n.norm1, n.norm2),
+        (n.k0, n.w0),
+        lambda *v: narrow(axes[4], regroup(jnp.concatenate(v, axis=0), 4)),
+        (n.h0, n.w0, moves[4]),
+    )
+    s.s1 = ((n.k0, n.h0), (n.k1, n.w1), sum_narrow(axes[3]), (n.h1, n.w1, moves[3]))
+    s.s2 = ((n.k1, n.h1), (n.k2, n.w2), sum_narrow(axes[2]), (n.h2, n.w2, moves[2]))
+    s.s3 = ((n.k2, n.h2), (n.k3, n.w3), sum_narrow(axes[1]), (n.h3, n.w3, moves[1]))
+    s.s4 = ((n.k3, n.h3), (n.k4, n.w4), sum_narrow(axes[0]), (n.h4, n.w4, moves[0]))
+    s.s5 = ((n.k4, n.h4), (n.norm_sums,), lambda v, g: (v + g,))
+    return (
+        s.frames,
+        s.w_self,
+        s.n0,
+        s.w_self_far,
+        s.w_mlp,
+        s.n1,
+        s.frames_in,
+        s.n2,
+        s.n3,
+        s.n4,
+        s.w_mlp_all,
+        s.norm0,
+        s.w_self_all,
+        s.trade,
+        s.w_cross,
+        s.a1_on,
+        s.w_cross_far,
+        s.a1_in,
+        s.qkv,
+        s.mix1,
+        s.w_cross_all,
+        s.w_mlp_go,
+        s.x1,
+        s.x1_on,
+        s.both,
+        s.text_go,
+        s.x1_end,
+        s.text_on,
+        s.a2_on,
+        s.text_in,
+        s.text_all,
+        s.c3_on,
+        s.a2_in,
+        s.text_kv,
+        s.query2,
+        s.mix2,
+        s.x2,
+        s.x2_on,
+        s.c3_on2,
+        s.x2_end,
+        s.c3_in,
+        s.c3_all,
+        s.a3_on,
+        s.a3_on2,
+        s.a3_in,
+        s.middle,
+        s.h3,
+        s.h3_go,
+        s.g_mlp,
+        s.h3_on,
+        s.act,
+        s.h3_on2,
+        s.h3_end,
+        s.c2_on,
+        s.c2_in,
+        s.act_go,
+        s.d2,
+        s.mix2_back,
+        s.h2,
+        s.g_cross,
+        s.h2_on,
+        s.h2_end,
+        s.c1_on,
+        s.g_mlp_row,
+        s.act_on,
+        s.c1_in,
+        s.d1,
+        s.mix1_back,
+        s.g_self,
+        s.g_cross_far,
+        s.h1,
+        s.act_on2,
+        s.h1_on,
+        s.g_mlp_end,
+        s.act_end,
+        s.g_cross_row,
+        s.g_self_far,
+        s.h1_end,
+        s.last,
+        s.tg,
+        s.s0,
+        s.s1,
+        s.tg_on,
+        s.s2,
+        s.g_cross_end,
+        s.g_self_row,
+        s.tg_end,
+        s.leave,
+        s.s3,
+        s.s4,
+        s.s5,
+        s.sent,
+        s.g_self_end,
+    )
+
+
+def on_device_pairs(
+    frames,
+    text_states,
+    self_q,
+    self_k,
+    self_v,
+    self_out,
+    cross_q,
+    cross_k,
+    cross_v,
+    cross_out,
+    mlp_up,
+    mlp_down,
+    norm_gains,
+    norm_shifts,
+    cotangent,
+):
+    n = Name()
+    values = {
+        n.frames: frames,
+        n.text_states: text_states,
+        n.self_q: self_q,
+        n.self_k: self_k,
+        n.self_v: self_v,
+        n.self_out: self_out.T,
+        n.cross_q: cross_q,
+        n.cross_k: cross_k,
+        n.cross_v: cross_v,
+        n.cross_out: cross_out.T,
+        n.mlp_up: mlp_up,
+        n.mlp_down: mlp_down.T,
+        n.norm_gains: norm_gains,
+        n.norm_shifts: norm_shifts,
+        n.cotangent: cotangent,
+    }
+    order = plan_pairs(
+        n, self_q.shape[1], mlp_up.shape[1], frames.shape[1], text_states.shape[1]
+    )
+    values = run_steps(values, order)
+    far_bit, own = bit("far"), frames.shape[1]
+
+    def arrive(own, other):
+        other = values[other] if isinstance(other, Name) else other
+        own, other = values[own], other.astype(values[own].dtype)
+        return jnp.stack([jnp.where(far_bit, other, own), jnp.where(far_bit, own, other)])
+
+    return (
+        arrive(n.keep_act, values[n.got_o2][:own]),
+        arrive(n.keep_e, n.got_e),
+        arrive(n.keep_text, values[n.got_o2][own:]),
+        values[n.grad_q],
+        values[n.grad_k],
+        values[n.grad_v],
+        values[n.grad_out].T,
+        values[n.grad_cq],
+        values[n.grad_ck],
+        values[n.grad_cv],
+        values[n.grad_cout].T,
+        values[n.grad_up],
+        values[n.grad_down].T,
+        values[n.norm_sums][::2],
+        values[n.norm_sums][1::2],
+    )
+
+
 def solution(mesh):
-    rows = P("dp", "tensor", None)
-    into = P("dp", "tensor")
-    out_of = P("tensor", "dp")
-    norms = P(None, ("dp", "tensor"))
+    paired = dict(mesh.shape) == {"dp": 8, "tensor": 4}
+    names = ("row", "column", "core", "far", "near")
+    dp, tensor = (names[:3], names[3:]) if paired else (("dp",), ("tensor",))
+    rows = P(dp, tensor, None)
+    into = P(dp, tensor)
+    out_of = P(tensor, dp)
+    norms = P(None, dp + tensor)
     weights = (into, into, into, out_of, into, into, into, out_of, into, out_of)
     return jax.shard_map(
-        on_device,
-        mesh=mesh,
+        on_device_pairs if paired else on_device,
+        mesh=Mesh(mesh.devices.reshape((2,) * 5), names) if paired else mesh,
         in_specs=(rows, rows, *weights, norms, norms, rows),
         out_specs=(rows, rows, rows, *weights, norms, norms),
         check_vma=False,

time: 898 us -> 588 us (0.65)
  waiting for transfers between devices: 604 us -> 202 us
  starting transfers between devices: 18.8 us -> 123 us
  matrix products: 97.9 us -> 0 us
  Pallas kernels: 0 us -> 85.2 us
  local copies, waits for them, and re-layouts: 80 us -> 108 us
  blocking collectives: 17.6 us -> 0 us
  other arithmetic: 52.9 us -> 42.3 us
    all_gather x9 -> x3, waiting for transfers between devices: 289 us -> 0.01 us  [to_all(): return lax.all_gather(v, ('column', 'core'), axis=0, tiled=True)]
    reduce_scatter x7 -> x3, waiting for transfers between devices: 200 us -> 6.56 us  [to_sum(): lax.psum_scatter(v, ('column', 'core'), scatter_dimension=0, tiled=True)]
    ppermute x10 -> x88, waiting for transfers between devices: 8.6 us -> 195 us  [the longest x64 147 us: exchange(): return lax.ppermute(value, axis, [(0, 1), (1, 0)])]
    ppermute x10 -> x88, starting transfers between devices: 16.5 us -> 122 us  [the longest x64 79.8 us: exchange(): return lax.ppermute(value, axis, [(0, 1), (1, 0)])]
    unnamed x22 -> x6, waiting for transfers between devices: 107 us -> 0.76 us
    dot_general x31 -> x0, matrix products: 94.8 us -> none  [the longest x7 36.7 us: product(): return jnp.dot(operand, matrix, preferred_element_type=WIDE)]
    pallas_call x0 -> x30, Pallas kernels: none -> 85.2 us  [the longest x7 21.5 us: pieces_product(): pl.pallas_call(body, grid=(depth // tile,), in_specs=specs, out_specs=[pl...]
    unnamed x159 -> x318, local copies, waits for them, and re-layouts: 49 us -> 76.7 us
  transfers between devices with their start and end apart: 29 -> 94, of which waited for: 26 -> 47; matrix products, arithmetic and copies ran while one was open for 19% -> 9% of each run, Pallas kernels for 0% -> 10%
where the time goes in v3:
time: 588 us; the launch traced here: 577 us
  waiting for transfers between devices  202 us (34%)
  starting transfers between devices  123 us (21%)
  local copies, waits for them, and re-layouts  108 us (18%)
  Pallas kernels  85.2 us (14%)
  other arithmetic  42.3 us (7%)
  between operations  16.6 us (3%)
    ppermute x64, waiting for transfers between devices, exchange(): return lax.ppermute(value, axis, [(0, 1), (1, 0)])  147 us
    ppermute x64, starting transfers between devices, exchange(): return lax.ppermute(value, axis, [(0, 1), (1, 0)])  79.8 us
    unnamed x318, local copies, waits for them, and re-layouts  76.7 us
    ppermute x24, waiting for transfers between devices, stepping(): return lambda v: lax.ppermute(v, ('far', 'near'), perm)  48.6 us
    ppermute x24, starting transfers between devices, stepping(): return lambda v: lax.ppermute(v, ('far', 'near'), perm)  42.5 us
    pallas_call x7, Pallas kernels, pieces_product(): pl.pallas_call(body, grid=(depth // tile,), in_specs=specs, out_specs=[pl...  21.5 us
    pallas_call x3, Pallas kernels, gradient_product(): pl.pallas_call(body, grid=(sum(tiles),), in_specs=specs, out_specs=pl.Blo...  18.3 us
    pallas_call x2, Pallas kernels, attention_back(): pl.pallas_call(functools.partial(attend_back_kernel, heads, causal), grid...  13.2 us
  transfers between devices with their start and end apart: 94, of which 47 were waited for; matrix products, arithmetic and copies ran while one was open for 9% of the time, Pallas kernels for 10%

profile of v3, /device:TPU:0, one launch (start us, length us, event | category | flops | bytes accessed | tf_op | source)
XLA Modules:
  0.0 577.1 jit_solution(14668448825499752406)
XLA Ops:
  13.2 7.0 %collective-permute-done.2 = bf16[192,768]{1,0:T(8,128)(2,1)S(1)} collective-permute-done((bf16[192,768]{1,0:T(8,128)(2,1)S(1)}, bf16[192,768]{1,0:T(8,128)(2,1)S(1)}, u32[]{:S(2)}, u32[]{:S(2)}) %collective-permute-start.2) | collective-permute-done | bytes 294944 | tf_op jit(solution)/shard_map/ppermute | solution.py:283
  38.7 9.4 %collective-permute-done.7 = bf16[192,3072]{1,0:T(8,128)(2,1)} collective-permute-done((bf16[192,3072]{1,0:T(8,128)(2,1)S(1)}, bf16[192,3072]{1,0:T(8,128)(2,1)}, u32[]{:S(2)}, u32[]{:S(2)}) %collective-permute-start.7) | collective-permute-done | bytes 1179680 | tf_op jit(solution)/shard_map/ppermute | solution.py:283
  53.3 11.4 %collective-permute-done.10 = bf16[384,768]{1,0:T(8,128)(2,1)} collective-permute-done((bf16[384,768]{1,0:T(8,128)(2,1)S(1)}, bf16[384,768]{1,0:T(8,128)(2,1)}, u32[]{:S(2)}, u32[]{:S(2)}) %collective-permute-start.10) | collective-permute-done | bytes 589856 | tf_op jit(solution)/shard_map/ppermute | solution.py:283
  72.8 5.6 collective-permute-done.8.refs_1_
  91.9 14.3 %collective-permute-done.11.refs_3_ = bf16[64,1536]{1,0:T(8,128)(2,1)S(1)} collective-permute-done((bf16[64,1536]{1,0:T(8,128)(2,1)S(1)}, bf16[64,1536]{1,0:T(8,128)(2,1)S(1)}, u32[]{:S(2)}, u32[]{:S(2)}) %collective-permute-start.11) | collective-permute-done | bytes 196640 | tf_op jit(solution)/shard_map/ppermute | solution.py:283
  167.5 5.8 %collective-permute-done.22 = bf16[32,1536]{1,0:T(8,128)(2,1)S(1)} collective-permute-done((bf16[32,1536]{1,0:T(8,128)(2,1)S(1)}, bf16[32,1536]{1,0:T(8,128)(2,1)S(1)}, u32[]{:S(2)}, u32[]{:S(2)}) %collective-permute-start.22) | collective-permute-done | bytes 98336 | tf_op jit(solution)/shard_map/ppermute | solution.py:283
  215.0 5.6 collective-permute-done.30.one_ref
  226.1 4.7 collective-permute-done.32.near_ref
  242.1 6.7 %collective-permute-done.37.refs_1_ = bf16[128,1536]{1,0:T(8,128)(2,1)S(1)} collective-permute-done((bf16[128,1536]{1,0:T(8,128)(2,1)S(1)}, bf16[128,1536]{1,0:T(8,128)(2,1)S(1)}, u32[]{:S(2)}, u32[]{:S(2)}) %collective-permute-start.37) | collective-permute-done | bytes 393248 | tf_op jit(solution)/shard_map/ppermute | solution.py:643
  252.3 11.4 %collective-permute-done.41.refs_3_ = bf16[128,1536]{1,0:T(8,128)(2,1)S(1)} collective-permute-done((bf16[128,1536]{1,0:T(8,128)(2,1)S(1)}, bf16[128,1536]{1,0:T(8,128)(2,1)S(1)}, u32[]{:S(2)}, u32[]{:S(2)}) %collective-permute-start.41) | collective-permute-done | bytes 393248 | tf_op jit(solution)/shard_map/ppermute | solution.py:643
  267.9 6.9 %collective-permute-done.43.refs_6_ = bf16[128,1536]{1,0:T(8,128)(2,1)S(1)} collective-permute-done((bf16[128,1536]{1,0:T(8,128)(2,1)S(1)}, bf16[128,1536]{1,0:T(8,128)(2,1)S(1)}, u32[]{:S(2)}, u32[]{:S(2)}) %collective-permute-start.43) | collective-permute-done | bytes 393248 | tf_op jit(solution)/shard_map/ppermute | solution.py:643
  284.0 9.6 %middle.1 = (bf16[512,1536]{1,0:T(8,128)(2,1)S(1)}, bf16[512,1536]{1,0:T(8,128)(2,1)S(1)}, bf16[512,1536]{1,0:T(8,128)(2,1)S(1)}) custom-call(bf16[128,1536]{1,0:T(8,128)(2,1)S(1)} %copy-done.95, bf16[128,1536]{1,0:T(8,128)(2,1)S(1)} %copy-done.99, bf16[128,1536]{1,0:T(8,128)(2,1)S(1)} %copy-done.105, bf16[128,1536]{1,0:T(8,128)(2,1)S(1)} %copy-done.103, ...), custom_call_target="tpu_custom_call" | custom-call | flops 1 | bytes 1 | tf_op jit(solution)/shard_map/middle/pallas_call | solution.py:388
  301.2 10.0 %gradient_product.3 = bf16[1536,3072]{1,0:T(8,128)(2,1)} custom-call(bf16[512,1536]{1,0:T(8,128)(2,1)S(1)} %get-tuple-element.522.refs_0_, bf16[512,1536]{1,0:T(8,128)(2,1)S(1)} %get-tuple-element.523.refs_0_.refs_1_, bf16[512,1536]{1,0:T(8,128)(2,1)S(1)} %copy-done.12, bf16[512,1536]{1,0:T(8,128)(2,1)S(1)} %get-tuple-element.530.refs_3_.refs_0_), custom_call_target="tpu_custom_call" | custom-call | flops 1 | bytes 1 | tf_op jit(solution)/shard_map/gradient_product/pallas_call | solution.py:463
  313.5 6.6 %collective-permute-done.45 = bf16[128,1536]{1,0:T(8,128)(2,1)S(1)} collective-permute-done((bf16[128,1536]{1,0:T(8,128)(2,1)}, bf16[128,1536]{1,0:T(8,128)(2,1)S(1)}, u32[]{:S(2)}, u32[]{:S(2)}) %collective-permute-start.45) | collective-permute-done | bytes 393248 | tf_op jit(solution)/shard_map/ppermute | solution.py:643
  332.2 5.1 pieces_product.10
  341.4 5.4 collective-permute-done.49.row_ref
  346.7 5.6 collective-permute-done.48.near_ref
  355.5 6.4 %collective-permute-done.50.refs_2_ = bf16[128,1536]{1,0:T(8,128)(2,1)S(1)} collective-permute-done((bf16[128,1536]{1,0:T(8,128)(2,1)S(1)}, bf16[128,1536]{1,0:T(8,128)(2,1)S(1)}, u32[]{:S(2)}, u32[]{:S(2)}) %collective-permute-start.50) | collective-permute-done | bytes 393248 | tf_op jit(solution)/shard_map/ppermute | solution.py:283
  370.2 5.7 attend_back.2
  398.9 9.0 %collective-permute-done.58.near_ref = bf16[128,1536]{1,0:T(8,128)(2,1)S(1)} collective-permute-done((bf16[128,1536]{1,0:T(8,128)(2,1)S(1)}, bf16[128,1536]{1,0:T(8,128)(2,1)S(1)}, u32[]{:S(2)}, u32[]{:S(2)}) %collective-permute-start.58) | collective-permute-done | bytes 393248 | tf_op jit(solution)/shard_map/ppermute | solution.py:283
  437.5 7.5 %attend_back.3 = (bf16[512,384]{1,0:T(8,128)(2,1)S(1)}, bf16[512,384]{1,0:T(8,128)(2,1)S(1)}, bf16[512,384]{1,0:T(8,128)(2,1)S(1)}) custom-call(bf16[512,1152]{1,0:T(8,128)(2,1)S(1)} %get-tuple-element.618.q_ref.k_ref.v_ref, bf16[512,1152]{1,0:T(8,128)(2,1)S(1)} %get-tuple-element.618.q_ref.k_ref.v_ref, ...), custom_call_target="tpu_custom_call" | custom-call | flops 1 | bytes 1 | tf_op jit(solution)/shard_map/attend_back/pallas_call | solution.py:602
  492.2 6.6 %reduce-scatter.8.cloned.1.call-done = bf16[384,1536]{1,0:T(8,128)(2,1)} async-done(((bf16[1536,1536]{1,0:T(8,128)(2,1)}), bf16[384,1536]{1,0:T(8,128)(2,1)}) %reduce-scatter.8.cloned.1.call-update) | async-done | bytes 1179664 | tf_op jit(solution)/shard_map/reduce_scatter | solution.py:663
  529.0 18.7 %collective-permute-done.79 = bf16[384,768]{1,0:T(8,128)(2,1)S(1)} collective-permute-done((bf16[384,768]{1,0:T(8,128)(2,1)S(1)}, bf16[384,768]{1,0:T(8,128)(2,1)S(1)}, u32[]{:S(2)}, u32[]{:S(2)}) %collective-permute-start.79) | collective-permute-done | bytes 589856 | tf_op jit(solution)/shard_map/ppermute | solution.py:283
  559.3 5.1 collective-permute-done.82
  (657 shorter events, 370.3 us)
Async XLA Ops:
  7.2 100.4 %all-gather.4.cloned.1.call-start = ((), (), s32[]{:S(2)}) async-start(), calls=%async_computation.3 | async-start | bytes 5898240 | tf_op jit(solution)/shard_map/all_gather | solution.py:659
  20.5 27.6 %collective-permute-start.7 = (bf16[192,3072]{1,0:T(8,128)(2,1)S(1)}, bf16[192,3072]{1,0:T(8,128)(2,1)}, u32[]{:S(2)}, u32[]{:S(2)}) collective-permute-start(bf16[192,3072]{1,0:T(8,128)(2,1)S(1)} %constant_dynamic-update-slice_fusion), channel_id=1, source_target_pairs={{0,16},{16,0},{1,17},{17,1},{2,18},{18,2},{3,19},{19,3},{4,20},{20... | collective-permute-start | bytes 3538952 | tf_op jit(solution)/shard_map/ppermute | solution.py:283
  35.9 28.8 %collective-permute-start.10 = (bf16[384,768]{1,0:T(8,128)(2,1)S(1)}, bf16[384,768]{1,0:T(8,128)(2,1)}, u32[]{:S(2)}, u32[]{:S(2)}) collective-permute-start(bf16[384,768]{1,0:T(8,128)(2,1)S(1)} %maximum_select_fusion.1), channel_id=1, source_target_pairs={{0,2},{2,0},{1,3},{3,1},{4,6},{6,4},{5,7},{7,5},{8,10},{10,8},{9,1... | collective-permute-start | bytes 1769480 | tf_op jit(solution)/shard_map/ppermute | solution.py:283
  68.3 127.9 %all-gather.6.cloned.1.call-start = ((), (), s32[]{:S(2)}) async-start(), calls=%async_computation.4 | async-start | bytes 5898240 | tf_op jit(solution)/shard_map/all_gather | solution.py:659
  86.6 36.4 %collective-permute-start.14 = (bf16[384,768]{1,0:T(8,128)(2,1)}, bf16[384,768]{1,0:T(8,128)(2,1)}, u32[]{:S(2)}, u32[]{:S(2)}) collective-permute-start(bf16[384,768]{1,0:T(8,128)(2,1)} %maximum_select_fusion.2), channel_id=1, source_target_pairs={{0,2},{2,0},{1,3},{3,1},{4,6},{6,4},{5,7},{7,5},{8,10},{10,8},{9,1... | collective-permute-start | bytes 1769480 | tf_op jit(solution)/shard_map/ppermute | solution.py:283
  90.5 16.4 %collective-permute-start.12 = (bf16[64,1536]{1,0:T(8,128)(2,1)S(1)}, bf16[64,1536]{1,0:T(8,128)(2,1)S(1)}, u32[]{:S(2)}, u32[]{:S(2)}) collective-permute-start(bf16[64,1536]{1,0:T(8,128)(2,1)S(1)} %slice.605), channel_id=1, source_target_pairs={{0,16},{16,0},{1,17},{17,1},{2,18},{18,2},{3,19},{19,3},{4,20},{20... | collective-permute-start | bytes 589832 | tf_op jit(solution)/shard_map/ppermute | solution.py:283
  131.2 144.4 %all-gather.8.cloned.1.call-start = ((), (), s32[]{:S(2)}) async-start(), calls=%async_computation.5 | async-start | bytes 11796480 | tf_op jit(solution)/shard_map/all_gather | solution.py:659
  131.9 294.0 %reduce-scatter.4.cloned.1.call-start = ((), (), s32[]{:S(2)}) async-start(), calls=%async_computation.6 | async-start | bytes 11796480 | tf_op jit(solution)/shard_map/reduce_scatter | solution.py:663
  162.6 17.5 %collective-permute-start.20 = (bf16[128,1536]{1,0:T(8,128)(2,1)S(1)}, bf16[128,1536]{1,0:T(8,128)(2,1)S(1)}, u32[]{:S(2)}, u32[]{:S(2)}) collective-permute-start(bf16[128,1536]{1,0:T(8,128)(2,1)S(1)} %get-tuple-element.456.refs_0_), channel_id=1, source_target_pairs={{0,1},{1,0},{2,3},{3,2},{4,5},{5,4},{6,7},{7,6},{8,9},{9,8},{10,11... | collective-permute-start | bytes 1179656 | tf_op jit(solution)/shard_map/ppermute | solution.py:283
  162.7 18.7 %collective-permute-start.21 = (bf16[128,1536]{1,0:T(8,128)(2,1)S(1)}, bf16[128,1536]{1,0:T(8,128)(2,1)S(1)}, u32[]{:S(2)}, u32[]{:S(2)}) collective-permute-start(bf16[128,1536]{1,0:T(8,128)(2,1)S(1)} %get-tuple-element.456.refs_0_), channel_id=1, source_target_pairs={{0,16},{16,0},{1,17},{17,1},{2,18},{18,2},{3,19},{19,3},{4,20},{20... | collective-permute-start | bytes 1179656 | tf_op jit(solution)/shard_map/ppermute | solution.py:283
  190.8 33.3 %collective-permute-start.34 = (bf16[128,1536]{1,0:T(8,128)(2,1)}, bf16[128,1536]{1,0:T(8,128)(2,1)}, u32[]{:S(2)}, u32[]{:S(2)}) collective-permute-start(bf16[128,1536]{1,0:T(8,128)(2,1)} %collective-permute-done.26), channel_id=1, source_target_pairs={{1,2},{2,3},{5,6},{6,7},{9,10},{10,11},{13,14},{14,15},{17,18},{18... | collective-permute-start | bytes 1179656 | tf_op jit(solution)/shard_map/ppermute | solution.py:643
  192.3 31.8 %collective-permute-start.35 = (bf16[128,1536]{1,0:T(8,128)(2,1)}, bf16[128,1536]{1,0:T(8,128)(2,1)}, u32[]{:S(2)}, u32[]{:S(2)}) collective-permute-start(bf16[128,1536]{1,0:T(8,128)(2,1)} %collective-permute-done.27), channel_id=1, source_target_pairs={{2,1},{1,0},{6,5},{5,4},{10,9},{9,8},{14,13},{13,12},{18,17},{17,1... | collective-permute-start | bytes 1179656 | tf_op jit(solution)/shard_map/ppermute | solution.py:643
  311.2 147.5 %reduce-scatter.6.cloned.1.call-start = ((), (), s32[]{:S(2)}) async-start(), calls=%async_computation.7 | async-start | bytes 5898240 | tf_op jit(solution)/shard_map/reduce_scatter | solution.py:663
  387.4 111.3 %reduce-scatter.8.cloned.1.call-start = ((), (), s32[]{:S(2)}) async-start(), calls=%async_computation.8 | async-start | bytes 5898240 | tf_op jit(solution)/shard_map/reduce_scatter | solution.py:663
  455.2 17.1 %collective-permute-start.63 = (bf16[128,1536]{1,0:T(8,128)(2,1)S(1)}, bf16[128,1536]{1,0:T(8,128)(2,1)S(1)}, u32[]{:S(2)}, u32[]{:S(2)}) collective-permute-start(bf16[128,1536]{1,0:T(8,128)(2,1)S(1)} %copy-done.141), channel_id=1, source_target_pairs={{0,1},{1,2},{4,5},{5,6},{8,9},{9,10},{12,13},{13,14},{16,17},{17,1... | collective-permute-start | bytes 1179656 | tf_op jit(solution)/shard_map/ppermute | solution.py:643
  457.9 27.2 %collective-permute-start.68 = (bf16[192,3072]{1,0:T(8,128)(2,1)}, bf16[192,3072]{1,0:T(8,128)(2,1)}, u32[]{:S(2)}, u32[]{:S(2)}) collective-permute-start(bf16[192,3072]{1,0:T(8,128)(2,1)} %get-tuple-element.715), channel_id=1, source_target_pairs={{0,16},{16,0},{1,17},{17,1},{2,18},{18,2},{3,19},{19,3},{4,20},{20... | collective-permute-start | bytes 3538952 | tf_op jit(solution)/shard_map/ppermute | solution.py:283
  461.4 29.9 %collective-permute-start.73 = (bf16[384,768]{1,0:T(8,128)(2,1)S(1)}, bf16[384,768]{1,0:T(8,128)(2,1)S(1)}, u32[]{:S(2)}, u32[]{:S(2)}) collective-permute-start(bf16[384,768]{1,0:T(8,128)(2,1)S(1)} %pad_maximum_fusion.3), channel_id=1, source_target_pairs={{0,2},{2,0},{1,3},{3,1},{4,6},{6,4},{5,7},{7,5},{8,10},{10,8},{9,1... | collective-permute-start | bytes 1769480 | tf_op jit(solution)/shard_map/ppermute | solution.py:283
  483.9 19.0 %collective-permute-start.71 = (bf16[128,1536]{1,0:T(8,128)(2,1)S(1)}, bf16[128,1536]{1,0:T(8,128)(2,1)S(1)}, u32[]{:S(2)}, u32[]{:S(2)}) collective-permute-start(bf16[128,1536]{1,0:T(8,128)(2,1)S(1)} %get-tuple-element.651), channel_id=1, source_target_pairs={{0,1},{1,0},{2,3},{3,2},{4,5},{5,4},{6,7},{7,6},{8,9},{9,8},{10,11... | collective-permute-start | bytes 1179656 | tf_op jit(solution)/shard_map/ppermute | solution.py:283
  485.0 17.8 %collective-permute-start.72 = (bf16[128,1536]{1,0:T(8,128)(2,1)S(1)}, bf16[128,1536]{1,0:T(8,128)(2,1)S(1)}, u32[]{:S(2)}, u32[]{:S(2)}) collective-permute-start(bf16[128,1536]{1,0:T(8,128)(2,1)S(1)} %get-tuple-element.652), channel_id=1, source_target_pairs={{0,16},{16,0},{1,17},{17,1},{2,18},{18,2},{3,19},{19,3},{4,20},{20... | collective-permute-start | bytes 1179656 | tf_op jit(solution)/shard_map/ppermute | solution.py:283
  515.6 32.0 %collective-permute-start.79 = (bf16[384,768]{1,0:T(8,128)(2,1)S(1)}, bf16[384,768]{1,0:T(8,128)(2,1)S(1)}, u32[]{:S(2)}, u32[]{:S(2)}) collective-permute-start(bf16[384,768]{1,0:T(8,128)(2,1)S(1)} %copy-done.137), channel_id=1, source_target_pairs={{0,2},{2,0},{1,3},{3,1},{4,6},{6,4},{5,7},{7,5},{8,10},{10,8},{9,1... | collective-permute-start | bytes 1769480 | tf_op jit(solution)/shard_map/ppermute | solution.py:283
  521.2 30.1 %collective-permute-start.86 = (bf16[64,1536]{1,0:T(8,128)(2,1)}, bf16[64,1536]{1,0:T(8,128)(2,1)S(1)}, u32[]{:S(2)}, u32[]{:S(2)}) collective-permute-start(bf16[64,1536]{1,0:T(8,128)(2,1)} %slice.955), channel_id=1, source_target_pairs={{0,2},{2,0},{1,3},{3,1},{4,6},{6,4},{5,7},{7,5},{8,10},{10,8},{9,1... | collective-permute-start | bytes 589832 | tf_op jit(solution)/shard_map/ppermute | solution.py:283
  523.7 24.3 %collective-permute-start.77 = (bf16[32,1536]{1,0:T(8,128)(2,1)S(1)}, bf16[32,1536]{1,0:T(8,128)(2,1)S(1)}, u32[]{:S(2)}, u32[]{:S(2)}) collective-permute-start(bf16[32,1536]{1,0:T(8,128)(2,1)S(1)} %get-tuple-element.689), channel_id=1, source_target_pairs={{0,1},{1,0},{2,3},{3,2},{4,5},{5,4},{6,7},{7,6},{8,9},{9,8},{10,11... | collective-permute-start | bytes 294920 | tf_op jit(solution)/shard_map/ppermute | solution.py:283
  525.2 22.7 %collective-permute-start.78 = (bf16[32,1536]{1,0:T(8,128)(2,1)S(1)}, bf16[32,1536]{1,0:T(8,128)(2,1)S(1)}, u32[]{:S(2)}, u32[]{:S(2)}) collective-permute-start(bf16[32,1536]{1,0:T(8,128)(2,1)S(1)} %get-tuple-element.690), channel_id=1, source_target_pairs={{0,16},{16,0},{1,17},{17,1},{2,18},{18,2},{3,19},{19,3},{4,20},{20... | collective-permute-start | bytes 294920 | tf_op jit(solution)/shard_map/ppermute | solution.py:283
  526.5 22.9 %collective-permute-start.83 = (f32[6,192]{1,0:T(8,128)}, f32[6,192]{1,0:T(8,128)S(1)}, u32[]{:S(2)}, u32[]{:S(2)}) collective-permute-start(f32[6,192]{1,0:T(8,128)} %get-tuple-element.872), channel_id=1, source_target_pairs={{0,4},{4,0},{1,5},{5,1},{2,6},{6,2},{3,7},{7,3},{8,12},{12,8},{9,1... | collective-permute-start | bytes 13832 | tf_op jit(solution)/shard_map/ppermute | solution.py:283
  (227 other events, 1413.8 us)
Sparse Core Ops, SparseCore 0:
  68.4 36.2 all-gather.3
  131.3 35.6 all-gather.5
  168.6 64.2 all-gather.7
  311.3 74.9 reduce-scatter.3
  388.6 47.8 reduce-scatter.5
  454.4 44.3 reduce-scatter.7

commit v4 on v3

--- a/solution.py
+++ b/solution.py
@@ -1074,33 +1074,31 @@
         cut = [halves(regroup(v, 4)) for v in locals_]
         return *[v[0] for v in cut], jnp.concatenate([v[1].astype(LOW) for v in cut], axis=0)
 
-    s.leave = (
-        (n.act_local, n.text_sum),
-        (n.keep_act, n.keep_text, n.give_o),
-        leave,
-        (n.got_o, n.give_o, to_far),
-    )
-    s.sent = ((n.got_o,), (n.got_o2,), keep)
+    s.leave_act = ((n.act_local,), (n.keep_act, n.give_act), leave, (n.got_act, n.give_act, to_far))
+    s.leave_text = ((n.text_sum,), (n.keep_text, n.give_text), leave, (n.got_text, n.give_text, to_far))
+    s.sent = ((n.got_act, n.got_text), (n.got_act2, n.got_text2), keep)
     s.last = ((n.e0,), (n.keep_e, n.give_e), leave, (n.got_e, n.give_e, to_far))
-
-    def narrow(axis, value):
-        middle, upper = value.shape[1] // 2, bit(axis)
-        low, high = value[:, :middle], value[:, middle:]
+    s.last_in = ((n.got_e,), (n.got_e2,), keep)
+
+    def narrow(axis, outer, value):
+        count, upper = value.shape[0], bit(axis)
+        split = value.reshape(count, outer, 2, -1)
+        low, high = [split[:, :, i].reshape(count, -1) for i in range(2)]
         return jnp.where(upper, high, low), jnp.where(upper, low, high)
 
-    def sum_narrow(axis):
-        return lambda v, g: narrow(axis, v + g)
+    def sum_narrow(axis, outer):
+        return lambda v, g: narrow(axis, outer, v + g)
 
     s.s0 = (
         (n.norm0, n.norm1, n.norm2),
         (n.k0, n.w0),
-        lambda *v: narrow(axes[4], regroup(jnp.concatenate(v, axis=0), 4)),
-        (n.h0, n.w0, moves[4]),
-    )
-    s.s1 = ((n.k0, n.h0), (n.k1, n.w1), sum_narrow(axes[3]), (n.h1, n.w1, moves[3]))
-    s.s2 = ((n.k1, n.h1), (n.k2, n.w2), sum_narrow(axes[2]), (n.h2, n.w2, moves[2]))
-    s.s3 = ((n.k2, n.h2), (n.k3, n.w3), sum_narrow(axes[1]), (n.h3, n.w3, moves[1]))
-    s.s4 = ((n.k3, n.h3), (n.k4, n.w4), sum_narrow(axes[0]), (n.h4, n.w4, moves[0]))
+        lambda *v: narrow(axes[1], 8, regroup(jnp.concatenate(v, axis=0), 4)),
+        (n.h0, n.w0, moves[1]),
+    )
+    s.s1 = ((n.k0, n.h0), (n.k1, n.w1), sum_narrow(axes[0], 8), (n.h1, n.w1, moves[0]))
+    s.s2 = ((n.k1, n.h1), (n.k2, n.w2), sum_narrow(axes[2], 4), (n.h2, n.w2, moves[2]))
+    s.s3 = ((n.k2, n.h2), (n.k3, n.w3), sum_narrow(axes[3], 2), (n.h3, n.w3, moves[3]))
+    s.s4 = ((n.k3, n.h3), (n.k4, n.w4), sum_narrow(axes[4], 1), (n.h4, n.w4, moves[4]))
     s.s5 = ((n.k4, n.h4), (n.norm_sums,), lambda v, g: (v + g,))
     return (
         s.frames,
@@ -1181,19 +1179,21 @@
         s.g_cross_row,
         s.g_self_far,
         s.h1_end,
+        s.leave_act,
         s.last,
+        s.s0,
         s.tg,
-        s.s0,
         s.s1,
         s.tg_on,
+        s.g_self_row,
         s.s2,
-        s.g_cross_end,
-        s.g_self_row,
         s.tg_end,
-        s.leave,
+        s.leave_text,
         s.s3,
         s.s4,
+        s.g_cross_end,
         s.s5,
+        s.last_in,
         s.sent,
         s.g_self_end,
     )
@@ -1238,17 +1238,16 @@
         n, self_q.shape[1], mlp_up.shape[1], frames.shape[1], text_states.shape[1]
     )
     values = run_steps(values, order)
-    far_bit, own = bit("far"), frames.shape[1]
+    far_bit = bit("far")
 
     def arrive(own, other):
-        other = values[other] if isinstance(other, Name) else other
-        own, other = values[own], other.astype(values[own].dtype)
+        own, other = values[own], values[other].astype(values[own].dtype)
         return jnp.stack([jnp.where(far_bit, other, own), jnp.where(far_bit, own, other)])
 
     return (
-        arrive(n.keep_act, values[n.got_o2][:own]),
-        arrive(n.keep_e, n.got_e),
-        arrive(n.keep_text, values[n.got_o2][own:]),
+        arrive(n.keep_act, n.got_act2),
+        arrive(n.keep_e, n.got_e2),
+        arrive(n.keep_text, n.got_text2),
         values[n.grad_q],
         values[n.grad_k],
         values[n.grad_v],

time: 588 us -> 587 us (level)
  waiting for transfers between devices: 202 us -> 195 us
    ppermute x64 -> x65, waiting for transfers between devices: 147 us -> 140 us  [exchange(): return lax.ppermute(value, axis, [(0, 1), (1, 0)])]
    ppermute x64 -> x65, starting transfers between devices: 79.8 us -> 81.8 us  [exchange(): return lax.ppermute(value, axis, [(0, 1), (1, 0)])]
    unnamed x318 -> x317, local copies, waits for them, and re-layouts: 76.7 us -> 75.9 us
  transfers between devices with their start and end apart: 94 -> 95, of which waited for: 47 -> 49; matrix products, arithmetic and copies ran while one was open for 9% -> 10% of each run, Pallas kernels for 10% -> 11%
where the time goes in v4:
time: 587 us; the launch traced here: 576 us
  waiting for transfers between devices  195 us (33%)
  starting transfers between devices  125 us (21%)
  local copies, waits for them, and re-layouts  109 us (19%)
  Pallas kernels  85.2 us (15%)
  other arithmetic  45.3 us (8%)
  between operations  16.6 us (3%)
    ppermute x65, waiting for transfers between devices, exchange(): return lax.ppermute(value, axis, [(0, 1), (1, 0)])  140 us
    ppermute x65, starting transfers between devices, exchange(): return lax.ppermute(value, axis, [(0, 1), (1, 0)])  81.8 us
    unnamed x317, local copies, waits for them, and re-layouts  75.9 us
    ppermute x24, waiting for transfers between devices, stepping(): return lambda v: lax.ppermute(v, ('far', 'near'), perm)  48.3 us
    ppermute x24, starting transfers between devices, stepping(): return lambda v: lax.ppermute(v, ('far', 'near'), perm)  42.8 us
    pallas_call x7, Pallas kernels, pieces_product(): pl.pallas_call(body, grid=(depth // tile,), in_specs=specs, out_specs=[pl...  21.5 us
    pallas_call x3, Pallas kernels, gradient_product(): pl.pallas_call(body, grid=(sum(tiles),), in_specs=specs, out_specs=pl.Blo...  18.3 us
    pallas_call x2, Pallas kernels, attention_back(): pl.pallas_call(functools.partial(attend_back_kernel, heads, causal), grid...  13.2 us
  transfers between devices with their start and end apart: 95, of which 49 were waited for; matrix products, arithmetic and copies ran while one was open for 10% of the time, Pallas kernels for 11%

profile of v4, /device:TPU:0, one launch (start us, length us, event | category | flops | bytes accessed | tf_op | source)
XLA Modules:
  0.0 576.4 jit_solution(13117475715233383534)
XLA Ops:
  13.2 7.0 %collective-permute-done.2 = bf16[192,768]{1,0:T(8,128)(2,1)S(1)} collective-permute-done((bf16[192,768]{1,0:T(8,128)(2,1)S(1)}, bf16[192,768]{1,0:T(8,128)(2,1)S(1)}, u32[]{:S(2)}, u32[]{:S(2)}) %collective-permute-start.2) | collective-permute-done | bytes 294944 | tf_op jit(solution)/shard_map/ppermute | solution.py:283
  38.7 9.4 %collective-permute-done.7 = bf16[192,3072]{1,0:T(8,128)(2,1)} collective-permute-done((bf16[192,3072]{1,0:T(8,128)(2,1)S(1)}, bf16[192,3072]{1,0:T(8,128)(2,1)}, u32[]{:S(2)}, u32[]{:S(2)}) %collective-permute-start.7) | collective-permute-done | bytes 1179680 | tf_op jit(solution)/shard_map/ppermute | solution.py:283
  53.2 11.5 %collective-permute-done.10 = bf16[384,768]{1,0:T(8,128)(2,1)} collective-permute-done((bf16[384,768]{1,0:T(8,128)(2,1)S(1)}, bf16[384,768]{1,0:T(8,128)(2,1)}, u32[]{:S(2)}, u32[]{:S(2)}) %collective-permute-start.10) | collective-permute-done | bytes 589856 | tf_op jit(solution)/shard_map/ppermute | solution.py:283
  72.8 5.6 collective-permute-done.8.refs_1_
  91.9 14.3 %collective-permute-done.11.refs_3_ = bf16[64,1536]{1,0:T(8,128)(2,1)S(1)} collective-permute-done((bf16[64,1536]{1,0:T(8,128)(2,1)S(1)}, bf16[64,1536]{1,0:T(8,128)(2,1)S(1)}, u32[]{:S(2)}, u32[]{:S(2)}) %collective-permute-start.11) | collective-permute-done | bytes 196640 | tf_op jit(solution)/shard_map/ppermute | solution.py:283
  167.5 5.8 %collective-permute-done.22 = bf16[32,1536]{1,0:T(8,128)(2,1)S(1)} collective-permute-done((bf16[32,1536]{1,0:T(8,128)(2,1)S(1)}, bf16[32,1536]{1,0:T(8,128)(2,1)S(1)}, u32[]{:S(2)}, u32[]{:S(2)}) %collective-permute-start.22) | collective-permute-done | bytes 98336 | tf_op jit(solution)/shard_map/ppermute | solution.py:283
  214.9 5.7 collective-permute-done.30.one_ref
  226.1 4.7 collective-permute-done.32.near_ref
  242.1 6.7 %collective-permute-done.37.refs_1_ = bf16[128,1536]{1,0:T(8,128)(2,1)S(1)} collective-permute-done((bf16[128,1536]{1,0:T(8,128)(2,1)S(1)}, bf16[128,1536]{1,0:T(8,128)(2,1)S(1)}, u32[]{:S(2)}, u32[]{:S(2)}) %collective-permute-start.37) | collective-permute-done | bytes 393248 | tf_op jit(solution)/shard_map/ppermute | solution.py:643
  252.3 11.4 %collective-permute-done.41.refs_3_ = bf16[128,1536]{1,0:T(8,128)(2,1)S(1)} collective-permute-done((bf16[128,1536]{1,0:T(8,128)(2,1)S(1)}, bf16[128,1536]{1,0:T(8,128)(2,1)S(1)}, u32[]{:S(2)}, u32[]{:S(2)}) %collective-permute-start.41) | collective-permute-done | bytes 393248 | tf_op jit(solution)/shard_map/ppermute | solution.py:643
  267.9 6.9 %collective-permute-done.43.refs_6_ = bf16[128,1536]{1,0:T(8,128)(2,1)S(1)} collective-permute-done((bf16[128,1536]{1,0:T(8,128)(2,1)S(1)}, bf16[128,1536]{1,0:T(8,128)(2,1)S(1)}, u32[]{:S(2)}, u32[]{:S(2)}) %collective-permute-start.43) | collective-permute-done | bytes 393248 | tf_op jit(solution)/shard_map/ppermute | solution.py:643
  283.9 9.6 %middle.1 = (bf16[512,1536]{1,0:T(8,128)(2,1)S(1)}, bf16[512,1536]{1,0:T(8,128)(2,1)S(1)}, bf16[512,1536]{1,0:T(8,128)(2,1)S(1)}) custom-call(bf16[128,1536]{1,0:T(8,128)(2,1)S(1)} %copy-done.95, bf16[128,1536]{1,0:T(8,128)(2,1)S(1)} %copy-done.99, bf16[128,1536]{1,0:T(8,128)(2,1)S(1)} %copy-done.105, bf16[128,1536]{1,0:T(8,128)(2,1)S(1)} %copy-done.103, ...), custom_call_target="tpu_custom_call" | custom-call | flops 1 | bytes 1 | tf_op jit(solution)/shard_map/middle/pallas_call | solution.py:388
  301.1 10.0 %gradient_product.3 = bf16[1536,3072]{1,0:T(8,128)(2,1)} custom-call(bf16[512,1536]{1,0:T(8,128)(2,1)S(1)} %get-tuple-element.523.refs_0_, bf16[512,1536]{1,0:T(8,128)(2,1)S(1)} %get-tuple-element.524.refs_0_.refs_1_, bf16[512,1536]{1,0:T(8,128)(2,1)S(1)} %copy-done.12, bf16[512,1536]{1,0:T(8,128)(2,1)S(1)} %get-tuple-element.531.refs_3_.refs_0_), custom_call_target="tpu_custom_call" | custom-call | flops 1 | bytes 1 | tf_op jit(solution)/shard_map/gradient_product/pallas_call | solution.py:463
  313.5 6.7 %collective-permute-done.45 = bf16[128,1536]{1,0:T(8,128)(2,1)S(1)} collective-permute-done((bf16[128,1536]{1,0:T(8,128)(2,1)}, bf16[128,1536]{1,0:T(8,128)(2,1)S(1)}, u32[]{:S(2)}, u32[]{:S(2)}) %collective-permute-start.45) | collective-permute-done | bytes 393248 | tf_op jit(solution)/shard_map/ppermute | solution.py:643
  332.4 5.1 pieces_product.10
  341.5 5.6 collective-permute-done.49.row_ref
  347.1 5.2 collective-permute-done.48.near_ref
  355.4 6.4 %collective-permute-done.50.refs_2_ = bf16[128,1536]{1,0:T(8,128)(2,1)S(1)} collective-permute-done((bf16[128,1536]{1,0:T(8,128)(2,1)S(1)}, bf16[128,1536]{1,0:T(8,128)(2,1)S(1)}, u32[]{:S(2)}, u32[]{:S(2)}) %collective-permute-start.50) | collective-permute-done | bytes 393248 | tf_op jit(solution)/shard_map/ppermute | solution.py:283
  370.1 5.7 attend_back.2
  398.9 8.9 %collective-permute-done.58.near_ref = bf16[128,1536]{1,0:T(8,128)(2,1)S(1)} collective-permute-done((bf16[128,1536]{1,0:T(8,128)(2,1)S(1)}, bf16[128,1536]{1,0:T(8,128)(2,1)S(1)}, u32[]{:S(2)}, u32[]{:S(2)}) %collective-permute-start.58) | collective-permute-done | bytes 393248 | tf_op jit(solution)/shard_map/ppermute | solution.py:283
  437.3 7.5 %attend_back.3 = (bf16[512,384]{1,0:T(8,128)(2,1)S(1)}, bf16[512,384]{1,0:T(8,128)(2,1)S(1)}, bf16[512,384]{1,0:T(8,128)(2,1)S(1)}) custom-call(bf16[512,1152]{1,0:T(8,128)(2,1)S(1)} %get-tuple-element.619.q_ref.k_ref.v_ref, bf16[512,1152]{1,0:T(8,128)(2,1)S(1)} %get-tuple-element.619.q_ref.k_ref.v_ref, ...), custom_call_target="tpu_custom_call" | custom-call | flops 1 | bytes 1 | tf_op jit(solution)/shard_map/attend_back/pallas_call | solution.py:602
  444.9 4.7 gradient_product.5
  492.0 6.6 %reduce-scatter.8.cloned.1.call-done = bf16[384,1536]{1,0:T(8,128)(2,1)} async-done(((bf16[1536,1536]{1,0:T(8,128)(2,1)}), bf16[384,1536]{1,0:T(8,128)(2,1)}) %reduce-scatter.8.cloned.1.call-update) | async-done | bytes 1179664 | tf_op jit(solution)/shard_map/reduce_scatter | solution.py:663
  517.4 14.2 %collective-permute-done.77 = f32[6,768]{1,0:T(8,128)S(1)} collective-permute-done((f32[6,768]{1,0:T(8,128)S(1)}, f32[6,768]{1,0:T(8,128)S(1)}, u32[]{:S(2)}, u32[]{:S(2)}) %collective-permute-start.77) | collective-permute-done | bytes 18464 | tf_op jit(solution)/shard_map/ppermute | solution.py:283
  (672 shorter events, 374.6 us)
Async XLA Ops:
  7.2 100.4 %all-gather.4.cloned.1.call-start = ((), (), s32[]{:S(2)}) async-start(), calls=%async_computation.3 | async-start | bytes 5898240 | tf_op jit(solution)/shard_map/all_gather | solution.py:659
  20.5 27.6 %collective-permute-start.7 = (bf16[192,3072]{1,0:T(8,128)(2,1)S(1)}, bf16[192,3072]{1,0:T(8,128)(2,1)}, u32[]{:S(2)}, u32[]{:S(2)}) collective-permute-start(bf16[192,3072]{1,0:T(8,128)(2,1)S(1)} %constant_dynamic-update-slice_fusion), channel_id=1, source_target_pairs={{0,16},{16,0},{1,17},{17,1},{2,18},{18,2},{3,19},{19,3},{4,20},{20... | collective-permute-start | bytes 3538952 | tf_op jit(solution)/shard_map/ppermute | solution.py:283
  35.9 28.8 %collective-permute-start.10 = (bf16[384,768]{1,0:T(8,128)(2,1)S(1)}, bf16[384,768]{1,0:T(8,128)(2,1)}, u32[]{:S(2)}, u32[]{:S(2)}) collective-permute-start(bf16[384,768]{1,0:T(8,128)(2,1)S(1)} %maximum_select_fusion.1), channel_id=1, source_target_pairs={{0,2},{2,0},{1,3},{3,1},{4,6},{6,4},{5,7},{7,5},{8,10},{10,8},{9,1... | collective-permute-start | bytes 1769480 | tf_op jit(solution)/shard_map/ppermute | solution.py:283
  68.3 127.9 %all-gather.6.cloned.1.call-start = ((), (), s32[]{:S(2)}) async-start(), calls=%async_computation.4 | async-start | bytes 5898240 | tf_op jit(solution)/shard_map/all_gather | solution.py:659
  86.6 36.4 %collective-permute-start.14 = (bf16[384,768]{1,0:T(8,128)(2,1)}, bf16[384,768]{1,0:T(8,128)(2,1)}, u32[]{:S(2)}, u32[]{:S(2)}) collective-permute-start(bf16[384,768]{1,0:T(8,128)(2,1)} %maximum_select_fusion.2), channel_id=1, source_target_pairs={{0,2},{2,0},{1,3},{3,1},{4,6},{6,4},{5,7},{7,5},{8,10},{10,8},{9,1... | collective-permute-start | bytes 1769480 | tf_op jit(solution)/shard_map/ppermute | solution.py:283
  131.2 144.4 %all-gather.8.cloned.1.call-start = ((), (), s32[]{:S(2)}) async-start(), calls=%async_computation.5 | async-start | bytes 11796480 | tf_op jit(solution)/shard_map/all_gather | solution.py:659
  131.9 293.9 %reduce-scatter.4.cloned.1.call-start = ((), (), s32[]{:S(2)}) async-start(), calls=%async_computation.6 | async-start | bytes 11796480 | tf_op jit(solution)/shard_map/reduce_scatter | solution.py:663
  162.6 17.5 %collective-permute-start.20 = (bf16[128,1536]{1,0:T(8,128)(2,1)S(1)}, bf16[128,1536]{1,0:T(8,128)(2,1)S(1)}, u32[]{:S(2)}, u32[]{:S(2)}) collective-permute-start(bf16[128,1536]{1,0:T(8,128)(2,1)S(1)} %get-tuple-element.457.refs_0_), channel_id=1, source_target_pairs={{0,1},{1,0},{2,3},{3,2},{4,5},{5,4},{6,7},{7,6},{8,9},{9,8},{10,11... | collective-permute-start | bytes 1179656 | tf_op jit(solution)/shard_map/ppermute | solution.py:283
  162.7 18.7 %collective-permute-start.21 = (bf16[128,1536]{1,0:T(8,128)(2,1)S(1)}, bf16[128,1536]{1,0:T(8,128)(2,1)S(1)}, u32[]{:S(2)}, u32[]{:S(2)}) collective-permute-start(bf16[128,1536]{1,0:T(8,128)(2,1)S(1)} %get-tuple-element.457.refs_0_), channel_id=1, source_target_pairs={{0,16},{16,0},{1,17},{17,1},{2,18},{18,2},{3,19},{19,3},{4,20},{20... | collective-permute-start | bytes 1179656 | tf_op jit(solution)/shard_map/ppermute | solution.py:283
  190.8 33.2 %collective-permute-start.34 = (bf16[128,1536]{1,0:T(8,128)(2,1)}, bf16[128,1536]{1,0:T(8,128)(2,1)}, u32[]{:S(2)}, u32[]{:S(2)}) collective-permute-start(bf16[128,1536]{1,0:T(8,128)(2,1)} %collective-permute-done.26), channel_id=1, source_target_pairs={{1,2},{2,3},{5,6},{6,7},{9,10},{10,11},{13,14},{14,15},{17,18},{18... | collective-permute-start | bytes 1179656 | tf_op jit(solution)/shard_map/ppermute | solution.py:643
  192.3 31.8 %collective-permute-start.35 = (bf16[128,1536]{1,0:T(8,128)(2,1)}, bf16[128,1536]{1,0:T(8,128)(2,1)}, u32[]{:S(2)}, u32[]{:S(2)}) collective-permute-start(bf16[128,1536]{1,0:T(8,128)(2,1)} %collective-permute-done.27), channel_id=1, source_target_pairs={{2,1},{1,0},{6,5},{5,4},{10,9},{9,8},{14,13},{13,12},{18,17},{17,1... | collective-permute-start | bytes 1179656 | tf_op jit(solution)/shard_map/ppermute | solution.py:643
  311.1 147.4 %reduce-scatter.6.cloned.1.call-start = ((), (), s32[]{:S(2)}) async-start(), calls=%async_computation.7 | async-start | bytes 5898240 | tf_op jit(solution)/shard_map/reduce_scatter | solution.py:663
  387.3 111.4 %reduce-scatter.8.cloned.1.call-start = ((), (), s32[]{:S(2)}) async-start(), calls=%async_computation.8 | async-start | bytes 5898240 | tf_op jit(solution)/shard_map/reduce_scatter | solution.py:663
  457.7 27.2 %collective-permute-start.68 = (bf16[192,3072]{1,0:T(8,128)(2,1)}, bf16[192,3072]{1,0:T(8,128)(2,1)}, u32[]{:S(2)}, u32[]{:S(2)}) collective-permute-start(bf16[192,3072]{1,0:T(8,128)(2,1)} %get-tuple-element.725), channel_id=1, source_target_pairs={{0,16},{16,0},{1,17},{17,1},{2,18},{18,2},{3,19},{19,3},{4,20},{20... | collective-permute-start | bytes 3538952 | tf_op jit(solution)/shard_map/ppermute | solution.py:283
  461.4 29.7 %collective-permute-start.73 = (bf16[384,768]{1,0:T(8,128)(2,1)S(1)}, bf16[384,768]{1,0:T(8,128)(2,1)S(1)}, u32[]{:S(2)}, u32[]{:S(2)}) collective-permute-start(bf16[384,768]{1,0:T(8,128)(2,1)S(1)} %pad_maximum_fusion.3), channel_id=1, source_target_pairs={{0,2},{2,0},{1,3},{3,1},{4,6},{6,4},{5,7},{7,5},{8,10},{10,8},{9,1... | collective-permute-start | bytes 1769480 | tf_op jit(solution)/shard_map/ppermute | solution.py:283
  483.8 21.4 %collective-permute-start.71 = (bf16[128,1536]{1,0:T(8,128)(2,1)S(1)}, bf16[128,1536]{1,0:T(8,128)(2,1)S(1)}, u32[]{:S(2)}, u32[]{:S(2)}) collective-permute-start(bf16[128,1536]{1,0:T(8,128)(2,1)S(1)} %get-tuple-element.652), channel_id=1, source_target_pairs={{0,1},{1,0},{2,3},{3,2},{4,5},{5,4},{6,7},{7,6},{8,9},{9,8},{10,11... | collective-permute-start | bytes 1179656 | tf_op jit(solution)/shard_map/ppermute | solution.py:283
  484.8 20.4 %collective-permute-start.72 = (bf16[128,1536]{1,0:T(8,128)(2,1)S(1)}, bf16[128,1536]{1,0:T(8,128)(2,1)S(1)}, u32[]{:S(2)}, u32[]{:S(2)}) collective-permute-start(bf16[128,1536]{1,0:T(8,128)(2,1)S(1)} %get-tuple-element.653), channel_id=1, source_target_pairs={{0,16},{16,0},{1,17},{17,1},{2,18},{18,2},{3,19},{19,3},{4,20},{20... | collective-permute-start | bytes 1179656 | tf_op jit(solution)/shard_map/ppermute | solution.py:283
  501.7 33.9 %collective-permute-start.81 = (bf16[384,768]{1,0:T(8,128)(2,1)}, bf16[384,768]{1,0:T(8,128)(2,1)}, u32[]{:S(2)}, u32[]{:S(2)}) collective-permute-start(bf16[384,768]{1,0:T(8,128)(2,1)} %pad_maximum_fusion.5), channel_id=1, source_target_pairs={{0,2},{2,0},{1,3},{3,1},{4,6},{6,4},{5,7},{7,5},{8,10},{10,8},{9,1... | collective-permute-start | bytes 1769480 | tf_op jit(solution)/shard_map/ppermute | solution.py:283
  509.7 22.0 %collective-permute-start.77 = (f32[6,768]{1,0:T(8,128)S(1)}, f32[6,768]{1,0:T(8,128)S(1)}, u32[]{:S(2)}, u32[]{:S(2)}) collective-permute-start(f32[6,768]{1,0:T(8,128)S(1)} %select_n.354), channel_id=1, source_target_pairs={{0,2},{2,0},{1,3},{3,1},{4,6},{6,4},{5,7},{7,5},{8,10},{10,8},{9,1... | collective-permute-start | bytes 55304 | tf_op jit(solution)/shard_map/ppermute | solution.py:283
  514.4 18.2 %collective-permute-start.75 = (bf16[16,1536]{1,0:T(8,128)(2,1)S(1)}, bf16[16,1536]{1,0:T(8,128)(2,1)S(1)}, u32[]{:S(2)}, u32[]{:S(2)}) collective-permute-start(bf16[16,1536]{1,0:T(8,128)(2,1)S(1)} %get-tuple-element.683), channel_id=1, source_target_pairs={{0,16},{16,0},{1,17},{17,1},{2,18},{18,2},{3,19},{19,3},{4,20},{20... | collective-permute-start | bytes 147464 | tf_op jit(solution)/shard_map/ppermute | solution.py:283
  541.3 17.2 %collective-permute-start.83 = (bf16[64,1536]{1,0:T(8,128)(2,1)}, bf16[64,1536]{1,0:T(8,128)(2,1)}, u32[]{:S(2)}, u32[]{:S(2)}) collective-permute-start(bf16[64,1536]{1,0:T(8,128)(2,1)} %slice.961), channel_id=1, source_target_pairs={{0,2},{2,0},{1,3},{3,1},{4,6},{6,4},{5,7},{7,5},{8,10},{10,8},{9,1... | collective-permute-start | bytes 589832 | tf_op jit(solution)/shard_map/ppermute | solution.py:283
  543.4 19.1 %collective-permute-start.74 = (bf16[64,1536]{1,0:T(8,128)(2,1)}, bf16[64,1536]{1,0:T(8,128)(2,1)}, u32[]{:S(2)}, u32[]{:S(2)}) collective-permute-start(bf16[64,1536]{1,0:T(8,128)(2,1)} %slice.782), channel_id=1, source_target_pairs={{0,2},{2,0},{1,3},{3,1},{4,6},{6,4},{5,7},{7,5},{8,10},{10,8},{9,1... | collective-permute-start | bytes 589832 | tf_op jit(solution)/shard_map/ppermute | solution.py:283
  544.3 18.6 %collective-permute-start.82 = (bf16[16,1536]{1,0:T(8,128)(2,1)S(1)}, bf16[16,1536]{1,0:T(8,128)(2,1)S(1)}, u32[]{:S(2)}, u32[]{:S(2)}) collective-permute-start(bf16[16,1536]{1,0:T(8,128)(2,1)S(1)} %slice.962), channel_id=1, source_target_pairs={{0,2},{2,0},{1,3},{3,1},{4,6},{6,4},{5,7},{7,5},{8,10},{10,8},{9,1... | collective-permute-start | bytes 147464 | tf_op jit(solution)/shard_map/ppermute | solution.py:283
  546.4 18.9 %collective-permute-start.88 = (bf16[192,768]{1,0:T(8,128)(2,1)}, bf16[192,768]{1,0:T(8,128)(2,1)S(1)}, u32[]{:S(2)}, u32[]{:S(2)}) collective-permute-start(bf16[192,768]{1,0:T(8,128)(2,1)} %select_convert_fusion), channel_id=1, source_target_pairs={{0,16},{16,0},{1,17},{17,1},{2,18},{18,2},{3,19},{19,3},{4,20},{20... | collective-permute-start | bytes 884744 | tf_op jit(solution)/shard_map/ppermute | solution.py:283
  (227 other events, 1417.1 us)
Sparse Core Ops, SparseCore 0:
  68.4 36.2 all-gather.3
  131.3 35.6 all-gather.5
  168.6 64.2 all-gather.7
  311.3 74.8 reduce-scatter.3
  388.6 47.8 reduce-scatter.5
  454.2 44.4 reduce-scatter.7
